TPU v7x, 32 devices: a whole 2x2x4 slice. The times are simulated.
32 devices in a mesh: dp: 16 (over z, x, core), mp: 2 (over y).
Axes of the slice: x: 2, y: 2, z: 4, core: 2. Of those that a mesh axis runs over, the one named last changes fastest.
Arguments:
- hidden_in: bfloat16 [16384, 1024], P(('dp', 'mp')), may hold values from -6 to 6
- segments: int32 [16, 1024], P('dp'), may hold values from 0 to 7, never falling along the last dimension, each value on 1 to 800 neighbouring positions
- timesteps: int32 [16], P('dp'), may hold values from 0 to 4999
- time_weight: bfloat16 [1024, 1024], P('dp'), may hold values from -0.1875 to 0.1875
- qkv_weight: bfloat16 [3, 1024, 1024], P(None, 'dp', 'mp'), may hold values from -0.1875 to 0.1875
- out_weight: bfloat16 [1024, 1024], P('mp', 'dp'), may hold values from -1 to 1
- in_weight: bfloat16 [1024, 4096], P('dp', 'mp'), may hold values from -0.1875 to 0.1875
- down_weight: bfloat16 [4096, 1024], P('mp', 'dp'), may hold values from -0.09375 to 0.09375
- biases: bfloat16 [7, 1024], P(None, 'dp'), may hold values from -2 to 2
- gains: bfloat16 [2, 1024], P(None, 'dp'), may hold values from 0.099609375 to 1.8984375
- ffn_bias: bfloat16 [4096], P('dp'), may hold values from -2 to 2
- out_grad: bfloat16 [16384, 1024], P(('dp', 'mp')), may hold values from -6 to 6
Outputs:
- layer_out: bfloat16 [16384, 1024], P(('dp', 'mp'))
- input_grad: float32 [16384, 1024], P(('dp', 'mp'))
- time_weight_grad: float32 [1024, 1024], P('dp')
- qkv_weight_grad: float32 [3, 1024, 1024], P(None, 'dp', 'mp')
- out_weight_grad: float32 [1024, 1024], P('mp', 'dp')
- in_weight_grad: float32 [1024, 4096], P('dp', 'mp')
- down_weight_grad: float32 [4096, 1024], P('mp', 'dp')
- bias_grad: float32 [7, 1024], P(None, 'dp')
- gain_grad: float32 [2, 1024], P(None, 'dp')
- ffn_bias_grad: float32 [4096], P('dp')
Inputs may be any that keep to these rules, and one draw needn't show every extreme that they name: `segments`: segment numbers never fall along a sequence; each document covers 1 to 800 consecutive tokens of it.
All inputs are finite; a program needn't handle non-finite values.
Results may differ from a plain program's by a relative error of at most 0.028.
Values may be sent and summed in bfloat16 or wider, within the bound.
A program may use at most 192 MiB of HBM per device.

v0:
```python
import math

import jax
import jax.numpy as jnp
from jax import lax
from jax.sharding import PartitionSpec as P

HD = 64


eps = 1e-05
neg_big = -1000000000.0
highest = lax.Precision.HIGHEST


def time_features(step_ids, model_width):
    half_width = model_width // 2
    frequency = jnp.exp(
        jnp.arange(half_width, dtype=jnp.float32) * (-math.log(10000.0) / half_width)
    )
    angles = step_ids.astype(jnp.float32)[:, None] * frequency[None, :]
    return jnp.concatenate([jnp.sin(angles), jnp.cos(angles)], axis=1)


def normalize(array_in):
    row_mean = jnp.mean(array_in, axis=-1, keepdims=True)
    centered = array_in - row_mean
    variance = jnp.mean(centered * centered, axis=-1, keepdims=True)
    inv_std = lax.rsqrt(variance + eps)
    return (centered * inv_std, inv_std)


def norm_back(grad_rows, unit_rows, inv_std, gain_row):
    d_unit = grad_rows * gain_row
    return inv_std * (
        d_unit
        - jnp.mean(d_unit, axis=-1, keepdims=True)
        - unit_rows * jnp.mean(d_unit * unit_rows, axis=-1, keepdims=True)
    )


def exact_gelu(array_in):
    return jax.nn.gelu(array_in, approximate=False)


def contract_rows(left, right):
    return lax.dot_general(
        left, right, (((0,), (0,)), ((), ())), preferred_element_type=jnp.float32
    )


def contract_cols(left, right):
    return lax.dot_general(
        left, right, (((1,), (1,)), ((), ())), preferred_element_type=jnp.float32
    )


def score_block(q_block, key_rows, seg_block, doc_ids, score_scale):
    raw_score = jnp.einsum("qhd,khd->hqk", q_block, key_rows, preferred_element_type=jnp.float32)
    same_doc = seg_block[:, None] == doc_ids[None, :]
    return jnp.where(same_doc[None], raw_score * score_scale, neg_big)


def attend_sequence(queries, key_rows, values, doc_ids, score_scale):
    length, head_count, head_size = queries.shape
    block_rows = min(512, length)
    block_count = length // block_rows

    def per_block(packet):
        q_block, seg_block = packet
        scores = score_block(q_block, key_rows, seg_block, doc_ids, score_scale)
        row_max = jnp.max(scores, axis=-1, keepdims=True)
        exp_score = jnp.exp(scores - row_max)
        row_total = jnp.sum(exp_score, axis=-1, keepdims=True)
        attn_prob = (exp_score / row_total).astype(jnp.bfloat16)
        block_out = jnp.einsum(
            "hqk,khd->qhd", attn_prob, values, preferred_element_type=jnp.float32
        )
        return (block_out, (row_max + jnp.log(row_total))[..., 0])

    block_outs, log_total = lax.map(
        per_block,
        (
            queries.reshape(block_count, block_rows, head_count, head_size),
            doc_ids.reshape(block_count, block_rows),
        ),
    )
    return (block_outs.reshape(length, head_count * head_size), log_total)


def attend_back(queries, key_rows, values, doc_ids, log_total, d_mixed, score_scale):
    length, head_count, head_size = queries.shape
    block_rows = min(512, length)
    block_count = length // block_rows

    def per_block(totals, packet):
        grad_key, grad_value = totals
        q_block, seg_block, log_block, d_block = packet
        scores = score_block(q_block, key_rows, seg_block, doc_ids, score_scale)
        attn_prob = jnp.exp(scores - log_block[..., None])
        grad_prob = jnp.einsum("qhd,khd->hqk", d_block, values, preferred_element_type=jnp.float32)
        row_delta = jnp.sum(attn_prob * grad_prob, axis=-1, keepdims=True)
        grad_score = (attn_prob * (grad_prob - row_delta) * score_scale).astype(jnp.bfloat16)
        grad_query = jnp.einsum(
            "hqk,khd->qhd", grad_score, key_rows, preferred_element_type=jnp.float32
        )
        grad_key = grad_key + jnp.einsum(
            "hqk,qhd->khd", grad_score, q_block, preferred_element_type=jnp.float32
        )
        grad_value = grad_value + jnp.einsum(
            "hqk,qhd->khd",
            attn_prob.astype(jnp.bfloat16),
            d_block,
            preferred_element_type=jnp.float32,
        )
        return ((grad_key, grad_value), grad_query)

    zeros_kv = jnp.zeros(key_rows.shape, jnp.float32)
    block_shape = (block_count, block_rows, head_count, head_size)
    (grad_key, grad_value), grad_query = lax.scan(
        per_block,
        (zeros_kv, zeros_kv),
        (
            queries.reshape(block_shape),
            doc_ids.reshape(block_count, block_rows),
            log_total,
            d_mixed.reshape(block_shape),
        ),
    )
    flat = (length, head_count * head_size)
    return (grad_query.reshape(flat), grad_key.reshape(flat), grad_value.reshape(flat))


def on_device(
    hidden_in,
    segments,
    timesteps,
    time_weight,
    qkv_weight,
    out_weight,
    in_weight,
    down_weight,
    biases,
    gains,
    ffn_bias,
    out_grad,
):
    mp_index = lax.axis_index("mp")
    own_rows = hidden_in.shape[0]
    model_width = hidden_in.shape[1]
    seq_count, length = segments.shape
    group_rows = seq_count * length
    score_scale = 1.0 / math.sqrt(HD)
    gathered = (
        lax.all_gather(qkv_weight, "dp", axis=1, tiled=True),
        lax.all_gather(out_weight, "dp", axis=1, tiled=True),
        lax.all_gather(time_weight, "dp", axis=0, tiled=True),
        lax.all_gather(in_weight, "dp", axis=0, tiled=True),
        lax.all_gather(down_weight, "dp", axis=1, tiled=True),
        lax.all_gather(biases, "dp", axis=1, tiled=True),
        lax.all_gather(gains, "dp", axis=1, tiled=True),
        lax.all_gather(ffn_bias, "dp", axis=0, tiled=True),
    )
    qkv_w, out_w, time_w, in_w, down_w, bias_all, gain_all, ffn_b = gathered
    local_cols = qkv_w.shape[2]
    local_heads = local_cols // HD
    hidden_local = in_w.shape[1]
    column = mp_index * local_cols
    bias_query = lax.dynamic_slice_in_dim(bias_all[1], column, local_cols)
    bias_value = lax.dynamic_slice_in_dim(bias_all[2], column, local_cols)
    feature = time_features(timesteps, model_width).astype(jnp.bfloat16)
    time_rows = jnp.dot(feature, time_w, preferred_element_type=jnp.float32) + bias_all[0]
    seq_of_row = (mp_index * own_rows + jnp.arange(own_rows)) // length
    pick_seq = (seq_of_row[:, None] == jnp.arange(seq_count)[None, :]).astype(jnp.float32)
    embedded = hidden_in.astype(jnp.float32) + jnp.dot(pick_seq, time_rows, precision=highest)
    embed_low = embedded.astype(jnp.bfloat16)
    whole_rows = lax.all_gather(embed_low, "mp", axis=0, tiled=True)
    queries = (
        jnp.dot(whole_rows, qkv_w[0], preferred_element_type=jnp.float32) + bias_query
    ).astype(jnp.bfloat16)
    key_rows = jnp.dot(whole_rows, qkv_w[1], preferred_element_type=jnp.float32).astype(
        jnp.bfloat16
    )
    values = (
        jnp.dot(whole_rows, qkv_w[2], preferred_element_type=jnp.float32) + bias_value
    ).astype(jnp.bfloat16)
    head_shape = (seq_count, length, local_heads, HD)
    queries4 = queries.reshape(head_shape)
    keys4 = key_rows.reshape(head_shape)
    values4 = values.reshape(head_shape)

    def forward_sequence(packet):
        return attend_sequence(packet[0], packet[1], packet[2], packet[3], score_scale)

    mixed_heads, log_total = lax.map(forward_sequence, (queries4, keys4, values4, segments))
    mixed_low = mixed_heads.reshape(group_rows, local_cols).astype(jnp.bfloat16)
    attn_total = lax.psum_scatter(
        jnp.dot(mixed_low, out_w, preferred_element_type=jnp.float32),
        "mp",
        scatter_dimension=0,
        tiled=True,
    )
    unit_one, inv_one = normalize(embedded + attn_total + bias_all[3])
    middle = unit_one * gain_all[0] + bias_all[4]
    middle_low = middle.astype(jnp.bfloat16)
    ffn_input = lax.all_gather(middle_low, "mp", axis=0, tiled=True)
    bias_hidden = lax.dynamic_slice_in_dim(ffn_b, mp_index * hidden_local, hidden_local)
    pre_act = jnp.dot(ffn_input, in_w, preferred_element_type=jnp.float32) + bias_hidden
    hidden_act = exact_gelu(pre_act).astype(jnp.bfloat16)
    ffn_total = lax.psum_scatter(
        jnp.dot(hidden_act, down_w, preferred_element_type=jnp.float32).astype(jnp.bfloat16),
        "mp",
        scatter_dimension=0,
        tiled=True,
    ).astype(jnp.float32)
    unit_two, inv_two = normalize(middle + ffn_total + bias_all[5])
    layer_out = (unit_two * gain_all[1] + bias_all[6]).astype(jnp.bfloat16)
    qkv_w, out_w, in_w, down_w, gain_all = (
        lax.all_gather(qkv_weight, "dp", axis=1, tiled=True),
        lax.all_gather(out_weight, "dp", axis=1, tiled=True),
        lax.all_gather(in_weight, "dp", axis=0, tiled=True),
        lax.all_gather(down_weight, "dp", axis=1, tiled=True),
        lax.all_gather(gains, "dp", axis=1, tiled=True),
    )
    grad_out = out_grad.astype(jnp.float32)
    gain_two_part = jnp.sum(grad_out * unit_two, axis=0)
    shift_two_part = jnp.sum(grad_out, axis=0)
    d_pre_two = norm_back(grad_out, unit_two, inv_two, gain_all[1])
    bias_five_part = jnp.sum(d_pre_two, axis=0)
    d_ffn_low = d_pre_two.astype(jnp.bfloat16)
    d_ffn_whole = lax.all_gather(d_ffn_low, "mp", axis=0, tiled=True)
    d_act = contract_cols(d_ffn_whole, down_w)
    d_pre_act = jax.vjp(exact_gelu, pre_act)[1](d_act)[0]
    ffn_bias_part = lax.dynamic_update_slice_in_dim(
        jnp.zeros(ffn_b.shape, jnp.float32), jnp.sum(d_pre_act, axis=0), mp_index * hidden_local, 0
    )
    d_pre_low = d_pre_act.astype(jnp.bfloat16)
    in_grad_local = contract_rows(ffn_input, d_pre_low)
    down_grad_local = contract_rows(hidden_act, d_ffn_whole)
    d_middle_ffn = lax.psum_scatter(
        contract_cols(d_pre_low, in_w).astype(jnp.bfloat16), "mp", scatter_dimension=0, tiled=True
    ).astype(jnp.float32)
    d_middle = d_pre_two + d_middle_ffn
    gain_one_part = jnp.sum(d_middle * unit_one, axis=0)
    shift_one_part = jnp.sum(d_middle, axis=0)
    d_pre_one = norm_back(d_middle, unit_one, inv_one, gain_all[0])
    bias_three_part = jnp.sum(d_pre_one, axis=0)
    d_attn_whole = lax.all_gather(d_pre_one.astype(jnp.bfloat16), "mp", axis=0, tiled=True)
    out_grad_local = contract_rows(mixed_low, d_attn_whole)
    d_mixed = contract_cols(d_attn_whole, out_w).astype(jnp.bfloat16)

    def backward_sequence(packet):
        return attend_back(
            packet[0], packet[1], packet[2], packet[3], packet[4], packet[5], score_scale
        )

    grad_query, grad_key, grad_value = lax.map(
        backward_sequence,
        (queries4, keys4, values4, segments, log_total, d_mixed.reshape(head_shape)),
    )
    grad_query = grad_query.reshape(group_rows, local_cols)
    grad_value = grad_value.reshape(group_rows, local_cols)
    stacked_low = jnp.stack(
        [grad_query, grad_key.reshape(group_rows, local_cols), grad_value]
    ).astype(jnp.bfloat16)
    qkv_grad_local = jnp.einsum(
        "tnd,tnc->tdc",
        jnp.broadcast_to(whole_rows, (3,) + whole_rows.shape),
        stacked_low,
        preferred_element_type=jnp.float32,
    )
    input_grad = d_pre_one + lax.psum_scatter(
        jnp.einsum("tnc,tdc->nd", stacked_low, qkv_w, preferred_element_type=jnp.float32).astype(
            jnp.bfloat16
        ),
        "mp",
        scatter_dimension=0,
        tiled=True,
    ).astype(jnp.float32)
    seq_part = jnp.dot(pick_seq.T, input_grad, precision=highest)
    zero_row = jnp.zeros((model_width,), jnp.float32)
    query_bias_part = lax.dynamic_update_slice_in_dim(
        zero_row, jnp.sum(grad_query, axis=0), column, 0
    )
    value_bias_part = lax.dynamic_update_slice_in_dim(
        zero_row, jnp.sum(grad_value, axis=0), column, 0
    )
    bias_part = jnp.stack(
        [
            query_bias_part,
            value_bias_part,
            bias_three_part,
            shift_one_part,
            bias_five_part,
            shift_two_part,
        ]
    )
    gain_part = jnp.stack([gain_one_part, gain_two_part])
    seq_total, bias_total, gain_total, ffn_bias_total = (
        lax.psum(seq_part.astype(jnp.bfloat16), "mp").astype(jnp.float32),
        lax.psum(bias_part.astype(jnp.bfloat16), "mp").astype(jnp.float32),
        lax.psum(gain_part.astype(jnp.bfloat16), "mp").astype(jnp.float32),
        lax.psum(ffn_bias_part.astype(jnp.bfloat16), "mp").astype(jnp.float32),
    )
    bias_full = jnp.concatenate([jnp.sum(seq_total, axis=0)[None, :], bias_total], axis=0)
    time_grad_full = lax.dot_general(
        feature.astype(jnp.float32), seq_total, (((0,), (0,)), ((), ())), precision=highest
    )
    sums_out = (
        lax.psum_scatter(
            time_grad_full.astype(jnp.bfloat16), "dp", scatter_dimension=0, tiled=True
        ).astype(jnp.float32),
        lax.psum_scatter(
            qkv_grad_local.astype(jnp.bfloat16), "dp", scatter_dimension=1, tiled=True
        ).astype(jnp.float32),
        lax.psum_scatter(
            out_grad_local.astype(jnp.bfloat16), "dp", scatter_dimension=1, tiled=True
        ).astype(jnp.float32),
        lax.psum_scatter(
            in_grad_local.astype(jnp.bfloat16), "dp", scatter_dimension=0, tiled=True
        ).astype(jnp.float32),
        lax.psum_scatter(
            down_grad_local.astype(jnp.bfloat16), "dp", scatter_dimension=1, tiled=True
        ).astype(jnp.float32),
        lax.psum_scatter(
            bias_full.astype(jnp.bfloat16), "dp", scatter_dimension=1, tiled=True
        ).astype(jnp.float32),
        lax.psum_scatter(
            gain_total.astype(jnp.bfloat16), "dp", scatter_dimension=1, tiled=True
        ).astype(jnp.float32),
        lax.psum_scatter(
            ffn_bias_total.astype(jnp.bfloat16), "dp", scatter_dimension=0, tiled=True
        ).astype(jnp.float32),
    )
    return (
        layer_out,
        input_grad,
        sums_out[0],
        sums_out[1],
        sums_out[2],
        sums_out[3],
        sums_out[4],
        sums_out[5],
        sums_out[6],
        sums_out[7],
    )


def solution(mesh):
    placed = (
        P(("dp", "mp"), None),
        P("dp", None),
        P("dp"),
        P("dp", None),
        P(None, "dp", "mp"),
        P("mp", "dp"),
        P("dp", "mp"),
        P("mp", "dp"),
        P(None, "dp"),
        P(None, "dp"),
        P("dp"),
        P(("dp", "mp"), None),
    )
    return jax.shard_map(
        on_device,
        mesh=mesh,
        in_specs=placed,
        out_specs=(
            P(("dp", "mp"), None),
            P(("dp", "mp"), None),
            P("dp", None),
            P(None, "dp", "mp"),
            P("mp", "dp"),
            P("dp", "mp"),
            P("mp", "dp"),
            P(None, "dp"),
            P(None, "dp"),
            P("dp"),
        ),
        check_vma=False,
    )
```

profile of v0, /device:TPU:20, one launch (start us, length us, event | category | flops | bytes accessed | tf_op | source)
XLA Modules:
  0.0 1157.5 jit_solution(11855910216628012341)
XLA Ops:
  10.0 16.3 %all-gather = bf16[16,64,7]{1,2,0:T(8,128)(2,1)S(1)} all-gather(bf16[1,64,7]{1,2,0:T(8,128)(2,1)} %bitcast.210), channel_id=1, replica_groups=mesh['dp'=16,'mp'=2] {'dp'}, dimensions={0}, use_global_device_ids=true | all-gather | bytes 15232 | tf_op jit(solution)/shard_map/all_gather | solution.py:160
  27.1 23.8 %all-gather.13.cloned.1.call-done = bf16[1024,1024]{1,0:T(8,128)(2,1)} async-done(((bf16[64,1024]{1,0:T(8,128)(2,1)}), bf16[1024,1024]{1,0:T(8,128)(2,1)}) %all-gather.13.cloned.1.call-update) | async-done | bytes 2097168 | tf_op jit(solution)/shard_map/all_gather | solution.py:157
  59.1 39.3 %all-gather.17.cloned.1.call-done = bf16[3,1024,512]{2,1,0:T(8,128)(2,1)} async-done(((bf16[3,64,512]{2,1,0:T(8,128)(2,1)}), bf16[3,1024,512]{2,1,0:T(8,128)(2,1)}) %all-gather.17.cloned.1.call-update) | async-done | bytes 3145744 | tf_op jit(solution)/shard_map/all_gather | solution.py:155
  98.4 33.4 %all-gather.15.cloned.1.call-done = bf16[1024,1024]{1,0:T(8,128)(2,1)} async-done(((bf16[512,1024]{1,0:T(8,128)(2,1)}), bf16[1024,1024]{1,0:T(8,128)(2,1)}) %all-gather.15.cloned.1.call-update) | async-done | bytes 2097168 | tf_op jit(solution)/shard_map/all_gather | solution.py:177
  143.8 28.1 %while.49 = (s32[]{:T(128)}, bf16[2,512,8,64]{1,3,2,0:T(8,128)(2,1)}, f32[2,8,512]{2,1,0:T(8,128)S(1)}, s32[2,512]{1,0:T(2,128)S(1)}, s32[1024]{0:T(1024)S(1)}, ...) while((s32[]{:T(128)}, ...), condition=%wide.region_3.4_spmd.clone, body=%wide.region_0.3_spmd.sunk.clone | while | flops 1124593664 | bytes 64628900 | solution.py:81
  181.9 15.9 %all-gather.1 = bf16[16,64,2]{1,2,0:T(2,128)(2,1)S(1)} all-gather(bf16[1,64,2]{1,2,0:T(2,128)(2,1)S(1)} %bitcast.213), channel_id=1, replica_groups=mesh['dp'=16,'mp'=2] {'dp'}, dimensions={0}, use_global_device_ids=true | all-gather | bytes 4352 | tf_op jit(solution)/shard_map/all_gather | solution.py:161
  197.9 37.7 %reduce-scatter.16.cloned.1.call-done = f32[512,1024]{1,0:T(8,128)} async-done(((f32[1024,1024]{1,0:T(8,128)}), f32[512,1024]{1,0:T(8,128)}) %reduce-scatter.16.cloned.1.call-update) | async-done | bytes 2097168 | tf_op jit(solution)/shard_map/reduce_scatter | solution.py:197
  240.6 15.9 %all-gather.2 = bf16[16,1,256]{2,1,0:T(2,128)(2,1)S(1)} all-gather(bf16[1,1,256]{2,1,0:T(2,128)(2,1)S(1)} %reshape.266), channel_id=1, replica_groups=mesh['dp'=16,'mp'=2] {'dp'}, dimensions={0}, use_global_device_ids=true | all-gather | bytes 8704 | tf_op jit(solution)/shard_map/all_gather | solution.py:162
  256.7 31.7 %all-gather.23.cloned.1.call-done = bf16[1024,2048]{1,0:T(8,128)(2,1)} async-done(((bf16[64,2048]{1,0:T(8,128)(2,1)}), bf16[1024,2048]{1,0:T(8,128)(2,1)}) %all-gather.23.cloned.1.call-update) | async-done | bytes 4194320 | tf_op jit(solution)/shard_map/all_gather | solution.py:158
  288.4 33.4 %all-gather.21.cloned.1.call-done = bf16[1024,1024]{1,0:T(8,128)(2,1)} async-done(((bf16[512,1024]{1,0:T(8,128)(2,1)}), bf16[1024,1024]{1,0:T(8,128)(2,1)}) %all-gather.21.cloned.1.call-update) | async-done | bytes 2097168 | tf_op jit(solution)/shard_map/all_gather | solution.py:206
  321.8 26.2 %multiply_convert_fusion.1 = (bf16[1024,2048]{1,0:T(8,128)(2,1)}, f32[1024,2048]{1,0:T(8,128)}, f32[1024,2048]{1,0:T(8,128)}) fusion(f32[2048]{0:T(1024)S(1)} %dynamic-slice_convert_fusion, bf16[1024,1024]{1,0:T(8,128)(2,1)} %all-gather.21.cloned.1.call-done, bf16[1024,2048]{1,0:T(8,128)(2,1)} %all-gather.23.cloned.1.call-done), kind=kOutput, calls=%fused_computation.55 | convolution fusion | flops 4433379328 | bytes 27271168 | tf_op jit(solution)/shard_map/dot_general | solution.py:208
  348.0 26.8 %all-gather.25.cloned.1.call-done = bf16[2048,1024]{0,1:T(8,128)(2,1)} async-done(((bf16[2048,64]{0,1:T(8,128)(2,1)}), bf16[2048,1024]{0,1:T(8,128)(2,1)}) %all-gather.25.cloned.1.call-update) | async-done | bytes 4194320 | tf_op jit(solution)/shard_map/all_gather | solution.py:159
  374.7 9.3 convolution_convert_fusion.2
  384.4 30.0 %reduce-scatter.18.cloned.1.call-done = bf16[512,1024]{1,0:T(8,128)(2,1)} async-done(((bf16[1024,1024]{1,0:T(8,128)(2,1)}), bf16[512,1024]{1,0:T(8,128)(2,1)}) %reduce-scatter.18.cloned.1.call-update) | async-done | bytes 1048592 | tf_op jit(solution)/shard_map/reduce_scatter | solution.py:210
  420.7 33.2 %all-gather.27.cloned.1.call-done = bf16[1024,1024]{1,0:T(8,128)(2,1)} async-done(((bf16[512,1024]{1,0:T(8,128)(2,1)}), bf16[1024,1024]{1,0:T(8,128)(2,1)}) %all-gather.27.cloned.1.call-update) | async-done | bytes 2097168 | tf_op jit(solution)/shard_map/all_gather | solution.py:231
  453.9 13.9 %fusion.87 = (bf16[2048]{0:T(1024)(128)(2,1)}, bf16[1024,2048]{1,0:T(8,128)(2,1)S(1)}) fusion(f32[1024,2048]{1,0:T(8,128)} %get-tuple-element.320, f32[1024,2048]{1,0:T(8,128)} %get-tuple-element.341, f32[2048]{0:T(1024)S(1)} %dynamic-slice_convert_fusion, bf16[1024,1024]{1,0:T(8,128)(2,1)} %all-gather.27.cloned.1.call-done, ...), kind=kOutput, calls=%fused_computation.157 | convolution fusion | flops 4328519680 | bytes 27275264 | tf_op jit(solution)/shard_map/dot_general | solution.py:53
  475.7 32.0 %reduce-scatter.20.cloned.1.call-done = bf16[512,1024]{1,0:T(8,128)(2,1)} async-done(((bf16[1024,1024]{1,0:T(8,128)(2,1)}), bf16[512,1024]{1,0:T(8,128)(2,1)}) %reduce-scatter.20.cloned.1.call-update) | async-done | bytes 1048592 | tf_op jit(solution)/shard_map/reduce_scatter | solution.py:240
  516.3 32.2 %all-gather.29.cloned.1.call-done = bf16[1024,1024]{1,0:T(8,128)(2,1)} async-done(((bf16[512,1024]{1,0:T(8,128)(2,1)}), bf16[1024,1024]{1,0:T(8,128)(2,1)}) %all-gather.29.cloned.1.call-update) | async-done | bytes 2097168 | tf_op jit(solution)/shard_map/all_gather | solution.py:248
  559.7 134.2 %while.50 = (s32[]{:T(128)}, f32[1024,8,64]{0,2,1:T(8,128)}, f32[1024,8,64]{0,2,1:T(8,128)S(1)}, f32[2,512,8,64]{1,3,2,0:T(8,128)}, bf16[2,512,8,64]{1,3,2,0:T(8...) while((s32[]{:T(128)}, f32[1024,8,64]{0,2,1:T(8,128)}, ...), condition=%wide.region_17.18_spmd.clone.clone, body=%wide.region_15.17_spmd.clone.sunk.clone | while | flops 2745706496 | bytes 271640800 | solution.py:120
  580.4 23.5 %bitcast_add_fusion.6 = f32[1024,8,64]{0,2,1:T(8,128)} fusion(f32[1024,8,64]{0,2,1:T(8,128)} %get-tuple-element.549, f32[8,512,1024]{2,1,0:T(8,128)} %copy-done, f32[8,512,1024]{2,1,0:T(8,128)} %fusion.179, pred[]{:T(512)S(6)} %compare.14, bf16[2,512,8,64]{1,3,2,0:T(8,128)(2,1)} %get-tuple-element.563, s32[]{:T(128)S(6)} %copy.83), kind=kOutput, calls=%fused_computation.29.clone.1.clone | convolution fusion | flops 558896128 | bytes 71827464 | tf_op jit(solution)/shard_map/while/body/eval_jaxpr/while/body/eval_jaxpr/hqk,qhd->khd/dot_general | solution.py:107
  603.9 22.9 %fusion.180 = f32[2,512,8,64]{1,3,2,0:T(8,128)} fusion(f32[2,512,8,64]{1,3,2,0:T(8,128)} %get-tuple-element.551, s32[]{:T(128)S(6)} %copy.83, bf16[1024,8,64]{0,2,1:T(8,128)(2,1)} %get-tuple-element.566, f32[8,512,1024]{2,1,0:T(8,128)} %copy-done, f32[8,512,1024]{2,1,0:T(8,128)} %fusion.179), kind=kOutput, calls=%fused_computation.31.clone.1.clone | convolution fusion | flops 557847552 | bytes 69206016 | tf_op jit(solution)/shard_map/while/body/eval_jaxpr/while/body/eval_jaxpr/hqk,khd->qhd/dot_general | solution.py:104
  647.1 23.9 %bitcast_add_fusion.6 = f32[1024,8,64]{0,2,1:T(8,128)} fusion(f32[1024,8,64]{0,2,1:T(8,128)} %get-tuple-element.549, f32[8,512,1024]{2,1,0:T(8,128)} %copy-done, f32[8,512,1024]{2,1,0:T(8,128)} %fusion.179, pred[]{:T(512)S(6)} %compare.14, bf16[2,512,8,64]{1,3,2,0:T(8,128)(2,1)} %get-tuple-element.563, s32[]{:T(128)S(6)} %copy.83), kind=kOutput, calls=%fused_computation.29.clone.1.clone | convolution fusion | flops 558896128 | bytes 71827464 | tf_op jit(solution)/shard_map/while/body/eval_jaxpr/while/body/eval_jaxpr/hqk,qhd->khd/dot_general | solution.py:107
  671.0 22.9 %fusion.180 = f32[2,512,8,64]{1,3,2,0:T(8,128)} fusion(f32[2,512,8,64]{1,3,2,0:T(8,128)} %get-tuple-element.551, s32[]{:T(128)S(6)} %copy.83, bf16[1024,8,64]{0,2,1:T(8,128)(2,1)} %get-tuple-element.566, f32[8,512,1024]{2,1,0:T(8,128)} %copy-done, f32[8,512,1024]{2,1,0:T(8,128)} %fusion.179), kind=kOutput, calls=%fused_computation.31.clone.1.clone | convolution fusion | flops 557847552 | bytes 69206016 | tf_op jit(solution)/shard_map/while/body/eval_jaxpr/while/body/eval_jaxpr/hqk,khd->qhd/dot_general | solution.py:104
  712.6 8.3 convolution_convert_fusion
  722.5 8.3 convolution_convert_fusion.1
  741.8 23.6 %all-reduce = bf16[4096]{0:T(1024)(128)(2,1)S(1)} all-reduce(bf16[4096]{0:T(1024)(128)(2,1)S(1)} %dynamic_update_slice.36), channel_id=13, replica_groups=mesh['dp'=16,'mp'=2] {'dp'}, use_global_device_ids=true, to_apply=%region_39.40.clone | all-reduce | flops 4096 | bytes 16384
  788.2 32.7 %reduce-scatter.32.cloned.1.call-done = bf16[2048,64]{0,1:T(8,128)(2,1)} async-done(((bf16[2048,1024]{0,1:T(8,128)(2,1)}), bf16[2048,64]{0,1:T(8,128)(2,1)}) %reduce-scatter.32.cloned.1.call-update) | async-done | bytes 262160 | tf_op jit(solution)/shard_map/reduce_scatter | solution.py:322
  822.7 73.6 %reduce-scatter.30.cloned.1.call-done = bf16[64,2048]{1,0:T(8,128)(2,1)} async-done(((bf16[1024,2048]{1,0:T(8,128)(2,1)}), bf16[64,2048]{1,0:T(8,128)(2,1)}) %reduce-scatter.30.cloned.1.call-update) | async-done | bytes 262160 | tf_op jit(solution)/shard_map/reduce_scatter | solution.py:319
  898.1 58.6 %reduce-scatter.28.cloned.1.call-done = bf16[512,64]{0,1:T(8,128)(2,1)} async-done(((bf16[512,1024]{0,1:T(8,128)(2,1)}), bf16[512,64]{0,1:T(8,128)(2,1)}) %reduce-scatter.28.cloned.1.call-update) | async-done | bytes 65552 | tf_op jit(solution)/shard_map/reduce_scatter | solution.py:316
  959.3 56.1 %reduce-scatter.34.cloned.1.call-done = bf16[64,7]{1,0:T(8,128)(2,1)} async-done(((bf16[1024,7]{1,0:T(8,128)(2,1)}), bf16[64,7]{1,0:T(8,128)(2,1)}) %reduce-scatter.34.cloned.1.call-update) | async-done | bytes 912
  1016.8 67.6 %reduce-scatter.26.cloned.1.call-done = bf16[3,64,512]{2,1,0:T(8,128)(2,1)} async-done(((bf16[3,1024,512]{2,1,0:T(8,128)(2,1)}), bf16[3,64,512]{2,1,0:T(8,128)(2,1)}) %reduce-scatter.26.cloned.1.call-update) | async-done | bytes 196624 | tf_op jit(solution)/shard_map/reduce_scatter | solution.py:313
  1086.1 62.7 %reduce-scatter.24.cloned.1.call-done = bf16[64,1024]{1,0:T(8,128)(2,1)} async-done(((bf16[1024,1024]{1,0:T(8,128)(2,1)}), bf16[64,1024]{1,0:T(8,128)(2,1)}) %reduce-scatter.24.cloned.1.call-update) | async-done | bytes 131088 | tf_op jit(solution)/shard_map/reduce_scatter | solution.py:310
  (261 shorter events, 204.5 us)
Async XLA Ops:
  7.2 51.1 %copy-start.18 = (s32[1,1024]{1,0:T(1,128)S(1)}, s32[1,1024]{1,0:T(1,128)}, u32[]{:S(2)}) copy-start(s32[1,1024]{1,0:T(1,128)} %param.17) | copy-start | bytes 12292
  7.2 43.7 %all-gather.13.cloned.1.call-start = ((), (), s32[]{:S(2)}) async-start(), calls=%async_computation.11 | async-start | bytes 2228224 | tf_op jit(solution)/shard_map/all_gather | solution.py:157
  7.9 90.4 %all-gather.17.cloned.1.call-start = ((), (), s32[]{:S(2)}) async-start(), calls=%async_computation.13 | async-start | bytes 3342336 | tf_op jit(solution)/shard_map/all_gather | solution.py:155
  8.7 123.1 %all-gather.15.cloned.1.call-start = ((), (), s32[]{:S(2)}) async-start(), calls=%async_computation.12 | async-start | bytes 3145728 | tf_op jit(solution)/shard_map/all_gather | solution.py:177
  26.5 105.3 %copy-start.22 = (f32[512]{0:T(512)}, f32[512]{0:T(512)S(1)}, u32[]{:S(2)}) copy-start(f32[512]{0:T(512)S(1)} %fusion.85) | copy-start | bytes 6148
  56.0 120.2 %all-gather.19.cloned.1.call-start = ((), (), s32[]{:S(2)}) async-start(), calls=%async_computation.14 | async-start | bytes 1114112 | tf_op jit(solution)/shard_map/all_gather | solution.py:156
  56.6 179.0 %reduce-scatter.16.cloned.1.call-start = ((), (), s32[]{:S(2)}) async-start(), calls=%async_computation.15 | async-start | bytes 6291456 | tf_op jit(solution)/shard_map/reduce_scatter | solution.py:197
  181.0 54.6 %copy-start.21 = (f32[1024]{0:T(1024)S(1)}, f32[1024]{0:T(1024)}, u32[]{:S(2)}) copy-start(f32[1024]{0:T(1024)} %copy-done.20) | copy-start | bytes 12292
  181.0 54.6 %copy-start.23 = (f32[512]{0:T(512)S(1)}, f32[512]{0:T(512)}, u32[]{:S(2)}) copy-start(f32[512]{0:T(512)} %copy-done.22) | copy-start | bytes 6148
  181.0 54.6 %copy-start.27 = (f32[1,1024]{1,0:T(1,128)S(1)}, f32[1,1024]{1,0:T(1,128)}, u32[]{:S(2)}) copy-start(f32[1,1024]{1,0:T(1,128)} %get-tuple-element.333) | copy-start | bytes 12292
  181.0 57.4 %copy-start.19 = (f32[1,1024]{1,0:T(1,128)S(1)}, f32[1,1024]{1,0:T(1,128)}, u32[]{:S(2)}) copy-start(f32[1,1024]{1,0:T(1,128)} %get-tuple-element.332) | copy-start | bytes 12292
  181.1 107.3 %all-gather.23.cloned.1.call-start = ((), (), s32[]{:S(2)}) async-start(), calls=%async_computation.17 | async-start | bytes 4456448 | tf_op jit(solution)/shard_map/all_gather | solution.py:158
  181.6 140.2 %all-gather.21.cloned.1.call-start = ((), (), s32[]{:S(2)}) async-start(), calls=%async_computation.16 | async-start | bytes 3145728 | tf_op jit(solution)/shard_map/all_gather | solution.py:206
  239.8 134.9 %all-gather.25.cloned.1.call-start = ((), (), s32[]{:S(2)}) async-start(), calls=%async_computation.18 | async-start | bytes 4456448 | tf_op jit(solution)/shard_map/all_gather | solution.py:159
  240.6 173.8 %reduce-scatter.18.cloned.1.call-start = ((), (), s32[]{:S(2)}) async-start(), calls=%async_computation.19 | async-start | bytes 3145728 | tf_op jit(solution)/shard_map/reduce_scatter | solution.py:210
  374.7 39.6 %copy-start.25 = (f32[1,1024]{1,0:T(1,128)S(1)}, f32[1,1024]{1,0:T(1,128)}, u32[]{:S(2)}) copy-start(f32[1,1024]{1,0:T(1,128)} %get-tuple-element.331) | copy-start | bytes 12292
  384.1 69.8 %all-gather.27.cloned.1.call-start = ((), (), s32[]{:S(2)}) async-start(), calls=%async_computation.20 | async-start | bytes 3145728 | tf_op jit(solution)/shard_map/all_gather | solution.py:231
  420.7 87.0 %reduce-scatter.20.cloned.1.call-start = ((), (), s32[]{:S(2)}) async-start(), calls=%async_computation.21 | async-start | bytes 3145728 | tf_op jit(solution)/shard_map/reduce_scatter | solution.py:240
  475.6 72.9 %all-gather.29.cloned.1.call-start = ((), (), s32[]{:S(2)}) async-start(), calls=%async_computation.22 | async-start | bytes 3145728 | tf_op jit(solution)/shard_map/all_gather | solution.py:248
  515.2 250.4 %reduce-scatter.36.cloned.1.call-start = ((), (), s32[]{:S(2)}) async-start(), calls=%async_computation.30 | async-start | bytes 278528
  516.3 250.4 %reduce-scatter.22.cloned.1.call-start = ((), (), s32[]{:S(2)}) async-start(), calls=%async_computation.23 | async-start | bytes 3145728 | tf_op jit(solution)/shard_map/reduce_scatter | solution.py:272
  712.5 108.4 %reduce-scatter.32.cloned.1.call-start = ((), (), s32[]{:S(2)}) async-start(), calls=%async_computation.28 | async-start | bytes 4456448 | tf_op jit(solution)/shard_map/reduce_scatter | solution.py:322
  720.9 175.4 %reduce-scatter.30.cloned.1.call-start = ((), (), s32[]{:S(2)}) async-start(), calls=%async_computation.27 | async-start | bytes 4456448 | tf_op jit(solution)/shard_map/reduce_scatter | solution.py:319
  730.9 225.8 %reduce-scatter.28.cloned.1.call-start = ((), (), s32[]{:S(2)}) async-start(), calls=%async_computation.26 | async-start | bytes 1114112 | tf_op jit(solution)/shard_map/reduce_scatter | solution.py:316
  735.9 29.6 %copy-start.30 = (bf16[1024]{0:T(1024)(128)(2,1)S(1)}, bf16[1024]{0:T(1024)(128)(2,1)}, u32[]{:S(2)}) copy-start(bf16[1024]{0:T(1024)(128)(2,1)} %get-tuple-element.313) | copy-start | bytes 6148
  735.9 29.6 %copy-start.29 = (bf16[1024]{0:T(1024)(128)(2,1)S(1)}, bf16[1024]{0:T(1024)(128)(2,1)}, u32[]{:S(2)}) copy-start(bf16[1024]{0:T(1024)(128)(2,1)} %get-tuple-element.266) | copy-start | bytes 6148
  735.9 29.6 %copy-start.28 = (bf16[1024]{0:T(1024)(128)(2,1)S(1)}, bf16[1024]{0:T(1024)(128)(2,1)}, u32[]{:S(2)}) copy-start(bf16[1024]{0:T(1024)(128)(2,1)} %get-tuple-element.267) | copy-start | bytes 6148
  736.0 30.7 %copy-start.5 = (f32[512,1024]{1,0:T(8,128)S(1)}, f32[512,1024]{1,0:T(8,128)}, u32[]{:S(2)}) copy-start(f32[512,1024]{1,0:T(8,128)} %copy-done.4) | copy-start | bytes 6291460
  736.0 279.4 %reduce-scatter.34.cloned.1.call-start = ((), (), s32[]{:S(2)}) async-start(), calls=%async_computation.29 | async-start | bytes 278528
  741.5 38.1 %copy-start.16 = (bf16[1,1024,512]{2,1,0:T(8,128)(2,1)S(1)}, bf16[1,1024,512]{2,1,0:T(8,128)(2,1)}, u32[]{:S(2)}) copy-start(bf16[1,1024,512]{2,1,0:T(8,128)(2,1)} %copy-done.15) | copy-start | bytes 3145732
  779.6 304.8 %reduce-scatter.26.cloned.1.call-start = ((), (), s32[]{:S(2)}) async-start(), calls=%async_computation.25 | async-start | bytes 3342336 | tf_op jit(solution)/shard_map/reduce_scatter | solution.py:313
  786.3 362.5 %reduce-scatter.24.cloned.1.call-start = ((), (), s32[]{:S(2)}) async-start(), calls=%async_computation.24 | async-start | bytes 2228224 | tf_op jit(solution)/shard_map/reduce_scatter | solution.py:310
  (31 other events, 138.5 us)
Sparse Core Ops, SparseCore 0:
  10.2 40.7 all-gather.12
  53.1 45.2 all-gather.16
  100.5 31.2 all-gather.14
  133.8 37.2 all-gather.18
  181.2 54.3 reduce-scatter.15
  237.6 50.7 all-gather.22
  290.5 31.2 all-gather.20
  324.0 50.7 all-gather.24
  384.2 30.0 reduce-scatter.17
  420.8 33.0 all-gather.26
  475.7 31.8 reduce-scatter.19
  515.3 33.0 all-gather.28
  552.6 55.7 reduce-scatter.35
  712.6 31.9 reduce-scatter.21
  748.3 72.5 reduce-scatter.31
  824.6 71.6 reduce-scatter.29
  899.8 56.8 reduce-scatter.27
  960.7 54.7 reduce-scatter.33
  1019.2 65.1 reduce-scatter.25
  1088.0 60.7 reduce-scatter.23
where the time goes:
time: 1160 us
  waiting for transfers between devices  708 us (61%)
  matrix products  253 us (22%)
  blocking collectives  80 us (7%)
  other arithmetic  50 us (4%)
  local copies, waits for them, and re-layouts  48.4 us (4%)
  between operations  16.4 us (1%)
    reduce_scatter x1, waiting for transfers between devices, on_device(): lax.psum_scatter(in_grad_local.astype(jnp.bfloat16), 'dp', scatter_dimens...  73.6 us
    reduce_scatter x1, waiting for transfers between devices, on_device(): lax.psum_scatter(qkv_grad_local.astype(jnp.bfloat16), 'dp', scatter_dimen...  67.6 us
    reduce_scatter x1, waiting for transfers between devices, on_device(): lax.psum_scatter(time_grad_full.astype(jnp.bfloat16), 'dp', scatter_dimen...  62.7 us
    unnamed x22, waiting for transfers between devices  59.5 us
    reduce_scatter x1, waiting for transfers between devices, on_device(): lax.psum_scatter(out_grad_local.astype(jnp.bfloat16), 'dp', scatter_dimen...  58.6 us
    dot_general x2, matrix products, per_block(): jnp.einsum('hqk,qhd->khd', grad_score, q_block, preferred_element_type=jn...  47.4 us
    dot_general x2, matrix products, per_block(): jnp.einsum('hqk,khd->qhd', grad_score, key_rows, preferred_element_type=j...  45.8 us
    all_gather x1, waiting for transfers between devices, on_device(): lax.all_gather(qkv_weight, 'dp', axis=1, tiled=True)  39.3 us
  transfers between devices with their start and end apart: 20, of which 17 were waited for; matrix products, arithmetic and copies ran while one was open for 25% of the time, Pallas kernels for 0%

commit v1 on v0

v1 whole, which is shorter than its diff:
```python
import functools
import math

import jax
import jax.numpy as jnp
from jax import lax
from jax.experimental import pallas as pl
from jax.experimental.pallas import tpu as pltpu
from jax.sharding import PartitionSpec as P

HD = 64
eps = 1e-05
neg_big = -1000000000.0
MESH = pl.DeviceIdType.MESH
F32, BF16 = jnp.float32, jnp.bfloat16
VMEM_LIMIT = 64000000


def dg(left, right, left_dim, right_dim):
    return lax.dot_general(
        left, right, (((left_dim,), (right_dim,)), ((), ())), preferred_element_type=F32
    )


def place():
    i, y = lax.axis_index("dp"), lax.axis_index("mp")
    return i // 4, (i // 2) % 2, i % 2, y


def z_places(z):
    return [(z // 2) * 2 + 1 - z % 2, (z + 2) % 4, 3 - z]


def peers(z, x, c, y):
    def at(z_, x_, c_, y_):
        return ((z_ * 2 + x_) * 2 + c_, y_)

    return {
        "z": [at(p, x, c, y) for p in z_places(z)],
        "x": at(z, 1 - x, c, y),
        "y": at(z, x, c, 1 - y),
        "c": at(z, x, 1 - c, y),
    }


def enter(near):
    barrier = pltpu.get_barrier_semaphore()
    everyone = near["z"] + [near["x"], near["y"], near["c"]]
    for one in everyone:
        pl.semaphore_signal(barrier, inc=1, device_id=one, device_id_type=MESH)
    pl.semaphore_wait(barrier, len(everyone))


class Wire:
    def __init__(self, send_sems, recv_sems):
        self.send_sems, self.recv_sems, self.used, self.open = send_sems, recv_sems, 0, []

    def send(self, src, dst, to):
        k = self.used
        self.used += 1
        copy = pltpu.make_async_remote_copy(
            src_ref=src,
            dst_ref=dst,
            send_sem=self.send_sems.at[k],
            recv_sem=self.recv_sems.at[k],
            device_id=to,
            device_id_type=MESH,
        )
        copy.start()
        self.open.append(copy)
        return copy

    def close(self):
        assert self.used == self.send_sems.shape[0] == self.recv_sems.shape[0]
        for copy in self.open:
            copy.wait_send()


def gather_dp(wire, near, here, shard, whole):
    z, x, c, y = here
    own = whole.at[z, x, c]
    from_z = [wire.send(shard, own, to) for to in near["z"]]
    late = [wire.send(shard, own, near["c"])]
    yield
    for k in from_z:
        k.wait_recv()
    ref = whole.at[:, x, c]
    from_x = wire.send(ref, ref, near["x"])
    for p in z_places(z):
        ref = whole.at[p, x, c]
        late.append(wire.send(ref, ref, near["c"]))
    yield
    from_x.wait_recv()
    ref = whole.at[:, 1 - x, c]
    late.append(wire.send(ref, ref, near["c"]))
    yield
    for k in late:
        k.wait_recv()


def gather_all(wire, near, here, shard, whole, lo, mid, hi):
    z, x, c, y = here
    a, b, ab = pl.ds(lo, mid - lo), pl.ds(mid, hi - mid), pl.ds(lo, hi - lo)
    own = whole.at[y, z, x, c, :, ab]
    from_z = [wire.send(shard.at[:, ab], own, to) for to in near["z"]]
    late = [wire.send(shard.at[:, ab], own, near["c"])]
    yield
    for k in from_z:
        k.wait_recv()
    ref = whole.at[y, :, x, c, :, a]
    from_x_a = wire.send(ref, ref, near["x"])
    ref = whole.at[y, :, x, c, :, b]
    from_y_b = wire.send(ref, ref, near["y"])
    for p in z_places(z):
        ref = whole.at[y, p, x, c, :, ab]
        late.append(wire.send(ref, ref, near["c"]))
    yield
    from_x_a.wait_recv()
    ref = whole.at[y, :, :, c, :, a]
    from_y_a = wire.send(ref, ref, near["y"])
    from_y_b.wait_recv()
    ref = whole.at[:, :, x, c, :, b]
    from_x_b = wire.send(ref, ref, near["x"])
    for ref in (whole.at[y, :, 1 - x, c, :, a], whole.at[1 - y, :, x, c, :, b]):
        late.append(wire.send(ref, ref, near["c"]))
    yield
    from_y_a.wait_recv()
    from_x_b.wait_recv()
    for ref in (whole.at[1 - y, :, :, c, :, a], whole.at[:, :, 1 - x, c, :, b]):
        late.append(wire.send(ref, ref, near["c"]))
    yield
    for k in late:
        k.wait_recv()


def parts_of(width, parts):
    step = width // parts
    return [(p * step, p * step + step // 2, (p + 1) * step) for p in range(parts)]


def stagger(streams, ahead=0):
    for depth in range(ahead, len(streams) + 6):
        for k, s in enumerate(streams):
            if k <= depth:
                next(s, None)


def gather_kernel(
    v_ref, o_ref, i_ref, d_ref, h_ref, v_all, o_all, i_all, d_all, h_all, send_sems, recv_sems, local_sems
):
    here = place()
    z, x, c, y = here
    near = peers(*here)
    enter(near)
    wire = Wire(send_sems, recv_sems)
    first = gather_dp(wire, near, here, v_ref, v_all)
    next(first)
    from_y = wire.send(h_ref, h_all.at[y], near["y"])
    kept = (
        (v_ref, v_all.at[z, x, c]),
        (o_ref, o_all.at[y, z, x, c]),
        (i_ref, i_all.at[y, z, x, c]),
        (d_ref, d_all.at[y, z, x, c]),
        (h_ref, h_all.at[y]),
    )
    own = [pltpu.make_async_copy(s, d, local_sems.at[k]) for k, (s, d) in enumerate(kept)]
    for k in own:
        k.start()
    streams = [
        gather_all(wire, near, here, shard, whole, *cut)
        for shard, whole, parts in ((o_ref, o_all, 1), (i_ref, i_all, 2), (d_ref, d_all, 2))
        for cut in parts_of(shard.shape[1], parts)
    ]
    for s in streams:
        next(s)
    for k in own:
        k.wait()
    stagger([first] + streams)
    from_y.wait_recv()
    wire.close()


def gather_weights(v, o, i, d, h):
    def whole(a, lead):
        return jax.ShapeDtypeStruct(lead + a.shape, a.dtype)

    dp3 = (4, 2, 2)
    copies = 9 + 15 * 5 + 1
    return pl.pallas_call(
        gather_kernel,
        name="gather_weights",
        out_shape=[
            whole(v, dp3),
            whole(o, (2,) + dp3),
            whole(i, (2,) + dp3),
            whole(d, (2,) + dp3),
            whole(h, (2,)),
        ],
        in_specs=[pl.BlockSpec(memory_space=pltpu.VMEM)] * 5,
        out_specs=[pl.BlockSpec(memory_space=pl.ANY)] * 5,
        scratch_shapes=[
            pltpu.SemaphoreType.DMA((copies,)),
            pltpu.SemaphoreType.DMA((copies,)),
            pltpu.SemaphoreType.DMA((5,)),
        ],
        compiler_params=pltpu.CompilerParams(
            collective_id=0, has_side_effects=True, vmem_limit_bytes=16 * 1024 * 1024
        ),
    )(v, o, i, d, h)


def add_blocks(dst, left, right, lead):
    count = math.prod(lead)

    def one(t, _):
        at = []
        for n in reversed(lead):
            at.append(t % n)
            t = t // n
        at = tuple(reversed(at))
        dst[at] = (left[at].astype(F32) + right[at].astype(F32)).astype(dst.dtype)
        return 0

    lax.fori_loop(0, count, one, 0)


def reduce_dp(wire, near, here, grad, rc, rx, rz, out):
    z, x, c, y = here
    from_c = wire.send(grad.at[:, :, 1 - c], rc, near["c"])
    yield
    from_c.wait_recv()
    add_blocks(rc, grad.at[:, :, c], rc, (4, 2))
    from_x = wire.send(rc.at[:, 1 - x], rx, near["x"])
    yield
    from_x.wait_recv()
    add_blocks(rx, rc.at[:, x], rx, (4,))
    from_z = [wire.send(rx.at[p], rz.at[j], to) for j, (p, to) in enumerate(zip(z_places(z), near["z"]))]
    yield
    for k in from_z:
        k.wait_recv()
    out[...] = ((rx[z].astype(F32) + rz[0].astype(F32)) + rz[1].astype(F32)) + rz[2].astype(F32)


def reduce_all(wire, near, here, grad, rc, ya, xb, xa, yb, rz, out, lo, mid, hi):
    z, x, c, y = here
    a, b, ab = pl.ds(lo, mid - lo), pl.ds(mid, hi - mid), pl.ds(lo, hi - lo)
    half_a, half_b = pl.ds(0, mid - lo), pl.ds(mid - lo, hi - mid)
    from_c = wire.send(grad.at[:, :, :, 1 - c, :, ab], rc, near["c"])
    yield
    from_c.wait_recv()
    add_blocks(rc, grad.at[:, :, :, c, :, ab], rc, (2, 4, 2))
    from_y_a = wire.send(rc.at[1 - y, :, :, :, half_a], ya, near["y"])
    from_x_b = wire.send(rc.at[:, :, 1 - x, :, half_b], xb, near["x"])
    yield
    from_y_a.wait_recv()
    add_blocks(ya, rc.at[y, :, :, :, half_a], ya, (4, 2))
    from_x_a = wire.send(ya.at[:, 1 - x], xa, near["x"])
    from_x_b.wait_recv()
    add_blocks(xb, rc.at[:, :, x, :, half_b], xb, (2, 4))
    from_y_b = wire.send(xb.at[1 - y], yb, near["y"])
    yield
    from_x_a.wait_recv()
    add_blocks(xa, ya.at[:, x], xa, (4,))
    from_y_b.wait_recv()
    add_blocks(yb, xb.at[y], yb, (4,))
    from_z = []
    for j, (p, to) in enumerate(zip(z_places(z), near["z"])):
        from_z.append(wire.send(xa.at[p], rz.at[j, :, half_a], to))
        from_z.append(wire.send(yb.at[p], rz.at[j, :, half_b], to))
    yield
    for k in from_z:
        k.wait_recv()
    for acc, half, cols in ((xa, half_a, a), (yb, half_b, b)):
        out[:, cols] = (
            (acc[z].astype(F32) + rz[0, :, half].astype(F32)) + rz[1, :, half].astype(F32)
        ) + rz[2, :, half].astype(F32)


def reduce_small(wire, near, here, mine, sums, got, out):
    k = wire.send(mine, got.at[0], near["c"])
    yield
    k.wait_recv()
    sums[0] = mine[...] + got[0]
    k = wire.send(sums.at[0], got.at[1], near["x"])
    yield
    k.wait_recv()
    sums[1] = sums[0] + got[1]
    k = wire.send(sums.at[1], got.at[2], near["y"])
    yield
    k.wait_recv()
    sums[2] = sums[1] + got[2]
    last = [wire.send(sums.at[2], got.at[3 + j], to) for j, to in enumerate(near["z"])]
    yield
    for k in last:
        k.wait_recv()
    out[...] = ((sums[2] + got[3]) + got[4]) + got[5]


ALL_CUTS = (1, 2, 2)


def reduce_kernel(v_g, o_g, i_g, d_g, x_part, small, v_out, o_out, i_out, d_out, x_got, s_out, *rest):
    here = place()
    z, x, c, y = here
    near = peers(*here)
    enter(near)
    rest = list(rest)
    send_sems, recv_sems = rest[0], rest[1]
    scratch = iter(rest[2:])
    wire = Wire(send_sems, recv_sems)
    sums, got = next(scratch), next(scratch)
    tiny = reduce_small(wire, near, here, small, sums, got, s_out)
    from_y = wire.send(x_part.at[1 - y], x_got, near["y"])
    streams = []
    for grad, out, parts in ((d_g, d_out, ALL_CUTS[2]), (i_g, i_out, ALL_CUTS[1]), (o_g, o_out, ALL_CUTS[0])):
        for cut in parts_of(out.shape[1], parts):
            bufs = [next(scratch) for _ in range(6)]
            streams.append(reduce_all(wire, near, here, grad, *bufs, out, *cut))
    bufs = [next(scratch) for _ in range(3)]
    streams.append(reduce_dp(wire, near, here, v_g, *bufs, v_out))
    stagger([tiny] + streams)
    from_y.wait_recv()
    wire.close()


def reduce_grads(v_g, o_g, i_g, d_g, x_part, small):
    rows = v_g.shape[-2]
    out = [jax.ShapeDtypeStruct((rows, a.shape[-1]), F32) for a in (v_g, o_g, i_g, d_g)]
    scratch = [pltpu.VMEM((3,) + small.shape, F32), pltpu.VMEM((6,) + small.shape, F32)]
    copies = 6 + 1
    for a, parts in ((d_g, ALL_CUTS[2]), (i_g, ALL_CUTS[1]), (o_g, ALL_CUTS[0])):
        n = a.shape[-1] // parts
        h = n // 2
        for _ in range(parts):
            copies += 11
            scratch += [
                pltpu.VMEM(s, BF16)
                for s in (
                    (2, 4, 2, rows, n),
                    (4, 2, rows, h),
                    (2, 4, rows, h),
                    (4, rows, h),
                    (4, rows, h),
                    (3, rows, n),
                )
            ]
    n = v_g.shape[-1]
    copies += 5
    scratch += [pltpu.VMEM(s, BF16) for s in ((4, 2, rows, n), (4, rows, n), (3, rows, n))]
    vm = pl.BlockSpec(memory_space=pltpu.VMEM)
    hbm = pl.BlockSpec(memory_space=pl.ANY)
    return pl.pallas_call(
        reduce_kernel,
        name="reduce_grads",
        out_shape=out
        + [jax.ShapeDtypeStruct(x_part.shape[1:], x_part.dtype), jax.ShapeDtypeStruct(small.shape, F32)],
        in_specs=[vm] * 4 + [hbm, vm],
        out_specs=[vm] * 4 + [hbm, vm],
        scratch_shapes=[pltpu.SemaphoreType.DMA((copies,)), pltpu.SemaphoreType.DMA((copies,))] + scratch,
        compiler_params=pltpu.CompilerParams(
            collective_id=1, has_side_effects=True, vmem_limit_bytes=VMEM_LIMIT
        ),
    )(v_g, o_g, i_g, d_g, x_part, small)


def attend_kernel(tile, q_ref, k_ref, v_ref, sr_ref, sc_ref, o_ref, l_ref):
    length, width = q_ref.shape

    def step(t, _):
        rows = pl.ds(pl.multiple_of(t * tile, tile), tile)
        same = sc_ref[:, 0:1] == sr_ref[:, rows]
        for h in range(width // HD):
            cols = slice(h * HD, h * HD + HD)
            scores = dg(k_ref[:, cols], q_ref[rows, cols], 1, 1) * (1.0 / math.sqrt(HD))
            scores = jnp.where(same, scores, neg_big)
            row_max = jnp.max(scores, axis=0, keepdims=True)
            prob = jnp.exp(scores - row_max)
            total = jnp.sum(prob, axis=0, keepdims=True)
            mixed = dg(v_ref[:, cols], prob.astype(BF16), 0, 0) / total
            o_ref[rows, cols] = mixed.T.astype(BF16)
            l_ref[0, h : h + 1, rows] = row_max + jnp.log(total)
        return 0

    lax.fori_loop(0, length // tile, step, 0)


def attend_specs(length, heads_pairs):
    def col(k):
        return pl.BlockSpec((length, 2 * HD), lambda i, k=k: (0, k * heads_pairs + i))

    stats = pl.BlockSpec((1, 2, length), lambda i: (i, 0, 0))
    seg_row = pl.BlockSpec((1, length), lambda i: (0, 0))
    seg_col = pl.BlockSpec((length, 128), lambda i: (0, 0))
    return col, stats, seg_row, seg_col


def attend(qkv, segments):
    length = qkv.shape[0]
    pairs = qkv.shape[1] // 3 // (2 * HD)
    col, stats, seg_row, seg_col = attend_specs(length, pairs)
    return pl.pallas_call(
        functools.partial(attend_kernel, min(512, length)),
        name="attend",
        grid=(pairs,),
        in_specs=[col(0), col(1), col(2), seg_row, seg_col],
        out_specs=[col(0), stats],
        out_shape=[
            jax.ShapeDtypeStruct((length, pairs * 2 * HD), BF16),
            jax.ShapeDtypeStruct((pairs, 2, length), F32),
        ],
        cost_estimate=pl.CostEstimate(
            flops=8 * length * length * HD * pairs, bytes_accessed=4 * length * pairs * 256, transcendentals=0
        ),
    )(qkv, qkv, qkv, segments, jnp.broadcast_to(segments.reshape(length, 1), (length, 128)))


def attend_back_kernel(
    tile, q_ref, k_ref, v_ref, d_ref, o_ref, l_ref, sr_ref, sc_ref, dq_ref, dk_ref, dv_ref
):
    length, width = q_ref.shape
    scale = 1.0 / math.sqrt(HD)
    dk_ref[...] = jnp.zeros_like(dk_ref)
    dv_ref[...] = jnp.zeros_like(dv_ref)

    def step(t, _):
        rows = pl.ds(pl.multiple_of(t * tile, tile), tile)
        same = sc_ref[:, 0:1] == sr_ref[:, rows]
        for h in range(width // HD):
            cols = slice(h * HD, h * HD + HD)
            keys, q_rows, d_rows = k_ref[:, cols], q_ref[rows, cols], d_ref[rows, cols]
            delta = jnp.sum(
                (d_rows.astype(F32) * o_ref[rows, cols].astype(F32)).T, axis=0, keepdims=True
            )
            scores = dg(keys, q_rows, 1, 1) * scale
            prob = jnp.where(same, jnp.exp(scores - l_ref[0, h : h + 1, rows]), 0.0)
            d_prob = dg(v_ref[:, cols], d_rows, 1, 1)
            d_score = (prob * (d_prob - delta) * scale).astype(BF16)
            dv_ref[:, cols] += dg(prob.astype(BF16), d_rows, 1, 0)
            dk_ref[:, cols] += dg(d_score, q_rows, 1, 0)
            dq_ref[rows, cols] = dg(d_score, keys, 0, 0)
        return 0

    lax.fori_loop(0, length // tile, step, 0)


def attend_back(qkv, d_mixed, mixed, stats_in, segments):
    length = qkv.shape[0]
    pairs = qkv.shape[1] // 3 // (2 * HD)
    col, stats, seg_row, seg_col = attend_specs(length, pairs)
    return pl.pallas_call(
        functools.partial(attend_back_kernel, min(512, length)),
        name="attend_back",
        grid=(pairs,),
        in_specs=[col(0), col(1), col(2), col(0), col(0), stats, seg_row, seg_col],
        out_specs=[col(0)] * 3,
        out_shape=[jax.ShapeDtypeStruct((length, pairs * 2 * HD), F32)] * 3,
        cost_estimate=pl.CostEstimate(
            flops=20 * length * length * HD * pairs, bytes_accessed=8 * length * pairs * 256, transcendentals=0
        ),
    )(qkv, qkv, qkv, d_mixed, mixed, stats_in, segments, jnp.broadcast_to(segments.reshape(length, 1), (length, 128)))


def time_features(step_ids, model_width):
    half_width = model_width // 2
    frequency = jnp.exp(
        jnp.arange(half_width, dtype=F32) * (-math.log(10000.0) / half_width)
    )
    angles = step_ids.astype(F32)[:, None] * frequency[None, :]
    return jnp.concatenate([jnp.sin(angles), jnp.cos(angles)], axis=1)


def normalize(array_in):
    row_mean = jnp.mean(array_in, axis=-1, keepdims=True)
    centered = array_in - row_mean
    variance = jnp.mean(centered * centered, axis=-1, keepdims=True)
    inv_std = lax.rsqrt(variance + eps)
    return (centered * inv_std, inv_std)


def norm_back(grad_rows, unit_rows, inv_std, gain_row):
    d_unit = grad_rows * gain_row
    return inv_std * (
        d_unit
        - jnp.mean(d_unit, axis=-1, keepdims=True)
        - unit_rows * jnp.mean(d_unit * unit_rows, axis=-1, keepdims=True)
    )


def exact_gelu(array_in):
    return jax.nn.gelu(array_in, approximate=False)


def ein(spec, left, right):
    return jnp.einsum(spec, left, right, preferred_element_type=F32)


def on_device(
    hidden_in,
    segments,
    timesteps,
    time_weight,
    qkv_weight,
    out_weight,
    in_weight,
    down_weight,
    biases,
    gains,
    ffn_bias,
    out_grad,
    *,
    dp,
    mp,
):
    own_rows, width = hidden_in.shape
    length = segments.shape[1]
    rows = time_weight.shape[0]
    cols = qkv_weight.shape[2]
    hidden = in_weight.shape[1]
    dp_index, mp_index = lax.axis_index("dp"), lax.axis_index("mp")
    fast = (dp, mp) == (16, 2)

    bias_count = biases.shape[0] + gains.shape[0] + ffn_bias.shape[0] // rows
    v_shard = jnp.concatenate(
        [
            qkv_weight[0],
            qkv_weight[1],
            qkv_weight[2],
            time_weight,
            biases.T,
            gains.T,
            ffn_bias.reshape(rows, -1),
            jnp.broadcast_to(jnp.stack([timesteps // 64, timesteps % 64], axis=1), (rows, 2)).astype(BF16),
            jnp.zeros((rows, 126 - bias_count), BF16),
        ],
        axis=1,
    )
    shards = (v_shard, out_weight.T, in_weight, down_weight.T, hidden_in)
    if fast:
        v_all, o_all, i_all, d_all, h_all = gather_weights(*shards)
    else:
        v_all = lax.all_gather(shards[0], "dp", axis=0)
        o_all, i_all, d_all = (
            lax.all_gather(lax.all_gather(a, "dp", axis=0), "mp", axis=0) for a in shards[1:4]
        )
        h_all = lax.all_gather(hidden_in, "mp", axis=0)
    v_all = v_all.reshape(width, -1)
    o_all, i_all, d_all = (a.reshape(mp, width, -1) for a in (o_all, i_all, d_all))
    h_all = h_all.reshape(length, width)

    qkv_w = v_all[:, : 3 * cols]
    time_w = v_all[:, 3 * cols : 3 * cols + width]
    params = v_all[:, 3 * cols + width :].astype(F32)
    bias_all = params[:, :7].T
    gain_all = params[:, 7:9].T
    ffn_b = params[:, 9 : 9 + ffn_bias.shape[0] // rows].reshape(mp, hidden)

    feature = time_features(timesteps, width).astype(BF16)
    time_row = jnp.dot(feature, time_w, preferred_element_type=F32) + bias_all[0]
    embedded = hidden_in.astype(F32) + time_row
    embed_low = (h_all.astype(F32) + time_row).astype(BF16)
    column = mp_index * cols
    bias_qkv = jnp.concatenate(
        [
            lax.dynamic_slice_in_dim(bias_all[1], column, cols),
            jnp.zeros((cols,), F32),
            lax.dynamic_slice_in_dim(bias_all[2], column, cols),
        ]
    )
    qkv = (jnp.dot(embed_low, qkv_w, preferred_element_type=F32) + bias_qkv).astype(BF16)
    mixed_heads, stats = attend(qkv, segments)

    def heads_to_rows(array_in):
        cut = array_in.reshape(mp, own_rows, cols)
        return trade(cut)

    def rows_to_heads(array_in):
        return trade(array_in).reshape(length, cols)

    def trade(cut):
        if mp == 2:
            far = lax.ppermute(
                lax.dynamic_index_in_dim(cut, 1 - mp_index, 0, False), "mp", [(0, 1), (1, 0)]
            )
            own = jnp.arange(2)[:, None, None] == mp_index
            return jnp.where(own, cut, far[None])
        return lax.all_to_all(cut, "mp", 0, 0, tiled=True)

    mixed = heads_to_rows(mixed_heads)
    attn_total = ein("yrk,ynk->rn", mixed, o_all)
    unit_one, inv_one = normalize(embedded + attn_total + bias_all[3])
    middle = unit_one * gain_all[0] + bias_all[4]
    middle_low = middle.astype(BF16)
    pre_act = ein("rd,ydf->yrf", middle_low, i_all) + ffn_b[:, None, :]
    hidden_act = exact_gelu(pre_act).astype(BF16)
    ffn_total = ein("yrf,ynf->rn", hidden_act, d_all)
    unit_two, inv_two = normalize(middle + ffn_total + bias_all[5])
    layer_out = (unit_two * gain_all[1] + bias_all[6]).astype(BF16)

    grad_out = out_grad.astype(F32)
    gain_two_part = jnp.sum(grad_out * unit_two, axis=0)
    shift_two_part = jnp.sum(grad_out, axis=0)
    d_pre_two = norm_back(grad_out, unit_two, inv_two, gain_all[1])
    bias_five_part = jnp.sum(d_pre_two, axis=0)
    d_ffn = d_pre_two.astype(BF16)
    down_grad = ein("rn,yrf->ynf", d_ffn, hidden_act).astype(BF16)
    d_act = ein("rn,ynf->yrf", d_ffn, d_all)
    d_pre_act = jax.vjp(exact_gelu, pre_act)[1](d_act)[0]
    ffn_bias_part = jnp.sum(d_pre_act, axis=1).reshape(-1, width)
    d_pre_low = d_pre_act.astype(BF16)
    in_grad = ein("rd,yrf->ydf", middle_low, d_pre_low).astype(BF16)
    d_middle = d_pre_two + ein("yrf,ydf->rd", d_pre_low, i_all)
    gain_one_part = jnp.sum(d_middle * unit_one, axis=0)
    shift_one_part = jnp.sum(d_middle, axis=0)
    d_pre_one = norm_back(d_middle, unit_one, inv_one, gain_all[0])
    bias_three_part = jnp.sum(d_pre_one, axis=0)
    d_attn = d_pre_one.astype(BF16)
    out_grad_t = ein("rn,yrk->ynk", d_attn, mixed).astype(BF16)
    d_mixed = rows_to_heads(ein("rn,ynk->yrk", d_attn, o_all).astype(BF16))
    d_q, d_k, d_v = attend_back(qkv, d_mixed, mixed_heads, stats, segments)
    d_qkv = jnp.concatenate([d_q, d_k, d_v], axis=1).astype(BF16)
    v_grad = dg(embed_low, d_qkv, 0, 0).astype(BF16)
    d_embed = dg(d_qkv, qkv_w, 1, 1)
    time_part = bias_three_part + jnp.sum(d_embed, axis=0)
    d_embed = d_embed.astype(BF16).reshape(mp, own_rows, width)

    zero_row = jnp.zeros((width,), F32)
    seq_rows = jnp.where(jnp.arange(dp)[:, None] == dp_index, time_part[None, :], 0.0)
    small = jnp.concatenate(
        [
            seq_rows,
            jnp.stack(
                [
                    lax.dynamic_update_slice_in_dim(zero_row, jnp.sum(d_q, axis=0), column, 0),
                    lax.dynamic_update_slice_in_dim(zero_row, jnp.sum(d_v, axis=0), column, 0),
                    bias_three_part,
                    shift_one_part,
                    bias_five_part,
                    shift_two_part,
                    gain_one_part,
                    gain_two_part,
                ]
            ),
            ffn_bias_part,
        ],
        axis=0,
    )
    small = jnp.pad(small, ((0, -small.shape[0] % 8), (0, 0)))

    if fast:
        shape = (2, 4, 2, 2, rows, -1)
        v_sum, o_sum, i_sum, d_sum, d_far, small = reduce_grads(
            v_grad.reshape(shape[1:]),
            out_grad_t.reshape(shape),
            in_grad.reshape(shape),
            down_grad.reshape(shape),
            d_embed,
            small,
        )
        d_own = lax.dynamic_index_in_dim(d_embed, mp_index, 0, False).astype(F32) + d_far.astype(F32)
    else:
        v_sum = lax.psum_scatter(v_grad, "dp", scatter_dimension=0, tiled=True).astype(F32)

        def both(a):
            a = lax.psum_scatter(a, "mp", scatter_dimension=0)
            return lax.psum_scatter(a, "dp", scatter_dimension=0, tiled=True).astype(F32)

        o_sum, i_sum, d_sum = both(out_grad_t), both(in_grad), both(down_grad)
        d_own = lax.psum_scatter(d_embed, "mp", scatter_dimension=0).astype(F32)
        small = lax.psum(small, ("dp", "mp"))

    input_grad = d_pre_one + d_own
    d_time = small[:dp]
    start = dp_index * rows
    step_parts = params[::rows, bias_count : bias_count + 2]
    step_ids = 64.0 * step_parts[:, 0] + step_parts[:, 1]
    features = time_features(step_ids, width).astype(BF16).astype(F32)
    features = lax.dynamic_slice_in_dim(features, start, rows, axis=1)
    time_grad = lax.dot_general(
        features, d_time, (((0,), (0,)), ((), ())), precision=lax.Precision.HIGHEST
    )
    tail = small[dp:]
    bias_rows = jnp.concatenate([jnp.sum(d_time, axis=0)[None], tail[:6]], axis=0)
    bias_grad = lax.dynamic_slice_in_dim(bias_rows, start, rows, axis=1)
    gain_grad = lax.dynamic_slice_in_dim(tail[6:8], start, rows, axis=1)
    ffn_rows = ffn_bias.shape[0]
    ffn_all = tail[8:].reshape(-1)
    ffn_bias_grad = lax.dynamic_slice_in_dim(ffn_all, dp_index * ffn_rows, ffn_rows)
    qkv_grad = v_sum.reshape(rows, 3, cols).transpose(1, 0, 2)
    return (
        layer_out,
        input_grad,
        time_grad,
        qkv_grad,
        o_sum.T,
        i_sum,
        d_sum.T,
        bias_grad,
        gain_grad,
        ffn_bias_grad,
    )


def solution(mesh):
    dp, mp = mesh.shape["dp"], mesh.shape["mp"]
    placed = (
        P(("dp", "mp"), None),
        P("dp", None),
        P("dp"),
        P("dp", None),
        P(None, "dp", "mp"),
        P("mp", "dp"),
        P("dp", "mp"),
        P("mp", "dp"),
        P(None, "dp"),
        P(None, "dp"),
        P("dp"),
        P(("dp", "mp"), None),
    )
    return jax.shard_map(
        functools.partial(on_device, dp=dp, mp=mp),
        mesh=mesh,
        in_specs=placed,
        out_specs=(
            P(("dp", "mp"), None),
            P(("dp", "mp"), None),
            P("dp", None),
            P(None, "dp", "mp"),
            P("mp", "dp"),
            P("dp", "mp"),
            P("mp", "dp"),
            P(None, "dp"),
            P(None, "dp"),
            P("dp"),
        ),
        check_vma=False,
    )
```

time: 1160 us -> 537 us (0.46)
  waiting for transfers between devices: 708 us -> 8.56 us
  Pallas kernels: 0 us -> 353 us
  matrix products: 253 us -> 103 us
  blocking collectives: 80 us -> 0 us
  other arithmetic: 50 us -> 19.9 us
  between operations: 16.4 us -> 2.3 us
    reduce_scatter x9 -> x0, waiting for transfers between devices: 395 us -> none  [the longest x1 73.6 us: on_device(): lax.psum_scatter(in_grad_local.astype(jnp.bfloat16), 'dp', scatter_dimens...]
    pallas_call x0 -> x4, Pallas kernels: none -> 353 us  [the longest x1 156 us: gather_weights(): pl.pallas_call(gather_kernel, name='gather_weights', out_shape=[whole(v,...]
    all_gather x9 -> x0, waiting for transfers between devices: 254 us -> none  [the longest x1 39.3 us: on_device(): lax.all_gather(qkv_weight, 'dp', axis=1, tiled=True)]
    dot_general x30 -> x14, matrix products: 253 us -> 103 us  [the longest x9 80 us: ein(): return jnp.einsum(spec, left, right, preferred_element_type=F32)]
    unnamed x22 -> x0, waiting for transfers between devices: 59.5 us -> none
    all_gather x3 -> x0, blocking collectives: 48.1 us -> none  [the longest x1 16.3 us: on_device(): lax.all_gather(biases, 'dp', axis=1, tiled=True)]
    unnamed x1 -> x0, blocking collectives: 23.6 us -> none
    convert_element_type x15 -> x3, other arithmetic: 19.7 us -> 0.82 us  [the longest x1 0.7 us: on_device(): embed_low = (h_all.astype(F32) + time_row).astype(BF16)]
  transfers between devices with their start and end apart: 20 -> 2, of which waited for: 17 -> 1; matrix products, arithmetic and copies ran while one was open for 25% -> 4% of each run, Pallas kernels for 0% -> 0%
where the time goes in v1:
time: 537 us; the launch traced here: 527 us
  Pallas kernels  353 us (66%)
  matrix products  103 us (19%)
  local copies, waits for them, and re-layouts  38.1 us (7%)
  other arithmetic  19.9 us (4%)
  waiting for transfers between devices  8.56 us (2%)
    pallas_call x1, Pallas kernels, gather_weights(): pl.pallas_call(gather_kernel, name='gather_weights', out_shape=[whole(v,...  156 us
    pallas_call x1, Pallas kernels, reduce_grads(): pl.pallas_call(reduce_kernel, name='reduce_grads', out_shape=out + [jax.S...  146 us
    dot_general x9, matrix products, ein(): return jnp.einsum(spec, left, right, preferred_element_type=F32)  80 us
    pallas_call x1, Pallas kernels, attend_back(): pl.pallas_call(functools.partial(attend_back_kernel, min(512, length)), n...  28.6 us
    pallas_call x1, Pallas kernels, attend(): pl.pallas_call(functools.partial(attend_kernel, min(512, length)), name='...  21.2 us
    unnamed x85, local copies, waits for them, and re-layouts  20.5 us
    dot_general x2, matrix products, dg(): lax.dot_general(left, right, (((left_dim,), (right_dim,)), ((), ())), pre...  12.5 us
  transfers between devices with their start and end apart: 2, of which 1 were waited for; matrix products, arithmetic and copies ran while one was open for 4% of the time, Pallas kernels for 0%

profile of v1, /device:TPU:20, one launch (start us, length us, event | category | flops | bytes accessed | tf_op | source)
XLA Modules:
  0.0 527.2 jit_solution(16714369734254153520)
XLA Ops:
  9.7 156.5 %gather_weights.1 = (bf16[4,2,2,64,2688]{4,3,2,1,0:T(8,128)(2,1)S(1)}, bf16[2,4,2,2,64,512]{5,4,3,2,1,0:T(8,128)(2,1)S(1)}, bf16[2,4,2,2,64,2048]{5,4,3,2,1,0:T(...) custom-call(bf16[64,2688]{1,0:T(8,128)(2,1)S(1)} %concatenate.28.v_ref, ...), custom_call_target="tpu_custom_call" | custom-call | tf_op jit(solution)/shard_map/gather_weights/pallas_call | solution.py:189
  166.3 3.2 copy-done.6
  169.5 3.2 copy-done.7
  172.7 1.3 copy-done.8
  174.0 2.4 copy-done.2
  176.7 2.1 fusion.43
  179.7 7.4 %add_convert_fusion.q_ref.k_ref.v_ref = bf16[1024,1536]{1,0:T(8,128)(2,1)} fusion(bf16[1024,1024]{1,0:T(8,128)(2,1)S(1)} %fusion.21, f32[1536]{0:T(1024)S(1)} %pad_maximum_fusion.3, bf16[1024,2688]{1,0:T(8,128)(2,1)} %bitcast.203), kind=kOutput, calls=%fused_computation.30 | convolution fusion | flops 3224371200 | bytes 8394752 | tf_op jit(solution)/shard_map/dot_general | solution.py:569
  188.0 21.2 %attend.1 = (bf16[1024,512]{1,0:T(8,128)(2,1)}, f32[4,2,1024]{2,1,0:T(2,128)}) custom-call(bf16[1024,1536]{1,0:T(8,128)(2,1)} %add_convert_fusion.q_ref.k_ref.v_ref, bf16[1024,1536]{1,0:T(8,128)(2,1)} %add_convert_fusion.q_ref.k_ref.v_ref, bf16[1024,1536]{1,0:T(8,128)(2,1)} %add_convert_fusion.q_ref.k_ref.v_ref, s32[1,1024]{1,0:T(1,128)} %sr_ref.3, ...), custom_call_target="tpu_custom_call" | custom-call | flops 2147483648 | bytes 4194304 | tf_op jit(solution)/shard_map/attend/pallas_call | solution.py:401
  209.2 1.9 dynamic-slice_bitcast_fusion.1
  211.1 1.4 collective-permute-start
  214.4 1.4 add.174
  217.1 8.6 %collective-permute-done = bf16[512,512]{1,0:T(8,128)(2,1)} collective-permute-done((bf16[512,512]{1,0:T(8,128)(2,1)}, bf16[512,512]{1,0:T(8,128)(2,1)}, u32[]{:S(2)}, u32[]{:S(2)}) %collective-permute-start) | collective-permute-done | bytes 524320 | tf_op jit(solution)/shard_map/ppermute | solution.py:581
  225.7 2.9 fusion.78
  229.0 28.5 %fusion.8 = (bf16[2,512,2048]{2,1,0:T(8,128)(2,1)S(1)}, f32[2,512,2048]{2,1,0:T(8,128)}, f32[2,2048,512]{1,2,0:T(8,128)}) fusion(f32[2,2048]{1,0:T(2,128)S(1)} %add.174, bf16[2,1024,2048]{2,1,0:T(8,128)(2,1)} %bitcast.207, f32[512,1024]{1,0:T(8,128)S(1)} %get-tuple-element.87, f32[1024]{0:T(1024)S(1)} %bitcast.255, f32[1024]{0:T(1024)S(1)} %bitcast.241, ...), kind=kOutput, calls=%fused_computation.16 | convolution fusion | flops 4436000768 | bytes 31485952 | tf_op jit(solution)/shard_map/rd,ydf->yrf/dot_general | solution.py:494
  257.5 4.8 fusion.79
  263.7 2.6 fusion.69
  266.3 13.2 %fusion.80 = (f32[2,2048]{1,0:T(2,128)S(1)}, bf16[2,512,2048]{2,1,0:T(8,128)(2,1)}) fusion(f32[2,512,2048]{2,1,0:T(8,128)} %get-tuple-element.65, bf16[2,1024,2048]{2,1,0:T(8,128)(2,1)S(1)} %bitcast.214, f32[512,1024]{1,0:T(8,128)} %get-tuple-element.61, f32[2,2048,512]{1,2,0:T(8,128)} %get-tuple-element.88, f32[2,2048]{1,0:T(2,128)S(1)} %add.174), kind=kOutput, calls=%fused_computation.146 | convolution fusion | flops 4329041920 | bytes 31490048 | tf_op jit(solution)/shard_map/rn,ynf->yrf/dot_general | solution.py:494
  279.6 9.1 %multiply_reduce_fusion = (f32[1024]{0:T(1024)S(1)}, f32[512]{0:T(512)S(1)}, f32[512]{0:T(512)S(1)}, f32[1024]{0:T(1024)S(1)}, f32[512,1024]{1,0:T(8,128)}) fusion(f32[512,1024]{1,0:T(8,128)S(1)} %copy-done.14, f32[512]{0:T(512)S(1)} %add_rsqrt_fusion.1, f32[512]{0:T(512)S(1)} %broadcast_multiply_fusion.5, f32[1024]{0:T(1024)S(1)} %bitcast.243, ...), kind=kOutput, calls=%fused_computation.59 | convolution fusion | flops 4300207104 | bytes 18894848 | tf_op jit(solution)/shard_map/yrf,ydf->rd/dot_general | solution.py:494
  288.7 7.2 %convolution_convert_fusion.1 = bf16[2,2048,1024]{1,2,0:T(8,128)(2,1)} fusion(bf16[2,512,2048]{2,1,0:T(8,128)(2,1)S(1)} %copy-done.33, f32[512,1024]{1,0:T(8,128)S(1)} %copy-done.14, f32[1024]{0:T(1024)S(1)} %bitcast.257, f32[1024]{0:T(1024)S(1)} %bitcast.244, f32[512]{0:T(512)S(1)} %add_rsqrt_fusion.1, f32[512]{0:T(512)S(1)} %broadcast_multiply_fusion.5), kind=kOutput, calls=%fused_computation.32 | convolution fusion | flops 4301783040 | bytes 14692352 | tf_op jit(solution)/shard_map/rd,yrf->ydf/dot_general | solution.py:494
  295.9 3.0 fusion.71
  301.0 1.4 collective-permute-start.1
  302.4 2.4 convert_bitcast_fusion
  304.8 2.8 copy.35
  307.7 10.7 %convolution_convert_fusion = bf16[2,2048,1024]{1,2,0:T(8,128)(2,1)} fusion(bf16[2,512,2048]{2,1,0:T(8,128)(2,1)} %copy-done.32, f32[512,1024]{1,0:T(8,128)} %get-tuple-element.61), kind=kOutput, calls=%fused_computation.31 | convolution fusion | flops 4299685888 | bytes 14680064 | tf_op jit(solution)/shard_map/rn,yrf->ynf/dot_general | solution.py:494
  318.3 2.2 bitcast_select_fusion
  320.5 28.6 %attend_back.1 = (f32[1024,512]{1,0:T(8,128)}, f32[1024,512]{1,0:T(8,128)}, f32[1024,512]{1,0:T(8,128)}) custom-call(bf16[1024,1536]{1,0:T(8,128)(2,1)} %add_convert_fusion.q_ref.k_ref.v_ref, bf16[1024,1536]{1,0:T(8,128)(2,1)} %add_convert_fusion.q_ref.k_ref.v_ref, bf16[1024,1536]{1,0:T(8,128)(2,1)} %add_convert_fusion.q_ref.k_ref.v_ref, ...), custom_call_target="tpu_custom_call" | custom-call | flops 5368709120 | bytes 8388608 | tf_op jit(solution)/shard_map/attend_back/pallas_call | solution.py:450
  349.1 2.7 fusion.75
  352.9 6.7 %fusion.73 = (f32[1024]{0:T(1024)S(1)}, bf16[1024,1024]{1,0:T(8,128)(2,1)}) fusion(bf16[1024,2688]{1,0:T(8,128)(2,1)} %bitcast.204, bf16[1024,512]{1,0:T(8,128)(2,1)S(1)} %get-tuple-element.70, bf16[1024,512]{1,0:T(8,128)(2,1)S(1)} %convert.36, bf16[1024,512]{1,0:T(8,128)(2,1)S(1)} %get-tuple-element.72), kind=kOutput, calls=%fused_computation.139 | convolution fusion | flops 3232758784 | bytes 8392704 | tf_op jit(solution)/shard_map/dot_general | solution.py:20
  359.6 5.8 %convolution_convert_fusion.2 = bf16[1024,1536]{1,0:T(8,128)(2,1)} fusion(bf16[1024,1024]{1,0:T(8,128)(2,1)S(1)} %copy-done.17, bf16[1024,512]{1,0:T(8,128)(2,1)S(1)} %get-tuple-element.70, bf16[1024,512]{1,0:T(8,128)(2,1)S(1)} %convert.36, bf16[1024,512]{1,0:T(8,128)(2,1)S(1)} %get-tuple-element.72), kind=kOutput, calls=%fused_computation.35 | convolution fusion | flops 3232235520 | bytes 8388608 | tf_op jit(solution)/shard_map/dot_general | solution.py:20
  366.3 146.3 %reduce_grads.1 = (f32[64,1536]{1,0:T(8,128)}, f32[64,512]{1,0:T(8,128)}, f32[64,2048]{1,0:T(8,128)}, f32[64,2048]{1,0:T(8,128)}, bf16[512,1024]{1,0:T(8,128)(2,1)}, /*index=5*/f32[32,1024]{1,0:T(8,128)}) custom-call(bf16[4,2,2,64,1536]{4,3,2,1,0:T(8,128)(2,1)} %bitcast.222, bf16[2,4,2,2,64,512]{5,4,3,2,1,0:T(8,128)(2,1)} %bitcast.219, ...), custom_call_target="tpu_custom_call" | custom-call | tf_op jit(solution)/shard_map/reduce_grads/pallas_call | solution.py:352
  515.8 1.3 reshape.180
  518.0 3.4 fusion.34
  (143 shorter events, 28.9 us)
Async XLA Ops:
  166.2 3.2 copy-start.6
  169.5 3.2 copy-start.7
  176.7 10.3 %copy-start.20 = (f32[1024,128]{0,1:T(8,128)}, f32[1024,128]{0,1:T(8,128)S(1)}, u32[]{:S(2)}) copy-start(f32[1024,128]{0,1:T(8,128)S(1)} %convert_element_type.98) | copy-start | bytes 1572868
  179.6 7.4 %copy-start.16 = (bf16[1024,1024]{1,0:T(8,128)(2,1)}, bf16[1024,1024]{1,0:T(8,128)(2,1)S(1)}, u32[]{:S(2)}) copy-start(bf16[1024,1024]{1,0:T(8,128)(2,1)S(1)} %fusion.21) | copy-start | bytes 6291460
  179.6 7.4 %copy-start.28 = (s32[1,1024]{1,0:T(1,128)S(1)}, s32[1,1024]{1,0:T(1,128)}, u32[]{:S(2)}) copy-start(s32[1,1024]{1,0:T(1,128)} %sr_ref.3) | copy-start | bytes 12292
  188.0 37.7 %copy-start.1 = (bf16[512,1024]{1,0:T(8,128)(2,1)S(1)}, bf16[512,1024]{1,0:T(8,128)(2,1)}, u32[]{:S(2)}) copy-start(bf16[512,1024]{1,0:T(8,128)(2,1)} %h_ref.1) | copy-start | bytes 3145732
  188.0 37.7 %copy-start.9 = (bf16[2,4,2,2,64,512]{5,4,3,2,1,0:T(8,128)(2,1)S(1)}, bf16[2,4,2,2,64,512]{5,4,3,2,1,0:T(8,128)(2,1)}, u32[]{:S(2)}) copy-start(bf16[2,4,2,2,64,512]{5,4,3,2,1,0:T(8,128)(2,1)} %copy-done.8) | copy-start | bytes 6291460
  211.1 14.6 %collective-permute-start = (bf16[512,512]{1,0:T(8,128)(2,1)}, bf16[512,512]{1,0:T(8,128)(2,1)}, u32[]{:S(2)}, u32[]{:S(2)}) collective-permute-start(bf16[512,512]{1,0:T(8,128)(2,1)} %dynamic-slice_bitcast_fusion.1), channel_id=1, source_target_pairs={{0,1},{1,0},{2,3},{3,2},{4,5},{5,4},{6,7},{7,6},{8,9},{9,8},{10,11... | collective-permute-start | bytes 1572872 | tf_op jit(solution)/shard_map/ppermute | solution.py:581
  212.4 16.2 %copy-start.30 = (pred[2]{0:T(512)(128)(4,1)}, pred[2]{0:T(512)(128)(4,1)S(1)}, u32[]{:S(2)}) copy-start(pred[2]{0:T(512)(128)(4,1)S(1)} %iota_compare_fusion.1) | copy-start | bytes 10
  225.7 31.8 %slice-start.2 = ((s8[8388608]{0:T(1024)(128)(4,1)}), s8[4194304]{0:T(1024)(128)(4,1)S(1)}, s32[]{:S(2)}) async-start(s8[8388608]{0:T(1024)(128)(4,1)} %bitcast.211), calls=%async_computation.2 | async-start | bytes 8388608
  228.6 28.9 %copy-start.13 = (f32[512,1024]{1,0:T(8,128)}, f32[512,1024]{1,0:T(8,128)S(1)}, u32[]{:S(2)}) copy-start(f32[512,1024]{1,0:T(8,128)S(1)} %get-tuple-element.87) | copy-start | bytes 6291460
  229.0 28.5 %slice-start.3 = ((s8[8388608]{0:T(1024)(128)(4,1)}), s8[4194304]{0:T(1024)(128)(4,1)S(1)}, s32[]{:S(2)}) async-start(s8[8388608]{0:T(1024)(128)(4,1)} %bitcast.211), calls=%async_computation.3 | async-start | bytes 8388608
  257.5 4.9 copy-start.32
  257.5 5.2 copy-start.15
  263.7 15.8 %slice-start = ((s8[8388608]{0:T(1024)(128)(4,1)}), s8[4194304]{0:T(1024)(128)(4,1)S(1)}, s32[]{:S(2)}) async-start(s8[8388608]{0:T(1024)(128)(4,1)} %bitcast.208), calls=%async_computation | async-start | bytes 8388608
  266.3 13.2 %slice-start.1 = ((s8[8388608]{0:T(1024)(128)(4,1)}), s8[4194304]{0:T(1024)(128)(4,1)S(1)}, s32[]{:S(2)}) async-start(s8[8388608]{0:T(1024)(128)(4,1)} %bitcast.208), calls=%async_computation.1 | async-start | bytes 8388608
  266.3 13.2 %copy-start.14 = (f32[512,1024]{1,0:T(8,128)S(1)}, f32[512,1024]{1,0:T(8,128)}, u32[]{:S(2)}) copy-start(f32[512,1024]{1,0:T(8,128)} %copy-done.13) | copy-start | bytes 6291460
  279.6 9.1 %copy-start.33 = (bf16[2,512,2048]{2,1,0:T(8,128)(2,1)S(1)}, bf16[2,512,2048]{2,1,0:T(8,128)(2,1)}, u32[]{:S(2)}) copy-start(bf16[2,512,2048]{2,1,0:T(8,128)(2,1)} %get-tuple-element.94) | copy-start | bytes 12582916
  298.9 3.5 copy-start.11
  298.9 3.5 copy-start.24
  298.9 3.5 copy-start.31
  301.0 17.3 %collective-permute-start.1 = (bf16[512,512]{1,0:T(8,128)(2,1)}, bf16[512,512]{1,0:T(8,128)(2,1)}, u32[]{:S(2)}, u32[]{:S(2)}) collective-permute-start(bf16[512,512]{1,0:T(8,128)(2,1)} %dynamic-slice_bitcast_fusion), channel_id=1, source_target_pairs={{0,1},{1,0},{2,3},{3,2},{4,5},{5,4},{6,7},{7,6},{8,9},{9,8},{10,11... | collective-permute-start | bytes 1572872 | tf_op jit(solution)/shard_map/ppermute | solution.py:581
  349.1 3.5 copy-start.19
  352.9 6.7 %copy-start.17 = (bf16[1024,1024]{1,0:T(8,128)(2,1)S(1)}, bf16[1024,1024]{1,0:T(8,128)(2,1)}, u32[]{:S(2)}) copy-start(bf16[1024,1024]{1,0:T(8,128)(2,1)} %copy-done.16) | copy-start | bytes 6291460
  359.6 5.9 %copy-start.29 = (pred[16]{0:T(512)(128)(4,1)S(1)}, pred[16]{0:T(512)(128)(4,1)}, u32[]{:S(2)}) copy-start(pred[16]{0:T(512)(128)(4,1)} %iota_compare_fusion) | copy-start | bytes 52
  366.3 151.8 %copy-start.12 = (f32[512,1024]{1,0:T(8,128)S(1)}, f32[512,1024]{1,0:T(8,128)}, u32[]{:S(2)}) copy-start(f32[512,1024]{1,0:T(8,128)} %copy-done.11) | copy-start | bytes 6291460
  514.2 9.2 %copy-start.23 = (f32[32,1024]{1,0:T(8,128)S(1)}, f32[32,1024]{1,0:T(8,128)}, u32[]{:S(2)}) copy-start(f32[32,1024]{1,0:T(8,128)} %get-tuple-element.37) | copy-start | bytes 393220
  514.2 9.2 %copy-start.26 = (bf16[16,512]{1,0:T(8,128)(2,1)S(1)}, bf16[16,512]{1,0:T(8,128)(2,1)}, u32[]{:S(2)}) copy-start(bf16[16,512]{1,0:T(8,128)(2,1)} %get-tuple-element.84) | copy-start | bytes 49156
  514.2 9.2 %copy-start.27 = (bf16[16,512]{1,0:T(8,128)(2,1)S(1)}, bf16[16,512]{1,0:T(8,128)(2,1)}, u32[]{:S(2)}) copy-start(bf16[16,512]{1,0:T(8,128)(2,1)} %get-tuple-element.85) | copy-start | bytes 49156
  515.8 8.7 %copy-start.25 = (f32[64,512]{1,0:T(8,128)S(1)}, f32[64,512]{1,0:T(8,128)}, u32[]{:S(2)}) copy-start(f32[64,512]{1,0:T(8,128)} %get-tuple-element.39) | copy-start | bytes 393220
  517.2 8.0 %copy-start.22 = (f32[64,2048]{1,0:T(8,128)S(1)}, f32[64,2048]{1,0:T(8,128)}, u32[]{:S(2)}) copy-start(f32[64,2048]{1,0:T(8,128)} %get-tuple-element.116) | copy-start | bytes 1572868
  518.0 7.9 %copy-start.21 = (f32[64,2048]{1,0:T(8,128)S(1)}, f32[64,2048]{1,0:T(8,128)}, u32[]{:S(2)}) copy-start(f32[64,2048]{1,0:T(8,128)} %get-tuple-element.41) | copy-start | bytes 1572868
  (8 other events, 13.7 us)

commit v2 on v1

--- a/solution.py
+++ b/solution.py
@@ -22,38 +22,39 @@
     )
 
 
-def place():
-    i, y = lax.axis_index("dp"), lax.axis_index("mp")
-    return i // 4, (i // 2) % 2, i % 2, y
-
-
-def z_places(z):
-    return [(z // 2) * 2 + 1 - z % 2, (z + 2) % 4, 3 - z]
-
-
-def peers(z, x, c, y):
-    def at(z_, x_, c_, y_):
-        return ((z_ * 2 + x_) * 2 + c_, y_)
-
-    return {
-        "z": [at(p, x, c, y) for p in z_places(z)],
-        "x": at(z, 1 - x, c, y),
-        "y": at(z, x, c, 1 - y),
-        "c": at(z, x, 1 - c, y),
-    }
-
-
-def enter(near):
-    barrier = pltpu.get_barrier_semaphore()
-    everyone = near["z"] + [near["x"], near["y"], near["c"]]
-    for one in everyone:
-        pl.semaphore_signal(barrier, inc=1, device_id=one, device_id_type=MESH)
-    pl.semaphore_wait(barrier, len(everyone))
+class Place:
+    def __init__(self):
+        i, y = lax.axis_index("dp"), lax.axis_index("mp")
+        z, x, c = i // 4, (i // 2) % 2, i % 2
+        self.i, self.z, self.x, self.c, self.y = i, z, x, c, y
+        self.nx, self.nc, self.ny, self.zero = 1 - x, 1 - c, 1 - y, 0 * i
+        low, high = z % 2, z // 2
+        flipped = [(1 - 2 * bit) * v + bit for v, bit in ((low, 1), (high, 1))]
+        self.zs = [high * 2 + flipped[0], flipped[1] * 2 + low, flipped[1] * 2 + flipped[0]]
+        self.to_z = [((p * 2 + x) * 2 + c, y) for p in self.zs]
+        self.to_x = ((z * 2 + self.nx) * 2 + c, y)
+        self.to_y = (i, self.ny)
+        self.to_c = ((z * 2 + x) * 2 + self.nc, y)
+        self.dp = [
+            (pz * 2 + px) * 2 + pc
+            for pz in [z] + self.zs
+            for px in (x, self.nx)
+            for pc in (c, self.nc)
+        ][1:]
+
+    def enter(self, all_dp):
+        barrier = pltpu.get_barrier_semaphore()
+        near = [self.to_y]
+        near += [(p, self.y) for p in self.dp] if all_dp else self.to_z + [self.to_x, self.to_c]
+        for one in near:
+            pl.semaphore_signal(barrier, inc=1, device_id=one, device_id_type=MESH)
+        pl.semaphore_wait(barrier, len(near))
 
 
 class Wire:
-    def __init__(self, send_sems, recv_sems):
-        self.send_sems, self.recv_sems, self.used, self.open = send_sems, recv_sems, 0, []
+    def __init__(self, at, send_sems, recv_sems):
+        self.sems = [(send_sems.at[at.zero + k], recv_sems.at[at.zero + k]) for k in range(send_sems.shape[0])]
+        self.used, self.open = 0, []
 
     def send(self, src, dst, to):
         k = self.used
@@ -61,8 +62,8 @@
         copy = pltpu.make_async_remote_copy(
             src_ref=src,
             dst_ref=dst,
-            send_sem=self.send_sems.at[k],
-            recv_sem=self.recv_sems.at[k],
+            send_sem=self.sems[k][0],
+            recv_sem=self.sems[k][1],
             device_id=to,
             device_id_type=MESH,
         )
@@ -71,66 +72,26 @@
         return copy
 
     def close(self):
-        assert self.used == self.send_sems.shape[0] == self.recv_sems.shape[0]
+        assert self.used == len(self.sems), self.used
         for copy in self.open:
             copy.wait_send()
 
 
-def gather_dp(wire, near, here, shard, whole):
-    z, x, c, y = here
-    own = whole.at[z, x, c]
-    from_z = [wire.send(shard, own, to) for to in near["z"]]
-    late = [wire.send(shard, own, near["c"])]
-    yield
-    for k in from_z:
-        k.wait_recv()
-    ref = whole.at[:, x, c]
-    from_x = wire.send(ref, ref, near["x"])
-    for p in z_places(z):
-        ref = whole.at[p, x, c]
-        late.append(wire.send(ref, ref, near["c"]))
-    yield
-    from_x.wait_recv()
-    ref = whole.at[:, 1 - x, c]
-    late.append(wire.send(ref, ref, near["c"]))
-    yield
-    for k in late:
-        k.wait_recv()
-
-
-def gather_all(wire, near, here, shard, whole, lo, mid, hi):
-    z, x, c, y = here
-    a, b, ab = pl.ds(lo, mid - lo), pl.ds(mid, hi - mid), pl.ds(lo, hi - lo)
-    own = whole.at[y, z, x, c, :, ab]
-    from_z = [wire.send(shard.at[:, ab], own, to) for to in near["z"]]
-    late = [wire.send(shard.at[:, ab], own, near["c"])]
-    yield
-    for k in from_z:
-        k.wait_recv()
-    ref = whole.at[y, :, x, c, :, a]
-    from_x_a = wire.send(ref, ref, near["x"])
-    ref = whole.at[y, :, x, c, :, b]
-    from_y_b = wire.send(ref, ref, near["y"])
-    for p in z_places(z):
-        ref = whole.at[y, p, x, c, :, ab]
-        late.append(wire.send(ref, ref, near["c"]))
-    yield
-    from_x_a.wait_recv()
-    ref = whole.at[y, :, :, c, :, a]
-    from_y_a = wire.send(ref, ref, near["y"])
-    from_y_b.wait_recv()
-    ref = whole.at[:, :, x, c, :, b]
-    from_x_b = wire.send(ref, ref, near["x"])
-    for ref in (whole.at[y, :, 1 - x, c, :, a], whole.at[1 - y, :, x, c, :, b]):
-        late.append(wire.send(ref, ref, near["c"]))
-    yield
-    from_y_a.wait_recv()
-    from_x_b.wait_recv()
-    for ref in (whole.at[1 - y, :, :, c, :, a], whole.at[:, :, 1 - x, c, :, b]):
-        late.append(wire.send(ref, ref, near["c"]))
-    yield
-    for k in late:
-        k.wait_recv()
+class Local:
+    def __init__(self, sems):
+        self.sems, self.used, self.open = sems, 0, []
+
+    def copy(self, src, dst):
+        one = pltpu.make_async_copy(src, dst, self.sems.at[self.used])
+        self.used += 1
+        one.start()
+        self.open.append(one)
+        return one
+
+    def close(self):
+        assert self.used == self.sems.shape[0], self.used
+        for one in self.open:
+            one.wait()
 
 
 def parts_of(width, parts):
@@ -145,68 +106,324 @@
                 next(s, None)
 
 
-def gather_kernel(
-    v_ref, o_ref, i_ref, d_ref, h_ref, v_all, o_all, i_all, d_all, h_all, send_sems, recv_sems, local_sems
+def gather_dp(wire, at, shard, whole, lo, hi):
+    n = pl.ds(lo, hi - lo)
+    own = whole.at[at.z, at.x, at.c, :, n]
+    from_z = [wire.send(shard.at[:, n], own, to) for to in at.to_z]
+    late = [wire.send(shard.at[:, n], own, at.to_c)]
+    yield
+    for k in from_z:
+        k.wait_recv()
+    ref = whole.at[:, at.x, at.c, :, n]
+    from_x = wire.send(ref, ref, at.to_x)
+    for p in at.zs:
+        ref = whole.at[p, at.x, at.c, :, n]
+        late.append(wire.send(ref, ref, at.to_c))
+    yield
+    from_x.wait_recv()
+    ref = whole.at[:, at.nx, at.c, :, n]
+    late.append(wire.send(ref, ref, at.to_c))
+    yield
+    for k in late:
+        k.wait_recv()
+
+
+def gather_all(wire, at, shard, whole, lo, mid, hi):
+    a, b, ab = pl.ds(lo, mid - lo), pl.ds(mid, hi - mid), pl.ds(lo, hi - lo)
+    y, z, x, c = at.y, at.z, at.x, at.c
+    own = whole.at[y, z, x, c, :, ab]
+    from_z = [wire.send(shard.at[:, ab], own, to) for to in at.to_z]
+    late = [wire.send(shard.at[:, ab], own, at.to_c)]
+    yield
+    for k in from_z:
+        k.wait_recv()
+    ref = whole.at[y, :, x, c, :, a]
+    from_x_a = wire.send(ref, ref, at.to_x)
+    ref = whole.at[y, :, x, c, :, b]
+    from_y_b = wire.send(ref, ref, at.to_y)
+    for p in at.zs:
+        ref = whole.at[y, p, x, c, :, ab]
+        late.append(wire.send(ref, ref, at.to_c))
+    yield
+    from_x_a.wait_recv()
+    ref = whole.at[y, :, :, c, :, a]
+    from_y_a = wire.send(ref, ref, at.to_y)
+    from_y_b.wait_recv()
+    ref = whole.at[:, :, x, c, :, b]
+    from_x_b = wire.send(ref, ref, at.to_x)
+    for ref in (whole.at[y, :, at.nx, c, :, a], whole.at[at.ny, :, x, c, :, b]):
+        late.append(wire.send(ref, ref, at.to_c))
+    yield
+    from_y_a.wait_recv()
+    from_x_b.wait_recv()
+    for ref in (whole.at[at.ny, :, :, c, :, a], whole.at[:, :, at.nx, c, :, b]):
+        late.append(wire.send(ref, ref, at.to_c))
+    yield
+    for k in late:
+        k.wait_recv()
+
+
+def one_hot_rows(count, width, start):
+    down = lax.broadcasted_iota(jnp.int32, (count, width), 0)
+    across = lax.broadcasted_iota(jnp.int32, (count, width), 1)
+    return jnp.where(down == across + start, 1.0, 0.0).astype(BF16)
+
+
+def forward_kernel(
+    v_ref, t_ref, f_ref, b_ref, o_ref, i_ref, d_ref, h_ref, sr_ref, sc_ref,
+    v_out, o_out, i_out, d_all, few_out, par_out, time_out, embed_out, qkv_out, mine_out, far_out,
+    stats_out, unit_out, inv_out, mid_out, act_out, slope_out,
+    v_all, o_all, i_all, few, part, got, h_far, par, ffn_b, embed, qkv, mine, far, stats, unit, inv,
+    mid, act, slope, send_sems, recv_sems, local_sems, tile_sems,
 ):
-    here = place()
-    z, x, c, y = here
-    near = peers(*here)
-    enter(near)
-    wire = Wire(send_sems, recv_sems)
-    first = gather_dp(wire, near, here, v_ref, v_all)
-    next(first)
-    from_y = wire.send(h_ref, h_all.at[y], near["y"])
-    kept = (
-        (v_ref, v_all.at[z, x, c]),
-        (o_ref, o_all.at[y, z, x, c]),
-        (i_ref, i_all.at[y, z, x, c]),
-        (d_ref, d_all.at[y, z, x, c]),
-        (h_ref, h_all.at[y]),
-    )
-    own = [pltpu.make_async_copy(s, d, local_sems.at[k]) for k, (s, d) in enumerate(kept)]
-    for k in own:
-        k.start()
-    streams = [
-        gather_all(wire, near, here, shard, whole, *cut)
-        for shard, whole, parts in ((o_ref, o_all, 1), (i_ref, i_all, 2), (d_ref, d_all, 2))
-        for cut in parts_of(shard.shape[1], parts)
+    at = Place()
+    y, z, x, c = at.y, at.z, at.x, at.c
+    at.enter(True)
+    wire, local = Wire(at, send_sems, recv_sems), Local(local_sems)
+    width = h_ref.shape[1]
+    own_rows = h_ref.shape[0]
+    rows = v_ref.shape[0]
+    cols = o_ref.shape[1]
+    hidden = i_ref.shape[1]
+    length = 2 * own_rows
+
+    from_few = [wire.send(f_ref, few.at[at.i], (p, y)) for p in at.dp]
+    from_h = wire.send(h_ref, h_far, at.to_y)
+    v_mid = 7 * 128
+    v0 = gather_dp(wire, at, v_ref, v_all, 0, v_mid)
+    v1 = gather_dp(wire, at, v_ref, v_all, v_mid, v_ref.shape[1])
+    out_w = gather_all(wire, at, o_ref, o_all, *parts_of(cols, 1)[0])
+    in_w = [gather_all(wire, at, i_ref, i_all, *cut) for cut in parts_of(hidden, 2)]
+    down_w = [gather_all(wire, at, d_ref, d_all, *cut) for cut in parts_of(hidden, 2)]
+    next(v0)
+    kept = [
+        local.copy(v_ref, v_all.at[z, x, c]),
+        local.copy(o_ref, o_all.at[y, z, x, c]),
+        local.copy(i_ref, i_all.at[y, z, x, c]),
+        local.copy(d_ref, d_all.at[y, z, x, c]),
     ]
-    for s in streams:
-        next(s)
-    for k in own:
+    few[at.i] = f_ref[...]
+    for k in from_few:
+        k.wait_recv()
+    seqs = few.shape[0]
+    table = jnp.concatenate([few[s] for s in range(seqs)], axis=0)
+    pick = one_hot_rows(width, rows, at.i * rows)
+    feats = dg(table[:, :width].astype(BF16), pick, 1, 0).astype(BF16)
+    partial = dg(feats, t_ref[...], 1, 0) + dg(b_ref[...], pick, 1, 1)
+    for s in range(seqs):
+        part[s] = partial[s : s + 1]
+    ffn_b[...] = jnp.concatenate([few[s][:, width:] for s in range(seqs)], axis=1)
+    local.copy(few, few_out)
+    from_part = [wire.send(part.at[p], got.at[j], (p, y)) for j, p in enumerate(at.dp)]
+    next(v1)
+    next(out_w)
+    next(in_w[0])
+    for k in kept:
         k.wait()
-    stagger([first] + streams)
-    from_y.wait_recv()
+        local.open.remove(k)
+    next(v0)
+    next(v1)
+    next(in_w[1])
+    next(down_w[0])
+    next(down_w[1])
+    for k in from_part:
+        k.wait_recv()
+    total = part[at.i]
+    for j in range(seqs - 1):
+        total = total + got[j]
+    time_out[...] = total
+
+    from_h.wait_recv()
+    step = 128
+
+    def embed_rows(t, _):
+        r = pl.ds(pl.multiple_of(t * step, step), step)
+        embed[y, r] = (h_ref[r].astype(F32) + total).astype(BF16)
+        embed[at.ny, r] = (h_far[r].astype(F32) + total).astype(BF16)
+        return 0
+
+    lax.fori_loop(0, own_rows // step, embed_rows, 0)
+    local.copy(embed, embed_out)
+    next(v0)
+    next(out_w)
+    next(v1)
+    next(in_w[0])
+    next(v0, None)
+    next(v1, None)
+    local.copy(v_all, v_out)
+    par[...] = v_all[:, :, :, :, 3 * cols :].reshape(width, 128).astype(F32).T
+    local.copy(par, par_out)
+    heads = pl.ds(pl.multiple_of(y * cols, cols), cols)
+    bias_q, bias_v = par[1:2, heads], par[2:3, heads]
+
+    step_q = 256
+
+    def project(t, _):
+        half, r = t // (own_rows // step_q), pl.ds(pl.multiple_of((t % (own_rows // step_q)) * step_q, step_q), step_q)
+        whole_r = pl.ds(pl.multiple_of(t * step_q, step_q), step_q)
+        left = embed[half, r]
+        for j, bias in enumerate((bias_q, None, bias_v)):
+            n = slice(j * cols, (j + 1) * cols)
+            made = dg(left, v_all[:, :, :, :, n].reshape(width, cols), 1, 0)
+            qkv[whole_r, n] = (made if bias is None else made + bias).astype(BF16)
+        return 0
+
+    lax.fori_loop(0, length // step_q, project, 0)
+    local.copy(qkv, qkv_out)
+    next(out_w)
+    next(in_w[1])
+
+    pair, tile = 2 * HD, own_rows
+    from_far = []
+
+    def give(p):
+        n = pl.ds(p * pair, pair)
+        from_far.append(wire.send(mine.at[at.ny, :, n], far.at[:, n], at.to_y))
+
+    ticks = {
+        0: lambda: next(in_w[0]),
+        1: lambda: (give(0), next(out_w)),
+        2: lambda: next(down_w[0]),
+        3: lambda: (give(1), next(in_w[0])),
+        4: lambda: next(in_w[1]),
+        5: lambda: (give(2), next(down_w[1])),
+        6: lambda: next(down_w[0]),
+        7: lambda: (give(3), next(out_w, None), next(in_w[0], None)),
+    }
+
+    def attend_step(t, _):
+        p, half = t // 2, t % 2
+        r = pl.ds(pl.multiple_of(half * tile, tile), tile)
+        n = pl.multiple_of(p * pair, pair)
+        queries = qkv[r, pl.ds(n, pair)]
+        keys = qkv[:, pl.ds(cols + n, pair)]
+        values = qkv[:, pl.ds(2 * cols + n, pair)]
+        same = sc_ref[:, 0:1] == sr_ref[:, r]
+        made = []
+        for h in range(2):
+            k = slice(h * HD, h * HD + HD)
+            scores = dg(keys[:, k], queries[:, k], 1, 1) * (1.0 / math.sqrt(HD))
+            scores = jnp.where(same, scores, neg_big)
+            row_max = jnp.max(scores, axis=0, keepdims=True)
+            prob = jnp.exp(scores - row_max)
+            row_total = jnp.sum(prob, axis=0, keepdims=True)
+            made.append((dg(values[:, k], prob.astype(BF16), 0, 0) / row_total).T)
+            stats[p, h : h + 1, r] = row_max + jnp.log(row_total)
+        mine[half, :, pl.ds(n, pair)] = jnp.concatenate(made, axis=1).astype(BF16)
+        for k, tick in ticks.items():
+            pl.when(t == k)(lambda tick=tick: (tick(), None)[1])
+        return 0
+
+    lax.fori_loop(0, 2 * (cols // pair), attend_step, 0)
+    local.copy(mine, mine_out)
+    local.copy(stats, stats_out)
+    local.copy(o_all, o_out)
+
+    for k in from_far:
+        k.wait_recv()
+    local.copy(far, far_out)
+
+    def project_out(t, _):
+        r = pl.ds(pl.multiple_of(t * step_q, step_q), step_q)
+        total_r = dg(mine[y, r], o_all[y].reshape(width, cols), 1, 1)
+        total_r += dg(far[r], o_all[at.ny].reshape(width, cols), 1, 1)
+        total_r += h_ref[r].astype(F32) + total + par[3:4]
+        made, inv_std = normalize(total_r)
+        unit[r] = made
+        inv[r] = jnp.broadcast_to(inv_std, (step_q, 128))
+        mid[r] = (made * par[7:8] + par[4:5]).astype(BF16)
+        return 0
+
+    lax.fori_loop(0, own_rows // step_q, project_out, 0)
+    local.copy(unit, unit_out)
+    local.copy(inv, inv_out)
+    local.copy(mid, mid_out)
+
+    chunk = 512
+    per = hidden // 2 // chunk
+    later = {
+        0: lambda: next(in_w[1]),
+        1: lambda: next(down_w[1]),
+        3: lambda: next(in_w[1], None),
+        4: lambda: next(down_w[0]),
+        6: lambda: next(down_w[1]),
+    }
+
+    def feed_step(t, _):
+        side = (t // per) % 2
+        n = pl.multiple_of((t // (2 * per)) * (hidden // 2) + (t % per) * chunk, chunk)
+        made = dg(mid[...], i_all[side, :, :, :, :, pl.ds(n, chunk)].reshape(width, chunk), 1, 0)
+        made = made + ffn_b[:, pl.ds(pl.multiple_of(side * hidden, hidden) + n, chunk)]
+        below = 0.5 + 0.5 * lax.erf(made * math.sqrt(0.5))
+        act[side, :, pl.ds(n, chunk)] = (made * below).astype(BF16)
+        bell = jnp.exp(-0.5 * made * made) * (1.0 / math.sqrt(2.0 * math.pi))
+        slope[side, :, pl.ds(n, chunk)] = (below + made * bell).astype(BF16)
+        pltpu.make_async_copy(
+            act.at[side, :, pl.ds(n, chunk)], act_out.at[side, :, pl.ds(n, chunk)], tile_sems.at[0, t]
+        ).start()
+        pltpu.make_async_copy(
+            slope.at[side, :, pl.ds(n, chunk)], slope_out.at[side, :, pl.ds(n, chunk)], tile_sems.at[1, t]
+        ).start()
+        for k, tick in later.items():
+            pl.when(t == k)(lambda tick=tick: (tick(), None)[1])
+        return 0
+
+    tiles = 4 * per
+    lax.fori_loop(0, tiles, feed_step, 0)
+    local.copy(i_all, i_out)
+    next(down_w[0], None)
+    next(down_w[1], None)
+    for t in range(tiles):
+        n = pl.ds(0, chunk)
+        pltpu.make_async_copy(act.at[0, :, n], act_out.at[0, :, n], tile_sems.at[0, t]).wait()
+        pltpu.make_async_copy(slope.at[0, :, n], slope_out.at[0, :, n], tile_sems.at[1, t]).wait()
+    local.close()
     wire.close()
 
 
-def gather_weights(v, o, i, d, h):
-    def whole(a, lead):
-        return jax.ShapeDtypeStruct(lead + a.shape, a.dtype)
-
+def forward(v, t, few_row, bias_zero, o, i, d, h, seg_row, seg_col):
+    rows, cols, hidden = v.shape[0], o.shape[1], i.shape[1]
+    own_rows, width = h.shape
+    length = 2 * own_rows
+    pairs = cols // (2 * HD)
+    S = jax.ShapeDtypeStruct
     dp3 = (4, 2, 2)
-    copies = 9 + 15 * 5 + 1
+    v_all, o_all, i_all = S(dp3 + v.shape, BF16), S((2,) + dp3 + o.shape, BF16), S((2,) + dp3 + i.shape, BF16)
+    few = S((16,) + few_row.shape, F32)
+    par, time_row = S((128, width), F32), S((1, width), F32)
+    embed, qkv = S((2, own_rows, width), BF16), S((length, 3 * cols), BF16)
+    mine, far = S((2, own_rows, cols), BF16), S((own_rows, cols), BF16)
+    stats = S((pairs, 2, length), F32)
+    unit, inv, mid = S((own_rows, width), F32), S((own_rows, 128), F32), S((own_rows, width), BF16)
+    act = S((2, own_rows, hidden), BF16)
+    outs = [v_all, o_all, i_all, i_all, few, par, time_row, embed, qkv, mine, far, stats, unit, inv, mid, act, act]
+    vm, hbm = pl.BlockSpec(memory_space=pltpu.VMEM), pl.BlockSpec(memory_space=pl.ANY)
+    out_specs = [hbm] * len(outs)
+    out_specs[6] = vm
+    part, got = S((16, 1, width), F32), S((15, 1, width), F32)
+    h_far, ffn_b = S(h.shape, BF16), S((1, 2 * hidden), F32)
+    scratch = [v_all, o_all, i_all, few, part, got, h_far, par, ffn_b, embed, qkv, mine, far, stats, unit, inv, mid, act, act]
+    copies = 15 + 15 + 1 + 2 * 9 + 5 * 15 + pairs
     return pl.pallas_call(
-        gather_kernel,
-        name="gather_weights",
-        out_shape=[
-            whole(v, dp3),
-            whole(o, (2,) + dp3),
-            whole(i, (2,) + dp3),
-            whole(d, (2,) + dp3),
-            whole(h, (2,)),
-        ],
-        in_specs=[pl.BlockSpec(memory_space=pltpu.VMEM)] * 5,
-        out_specs=[pl.BlockSpec(memory_space=pl.ANY)] * 5,
-        scratch_shapes=[
+        forward_kernel,
+        name="forward",
+        out_shape=outs,
+        in_specs=[vm] * 10,
+        out_specs=out_specs,
+        scratch_shapes=[pltpu.VMEM(a.shape, a.dtype) for a in scratch]
+        + [
             pltpu.SemaphoreType.DMA((copies,)),
             pltpu.SemaphoreType.DMA((copies,)),
-            pltpu.SemaphoreType.DMA((5,)),
+            pltpu.SemaphoreType.DMA((FORWARD_LOCAL,)),
+            pltpu.SemaphoreType.DMA((2, 2 * hidden // 512)),
         ],
         compiler_params=pltpu.CompilerParams(
-            collective_id=0, has_side_effects=True, vmem_limit_bytes=16 * 1024 * 1024
+            collective_id=0, has_side_effects=True, vmem_limit_bytes=VMEM_LIMIT
         ),
-    )(v, o, i, d, h)
+    )(v, t, few_row, bias_zero, o, i, d, h, seg_row, seg_col)
+
+
+FORWARD_LOCAL = 17
 
 
 def add_blocks(dst, left, right, lead):
@@ -224,47 +441,47 @@
     lax.fori_loop(0, count, one, 0)
 
 
-def reduce_dp(wire, near, here, grad, rc, rx, rz, out):
-    z, x, c, y = here
-    from_c = wire.send(grad.at[:, :, 1 - c], rc, near["c"])
+def reduce_dp(wire, at, grad, rc, rx, rz, out):
+    z, x, c, y = at.z, at.x, at.c, at.y
+    from_c = wire.send(grad.at[:, :, at.nc], rc, at.to_c)
     yield
     from_c.wait_recv()
     add_blocks(rc, grad.at[:, :, c], rc, (4, 2))
-    from_x = wire.send(rc.at[:, 1 - x], rx, near["x"])
+    from_x = wire.send(rc.at[:, at.nx], rx, at.to_x)
     yield
     from_x.wait_recv()
     add_blocks(rx, rc.at[:, x], rx, (4,))
-    from_z = [wire.send(rx.at[p], rz.at[j], to) for j, (p, to) in enumerate(zip(z_places(z), near["z"]))]
+    from_z = [wire.send(rx.at[p], rz.at[j], to) for j, (p, to) in enumerate(zip(at.zs, at.to_z))]
     yield
     for k in from_z:
         k.wait_recv()
     out[...] = ((rx[z].astype(F32) + rz[0].astype(F32)) + rz[1].astype(F32)) + rz[2].astype(F32)
 
 
-def reduce_all(wire, near, here, grad, rc, ya, xb, xa, yb, rz, out, lo, mid, hi):
-    z, x, c, y = here
+def reduce_all(wire, at, grad, rc, ya, xb, xa, yb, rz, out, lo, mid, hi):
+    z, x, c, y = at.z, at.x, at.c, at.y
     a, b, ab = pl.ds(lo, mid - lo), pl.ds(mid, hi - mid), pl.ds(lo, hi - lo)
     half_a, half_b = pl.ds(0, mid - lo), pl.ds(mid - lo, hi - mid)
-    from_c = wire.send(grad.at[:, :, :, 1 - c, :, ab], rc, near["c"])
+    from_c = wire.send(grad.at[:, :, :, at.nc, :, ab], rc, at.to_c)
     yield
     from_c.wait_recv()
     add_blocks(rc, grad.at[:, :, :, c, :, ab], rc, (2, 4, 2))
-    from_y_a = wire.send(rc.at[1 - y, :, :, :, half_a], ya, near["y"])
-    from_x_b = wire.send(rc.at[:, :, 1 - x, :, half_b], xb, near["x"])
+    from_y_a = wire.send(rc.at[at.ny, :, :, :, half_a], ya, at.to_y)
+    from_x_b = wire.send(rc.at[:, :, at.nx, :, half_b], xb, at.to_x)
     yield
     from_y_a.wait_recv()
     add_blocks(ya, rc.at[y, :, :, :, half_a], ya, (4, 2))
-    from_x_a = wire.send(ya.at[:, 1 - x], xa, near["x"])
+    from_x_a = wire.send(ya.at[:, at.nx], xa, at.to_x)
     from_x_b.wait_recv()
     add_blocks(xb, rc.at[:, :, x, :, half_b], xb, (2, 4))
-    from_y_b = wire.send(xb.at[1 - y], yb, near["y"])
+    from_y_b = wire.send(xb.at[at.ny], yb, at.to_y)
     yield
     from_x_a.wait_recv()
     add_blocks(xa, ya.at[:, x], xa, (4,))
     from_y_b.wait_recv()
     add_blocks(yb, xb.at[y], yb, (4,))
     from_z = []
-    for j, (p, to) in enumerate(zip(z_places(z), near["z"])):
+    for j, (p, to) in enumerate(zip(at.zs, at.to_z)):
         from_z.append(wire.send(xa.at[p], rz.at[j, :, half_a], to))
         from_z.append(wire.send(yb.at[p], rz.at[j, :, half_b], to))
     yield
@@ -276,20 +493,20 @@
         ) + rz[2, :, half].astype(F32)
 
 
-def reduce_small(wire, near, here, mine, sums, got, out):
-    k = wire.send(mine, got.at[0], near["c"])
+def reduce_small(wire, at, mine, sums, got, out):
+    k = wire.send(mine, got.at[0], at.to_c)
     yield
     k.wait_recv()
     sums[0] = mine[...] + got[0]
-    k = wire.send(sums.at[0], got.at[1], near["x"])
+    k = wire.send(sums.at[0], got.at[1], at.to_x)
     yield
     k.wait_recv()
     sums[1] = sums[0] + got[1]
-    k = wire.send(sums.at[1], got.at[2], near["y"])
+    k = wire.send(sums.at[1], got.at[2], at.to_y)
     yield
     k.wait_recv()
     sums[2] = sums[1] + got[2]
-    last = [wire.send(sums.at[2], got.at[3 + j], to) for j, to in enumerate(near["z"])]
+    last = [wire.send(sums.at[2], got.at[3 + j], to) for j, to in enumerate(at.to_z)]
     yield
     for k in last:
         k.wait_recv()
@@ -300,24 +517,22 @@
 
 
 def reduce_kernel(v_g, o_g, i_g, d_g, x_part, small, v_out, o_out, i_out, d_out, x_got, s_out, *rest):
-    here = place()
-    z, x, c, y = here
-    near = peers(*here)
-    enter(near)
+    at = Place()
+    at.enter(False)
     rest = list(rest)
     send_sems, recv_sems = rest[0], rest[1]
     scratch = iter(rest[2:])
-    wire = Wire(send_sems, recv_sems)
+    wire = Wire(at, send_sems, recv_sems)
     sums, got = next(scratch), next(scratch)
-    tiny = reduce_small(wire, near, here, small, sums, got, s_out)
-    from_y = wire.send(x_part.at[1 - y], x_got, near["y"])
+    tiny = reduce_small(wire, at, small, sums, got, s_out)
+    from_y = wire.send(x_part.at[at.ny], x_got, at.to_y)
     streams = []
     for grad, out, parts in ((d_g, d_out, ALL_CUTS[2]), (i_g, i_out, ALL_CUTS[1]), (o_g, o_out, ALL_CUTS[0])):
         for cut in parts_of(out.shape[1], parts):
             bufs = [next(scratch) for _ in range(6)]
-            streams.append(reduce_all(wire, near, here, grad, *bufs, out, *cut))
+            streams.append(reduce_all(wire, at, grad, *bufs, out, *cut))
     bufs = [next(scratch) for _ in range(3)]
-    streams.append(reduce_dp(wire, near, here, v_g, *bufs, v_out))
+    streams.append(reduce_dp(wire, at, v_g, *bufs, v_out))
     stagger([tiny] + streams)
     from_y.wait_recv()
     wire.close()
@@ -486,10 +701,6 @@
     )
 
 
-def exact_gelu(array_in):
-    return jax.nn.gelu(array_in, approximate=False)
-
-
 def ein(spec, left, right):
     return jnp.einsum(spec, left, right, preferred_element_type=F32)
 
@@ -519,79 +730,78 @@
     dp_index, mp_index = lax.axis_index("dp"), lax.axis_index("mp")
     fast = (dp, mp) == (16, 2)
 
-    bias_count = biases.shape[0] + gains.shape[0] + ffn_bias.shape[0] // rows
+    bias_count = biases.shape[0] + gains.shape[0]
     v_shard = jnp.concatenate(
-        [
-            qkv_weight[0],
-            qkv_weight[1],
-            qkv_weight[2],
-            time_weight,
-            biases.T,
-            gains.T,
-            ffn_bias.reshape(rows, -1),
-            jnp.broadcast_to(jnp.stack([timesteps // 64, timesteps % 64], axis=1), (rows, 2)).astype(BF16),
-            jnp.zeros((rows, 126 - bias_count), BF16),
-        ],
+        [qkv_weight[0], qkv_weight[1], qkv_weight[2], biases.T, gains.T, jnp.zeros((rows, 128 - bias_count), BF16)],
         axis=1,
     )
-    shards = (v_shard, out_weight.T, in_weight, down_weight.T, hidden_in)
+    feature = time_features(timesteps, width).astype(BF16)
+    few_row = jnp.concatenate([feature.astype(F32), ffn_bias.astype(F32)[None]], axis=1)
+    seg_col = jnp.broadcast_to(segments.reshape(length, 1), (length, 128))
     if fast:
-        v_all, o_all, i_all, d_all, h_all = gather_weights(*shards)
+        (
+            v_all, o_all, i_all, d_all, few, par, time_row, embed_low, qkv, mixed_heads, mixed_far,
+            stats, unit_one, inv_one, middle_low, hidden_act, slope,
+        ) = forward(
+            v_shard, time_weight, few_row, biases[:1], out_weight.T, in_weight, down_weight.T,
+            hidden_in, segments, seg_col,
+        )
+        few = few.reshape(dp, -1)
+        inv_one = inv_one[:, :1]
+        own = jnp.arange(2)[:, None, None] == mp_index
+        mixed = jnp.where(own, mixed_heads, mixed_far[None])
     else:
-        v_all = lax.all_gather(shards[0], "dp", axis=0)
+        v_all = lax.all_gather(v_shard, "dp", axis=0)
         o_all, i_all, d_all = (
-            lax.all_gather(lax.all_gather(a, "dp", axis=0), "mp", axis=0) for a in shards[1:4]
+            lax.all_gather(lax.all_gather(a, "dp", axis=0), "mp", axis=0)
+            for a in (out_weight.T, in_weight, down_weight.T)
         )
-        h_all = lax.all_gather(hidden_in, "mp", axis=0)
+        few = lax.all_gather(few_row, "dp", axis=0, tiled=True)
+        time_w = lax.all_gather(time_weight, "dp", axis=0, tiled=True)
     v_all = v_all.reshape(width, -1)
     o_all, i_all, d_all = (a.reshape(mp, width, -1) for a in (o_all, i_all, d_all))
-    h_all = h_all.reshape(length, width)
-
     qkv_w = v_all[:, : 3 * cols]
-    time_w = v_all[:, 3 * cols : 3 * cols + width]
-    params = v_all[:, 3 * cols + width :].astype(F32)
-    bias_all = params[:, :7].T
-    gain_all = params[:, 7:9].T
-    ffn_b = params[:, 9 : 9 + ffn_bias.shape[0] // rows].reshape(mp, hidden)
-
-    feature = time_features(timesteps, width).astype(BF16)
-    time_row = jnp.dot(feature, time_w, preferred_element_type=F32) + bias_all[0]
-    embedded = hidden_in.astype(F32) + time_row
-    embed_low = (h_all.astype(F32) + time_row).astype(BF16)
     column = mp_index * cols
-    bias_qkv = jnp.concatenate(
-        [
-            lax.dynamic_slice_in_dim(bias_all[1], column, cols),
-            jnp.zeros((cols,), F32),
-            lax.dynamic_slice_in_dim(bias_all[2], column, cols),
-        ]
-    )
-    qkv = (jnp.dot(embed_low, qkv_w, preferred_element_type=F32) + bias_qkv).astype(BF16)
-    mixed_heads, stats = attend(qkv, segments)
-
-    def heads_to_rows(array_in):
-        cut = array_in.reshape(mp, own_rows, cols)
-        return trade(cut)
-
-    def rows_to_heads(array_in):
-        return trade(array_in).reshape(length, cols)
-
-    def trade(cut):
+    if fast:
+        bias_all, gain_all = par[:7], par[7:9]
+        middle = unit_one * gain_all[0] + bias_all[4]
+    else:
+        params = v_all[:, 3 * cols :].astype(F32).T
+        bias_all, gain_all = params[:7], params[7:9]
+        time_row = jnp.dot(feature, time_w, preferred_element_type=F32) + bias_all[0]
+        h_all = lax.all_gather(hidden_in, "mp", axis=0, tiled=True)
+        embedded = hidden_in.astype(F32) + time_row
+        embed_low = (h_all.astype(F32) + time_row).astype(BF16)
+        bias_qkv = jnp.concatenate(
+            [
+                lax.dynamic_slice_in_dim(bias_all[1], column, cols),
+                jnp.zeros((cols,), F32),
+                lax.dynamic_slice_in_dim(bias_all[2], column, cols),
+            ]
+        )
+        qkv = (jnp.dot(embed_low, qkv_w, preferred_element_type=F32) + bias_qkv).astype(BF16)
+        mixed_heads, stats = attend(qkv, segments)
+        mixed = lax.all_to_all(mixed_heads.reshape(mp, own_rows, cols), "mp", 0, 0, tiled=True)
+        attn_total = ein("yrk,ynk->rn", mixed, o_all)
+        unit_one, inv_one = normalize(embedded + attn_total + bias_all[3])
+        middle = unit_one * gain_all[0] + bias_all[4]
+        middle_low = middle.astype(BF16)
+        ffn_b = few[:, width:].reshape(mp, hidden)
+        pre_act = ein("rd,ydf->yrf", middle_low, i_all) + ffn_b[:, None, :]
+        below = 0.5 + 0.5 * lax.erf(pre_act * math.sqrt(0.5))
+        hidden_act = (pre_act * below).astype(BF16)
+        slope = below + pre_act * jnp.exp(-0.5 * pre_act * pre_act) * (1.0 / math.sqrt(2.0 * math.pi))
+    embed_low = embed_low.reshape(length, width)
+    mixed_heads = mixed_heads.reshape(length, cols)
+
+    def rows_to_heads(cut):
         if mp == 2:
             far = lax.ppermute(
                 lax.dynamic_index_in_dim(cut, 1 - mp_index, 0, False), "mp", [(0, 1), (1, 0)]
             )
-            own = jnp.arange(2)[:, None, None] == mp_index
-            return jnp.where(own, cut, far[None])
-        return lax.all_to_all(cut, "mp", 0, 0, tiled=True)
-
-    mixed = heads_to_rows(mixed_heads)
-    attn_total = ein("yrk,ynk->rn", mixed, o_all)
-    unit_one, inv_one = normalize(embedded + attn_total + bias_all[3])
-    middle = unit_one * gain_all[0] + bias_all[4]
-    middle_low = middle.astype(BF16)
-    pre_act = ein("rd,ydf->yrf", middle_low, i_all) + ffn_b[:, None, :]
-    hidden_act = exact_gelu(pre_act).astype(BF16)
+            return jnp.where(own, cut, far[None]).reshape(length, cols)
+        return lax.all_to_all(cut, "mp", 0, 0, tiled=True).reshape(length, cols)
+
     ffn_total = ein("yrf,ynf->rn", hidden_act, d_all)
     unit_two, inv_two = normalize(middle + ffn_total + bias_all[5])
     layer_out = (unit_two * gain_all[1] + bias_all[6]).astype(BF16)
@@ -604,7 +814,7 @@
     d_ffn = d_pre_two.astype(BF16)
     down_grad = ein("rn,yrf->ynf", d_ffn, hidden_act).astype(BF16)
     d_act = ein("rn,ynf->yrf", d_ffn, d_all)
-    d_pre_act = jax.vjp(exact_gelu, pre_act)[1](d_act)[0]
+    d_pre_act = d_act * slope.astype(F32)
     ffn_bias_part = jnp.sum(d_pre_act, axis=1).reshape(-1, width)
     d_pre_low = d_pre_act.astype(BF16)
     in_grad = ein("rd,yrf->ydf", middle_low, d_pre_low).astype(BF16)
@@ -671,9 +881,7 @@
     input_grad = d_pre_one + d_own
     d_time = small[:dp]
     start = dp_index * rows
-    step_parts = params[::rows, bias_count : bias_count + 2]
-    step_ids = 64.0 * step_parts[:, 0] + step_parts[:, 1]
-    features = time_features(step_ids, width).astype(BF16).astype(F32)
+    features = few[:, :width]
     features = lax.dynamic_slice_in_dim(features, start, rows, axis=1)
     time_grad = lax.dot_general(
         features, d_time, (((0,), (0,)), ((), ())), precision=lax.Precision.HIGHEST

time: 537 us -> 455 us (0.85)
  matrix products: 103 us -> 65.6 us
  Pallas kernels: 353 us -> 336 us
  local copies, waits for them, and re-layouts: 38.1 us -> 26.9 us
  waiting for transfers between devices: 8.56 us -> 0.01 us
    dot_general x9 -> x7, matrix products: 80 us -> 53.5 us  [ein(): return jnp.einsum(spec, left, right, preferred_element_type=F32)]
    pallas_call x2 -> x1, Pallas kernels: 178 us -> 157 us  [forward(): pl.pallas_call(forward_kernel, name='forward', out_shape=outs, in_specs=[...]
    unnamed x85 -> x45, local copies, waits for them, and re-layouts: 20.5 us -> 9.74 us
    dot_general x2 -> x0, matrix products: 9.5 us -> none  [the longest x1 7.37 us: on_device(): jnp.dot(embed_low, qkv_w, preferred_element_type=F32) + bias_qkv]
    ppermute x2 -> x1, waiting for transfers between devices: 8.56 us -> 0.01 us  [rows_to_heads(): lax.ppermute(lax.dynamic_index_in_dim(cut, 1 - mp_index, 0, False), 'mp',...]
  transfers between devices with their start and end apart: 2 -> 1, of which waited for: 1 -> 0; matrix products, arithmetic and copies ran while one was open for 4% -> 6% of each run, Pallas kernels for 0% -> 0%
where the time goes in v2:
time: 455 us; the launch traced here: 449 us
  Pallas kernels  336 us (74%)
  matrix products  65.6 us (14%)
  local copies, waits for them, and re-layouts  26.9 us (6%)
  other arithmetic  17.2 us (4%)
    pallas_call x1, Pallas kernels, forward(): pl.pallas_call(forward_kernel, name='forward', out_shape=outs, in_specs=[...  157 us
    pallas_call x1, Pallas kernels, reduce_grads(): pl.pallas_call(reduce_kernel, name='reduce_grads', out_shape=out + [jax.S...  151 us
    dot_general x7, matrix products, ein(): return jnp.einsum(spec, left, right, preferred_element_type=F32)  53.5 us
    pallas_call x1, Pallas kernels, attend_back(): pl.pallas_call(functools.partial(attend_back_kernel, min(512, length)), n...  28.6 us
    dot_general x2, matrix products, dg(): lax.dot_general(left, right, (((left_dim,), (right_dim,)), ((), ())), pre...  10.2 us
    unnamed x45, local copies, waits for them, and re-layouts  9.74 us
  transfers between devices with their start and end apart: 1, of which 0 were waited for; matrix products, arithmetic and copies ran while one was open for 6% of the time, Pallas kernels for 0%

profile of v2, /device:TPU:20, one launch (start us, length us, event | category | flops | bytes accessed | tf_op | source)
XLA Modules:
  0.0 448.6 jit_solution(6937232523229367249)
XLA Ops:
  0.6 1.2 slice.64.b_ref
  4.8 0.9 slice_bitcast_fusion
  7.1 1.7 broadcast_in_dim.83.sc_ref
  8.8 156.6 %forward.1 = (bf16[4,2,2,64,1664]{4,3,2,1,0:T(8,128)(2,1)}, bf16[2,4,2,2,64,512]{5,4,3,2,1,0:T(8,128)(2,1)}, bf16[2,4,2,2,64,2048]{5,4,3,2,1,0:T(8,128)(2,1)}, b...) custom-call(bf16[64,1664]{1,0:T(8,128)(2,1)} %concatenate.33.v_ref, ...), custom_call_target="tpu_custom_call" | custom-call | tf_op jit(solution)/shard_map/forward/pallas_call | solution.py:407
  165.4 0.9 fusion.41
  166.3 1.1 slice_reduce_fusion
  167.4 10.0 %fusion.42 = (f32[512]{0:T(512)S(1)}, f32[512,1024]{1,0:T(8,128)S(1)}) fusion(f32[1024]{0:T(1024)S(1)} %bitcast.135, bf16[2,512,2048]{2,1,0:T(8,128)(2,1)} %get-tuple-element.37, bf16[2,1024,2048]{2,1,0:T(8,128)(2,1)} %bitcast.138, f32[1024]{0:T(1024)S(1)} %bitcast.136, f32[512,1024]{1,0:T(8,128)} %get-tuple-element.35, f32[1024]{0:T(1024)S(1)} %bitcast.125), kind=kOutput, calls=%fused_computation.87 | convolution fusion | flops 4297588224 | bytes 16791552 | tf_op jit(solution)/shard_map/yrf,ynf->rn/dot_general | solution.py:705
  177.8 0.9 copy-done
  178.6 1.0 fusion.10
  179.6 1.8 fusion.35
  181.5 0.9 copy-done.10
  182.4 7.1 %fusion = (f32[2,2048]{1,0:T(2,128)S(1)}, f32[2,2048,512]{1,2,0:T(8,128)}) fusion(bf16[2,512,2048]{2,1,0:T(8,128)(2,1)S(1)} %copy-done.11, bf16[2,1024,2048]{2,1,0:T(8,128)(2,1)S(1)} %bitcast.139, f32[512,1024]{1,0:T(8,128)S(1)} %get-tuple-element.79), kind=kOutput, calls=%fused_computation.1 | convolution fusion | flops 4301778944 | bytes 23085056 | tf_op jit(solution)/shard_map/rn,ynf->yrf/dot_general | solution.py:705
  189.5 13.2 %multiply_reduce_fusion = (f32[1024]{0:T(1024)S(1)}, f32[512]{0:T(512)S(1)}, f32[512]{0:T(512)S(1)}, f32[1024]{0:T(1024)S(1)}, f32[512,1024]{1,0:T(8,128)}) fusion(f32[512,1024]{1,0:T(8,128)S(1)} %copy-done.2, f32[1024]{0:T(1024)S(1)} %bitcast.126, f32[512,1024]{1,0:T(8,128)S(1)} %get-tuple-element.79, bf16[2,1024,2048]{2,1,0:T(8,128)(2,1)} %bitcast.137, ...), kind=kOutput, calls=%fused_computation.24 | convolution fusion | flops 4305449984 | bytes 27279360 | tf_op jit(solution)/shard_map/yrf,ydf->rd/dot_general | solution.py:705
  202.7 2.9 fusion.37
  205.6 1.3 convolution_convert_fusion.3
  206.9 0.8 dynamic-slice_bitcast_fusion
  208.6 7.0 %convolution_convert_fusion = bf16[2,2048,1024]{1,2,0:T(8,128)(2,1)} fusion(bf16[2,512,2048]{2,1,0:T(8,128)(2,1)S(1)} %copy-done.13, f32[512,1024]{1,0:T(8,128)S(1)} %copy-done.5), kind=kOutput, calls=%fused_computation.3 | convolution fusion | flops 4299685888 | bytes 14680064 | tf_op jit(solution)/shard_map/rn,yrf->ynf/dot_general | solution.py:705
  215.7 10.8 %convolution_convert_fusion.1 = bf16[2,2048,1024]{1,2,0:T(8,128)(2,1)} fusion(bf16[512,1024]{1,0:T(8,128)(2,1)S(1)} %copy-done.17, bf16[2,512,2048]{2,1,0:T(8,128)(2,1)S(1)} %copy-done.12, f32[2,2048,512]{1,2,0:T(8,128)} %get-tuple-element.102), kind=kOutput, calls=%fused_computation.4 | convolution fusion | flops 4305453056 | bytes 22020096 | tf_op jit(solution)/shard_map/rd,yrf->ydf/dot_general | solution.py:705
  226.6 4.0 convert_bitcast_fusion
  230.6 4.2 copy.32
  234.8 2.2 bitcast_select_fusion
  237.0 28.6 %attend_back.1 = (f32[1024,512]{1,0:T(8,128)}, f32[1024,512]{1,0:T(8,128)}, f32[1024,512]{1,0:T(8,128)}) custom-call(bf16[1024,1536]{1,0:T(8,128)(2,1)} %get-tuple-element.42.q_ref.k_ref.v_ref, bf16[1024,1536]{1,0:T(8,128)(2,1)} %get-tuple-element.42.q_ref.k_ref.v_ref, bf16[1024,1536]{1,0:T(8,128)(2,1)} %get-tuple-element.42.q_ref.k_ref.v_ref, ...), custom_call_target="tpu_custom_call" | custom-call | flops 5368709120 | bytes 8388608 | tf_op jit(solution)/shard_map/attend_back/pallas_call | solution.py:665
  265.6 2.7 fusion.40
  268.6 1.4 copy-done.3
  271.0 4.6 %fusion.38 = (f32[1024]{0:T(1024)S(1)}, bf16[1024,1024]{1,0:T(8,128)(2,1)}) fusion(bf16[1024,1664]{1,0:T(8,128)(2,1)S(1)} %bitcast.140, bf16[1024,512]{1,0:T(8,128)(2,1)S(1)} %get-tuple-element.86, bf16[1024,512]{1,0:T(8,128)(2,1)S(1)} %convert.23, bf16[1024,512]{1,0:T(8,128)(2,1)S(1)} %get-tuple-element.88), kind=kOutput, calls=%fused_computation.83 | convolution fusion | flops 3232758784 | bytes 8392704 | tf_op jit(solution)/shard_map/dot_general | solution.py:20
  275.6 5.5 %convolution_convert_fusion.2 = bf16[1024,1536]{1,0:T(8,128)(2,1)} fusion(bf16[1024,1024]{1,0:T(8,128)(2,1)S(1)} %bitcast.141, bf16[1024,512]{1,0:T(8,128)(2,1)S(1)} %get-tuple-element.86, bf16[1024,512]{1,0:T(8,128)(2,1)S(1)} %convert.23, bf16[1024,512]{1,0:T(8,128)(2,1)S(1)} %get-tuple-element.88), kind=kOutput, calls=%fused_computation.5 | convolution fusion | flops 3232235520 | bytes 8388608 | tf_op jit(solution)/shard_map/dot_general | solution.py:20
  282.0 151.1 %reduce_grads.1 = (f32[64,1536]{1,0:T(8,128)}, f32[64,512]{1,0:T(8,128)}, f32[64,2048]{1,0:T(8,128)}, f32[64,2048]{1,0:T(8,128)}, bf16[512,1024]{1,0:T(8,128)(2,1)}, /*index=5*/f32[32,1024]{1,0:T(8,128)}) custom-call(bf16[4,2,2,64,1536]{4,3,2,1,0:T(8,128)(2,1)} %bitcast.108, bf16[2,4,2,2,64,512]{5,4,3,2,1,0:T(8,128)(2,1)} %bitcast.105, ...), custom_call_target="tpu_custom_call" | custom-call | tf_op jit(solution)/shard_map/reduce_grads/pallas_call | solution.py:567
  433.1 0.9 slice_reduce_fusion.1
  436.9 2.0 fusion.26
  438.9 1.3 reshape.176
  440.2 0.9 copy.35
  441.1 3.5 fusion.11
  (76 shorter events, 13.6 us)
Async XLA Ops:
  167.4 14.1 %copy-start.11 = (bf16[2,512,2048]{2,1,0:T(8,128)(2,1)S(1)}, bf16[2,512,2048]{2,1,0:T(8,128)(2,1)}, u32[]{:S(2)}) copy-start(bf16[2,512,2048]{2,1,0:T(8,128)(2,1)} %get-tuple-element.40) | copy-start | bytes 12582916
  177.4 1.2 copy-start
  178.6 3.8 copy-start.10
  181.5 8.0 %copy-start.4 = (f32[512,1024]{1,0:T(8,128)}, f32[512,1024]{1,0:T(8,128)S(1)}, u32[]{:S(2)}) copy-start(f32[512,1024]{1,0:T(8,128)S(1)} %get-tuple-element.79) | copy-start | bytes 6291460
  182.4 7.1 %copy-start.2 = (f32[512,1024]{1,0:T(8,128)S(1)}, f32[512,1024]{1,0:T(8,128)}, u32[]{:S(2)}) copy-start(f32[512,1024]{1,0:T(8,128)} %get-tuple-element.35) | copy-start | bytes 6291460
  202.7 2.9 copy-start.16
  205.6 2.7 copy-start.5
  205.6 3.0 copy-start.13
  207.8 7.9 %copy-start.12 = (bf16[2,512,2048]{2,1,0:T(8,128)(2,1)S(1)}, bf16[2,512,2048]{2,1,0:T(8,128)(2,1)}, u32[]{:S(2)}) copy-start(bf16[2,512,2048]{2,1,0:T(8,128)(2,1)} %get-tuple-element.40) | copy-start | bytes 12582916
  207.8 7.9 %copy-start.17 = (bf16[512,1024]{1,0:T(8,128)(2,1)S(1)}, bf16[512,1024]{1,0:T(8,128)(2,1)}, u32[]{:S(2)}) copy-start(bf16[512,1024]{1,0:T(8,128)(2,1)} %get-tuple-element.52) | copy-start | bytes 3145732
  207.8 27.0 %collective-permute-start = (bf16[512,512]{1,0:T(8,128)(2,1)}, bf16[512,512]{1,0:T(8,128)(2,1)}, u32[]{:S(2)}, u32[]{:S(2)}) collective-permute-start(bf16[512,512]{1,0:T(8,128)(2,1)} %dynamic-slice_bitcast_fusion), channel_id=1, source_target_pairs={{0,1},{1,0},{2,3},{3,2},{4,5},{5,4},{6,7},{7,6},{8,9},{9,8},{10,11... | collective-permute-start | bytes 1572872 | tf_op jit(solution)/shard_map/ppermute | solution.py:799
  215.7 10.9 %copy-start.9 = (f32[16,1,1280]{2,1,0:T(1,128)S(1)}, f32[16,1,1280]{2,1,0:T(1,128)}, u32[]{:S(2)}) copy-start(f32[16,1,1280]{2,1,0:T(1,128)} %get-tuple-element.54) | copy-start | bytes 245764
  265.6 2.9 copy-start.1
  268.3 1.6 copy-start.3
  268.5 2.5 copy-start.14
  271.0 4.6 %copy-start.15 = (bf16[2,512,1024]{2,1,0:T(8,128)(2,1)S(1)}, bf16[2,512,1024]{2,1,0:T(8,128)(2,1)}, u32[]{:S(2)}) copy-start(bf16[2,512,1024]{2,1,0:T(8,128)(2,1)} %get-tuple-element.50) | copy-start | bytes 6291460
  441.1 4.8 %copy-start.8 = (f32[64,512]{1,0:T(8,128)S(1)}, f32[64,512]{1,0:T(8,128)}, u32[]{:S(2)}) copy-start(f32[64,512]{1,0:T(8,128)} %get-tuple-element.57) | copy-start | bytes 393220
  441.1 5.5 %copy-start.7 = (f32[64,2048]{1,0:T(8,128)S(1)}, f32[64,2048]{1,0:T(8,128)}, u32[]{:S(2)}) copy-start(f32[64,2048]{1,0:T(8,128)} %get-tuple-element.120) | copy-start | bytes 1572868
  441.1 6.3 %copy-start.6 = (f32[64,2048]{1,0:T(8,128)S(1)}, f32[64,2048]{1,0:T(8,128)}, u32[]{:S(2)}) copy-start(f32[64,2048]{1,0:T(8,128)} %get-tuple-element.59) | copy-start | bytes 1572868

commit v3 on v2

--- a/solution.py
+++ b/solution.py
@@ -13,7 +13,7 @@
 neg_big = -1000000000.0
 MESH = pl.DeviceIdType.MESH
 F32, BF16 = jnp.float32, jnp.bfloat16
-VMEM_LIMIT = 64000000
+VMEM_LIMIT, VMEM_ALL = 64000000, 67043328
 
 
 def dg(left, right, left_dim, right_dim):
@@ -35,6 +35,7 @@
         self.to_x = ((z * 2 + self.nx) * 2 + c, y)
         self.to_y = (i, self.ny)
         self.to_c = ((z * 2 + x) * 2 + self.nc, y)
+        self.count = [self.zero + j for j in range(3)]
         self.dp = [
             (pz * 2 + px) * 2 + pc
             for pz in [z] + self.zs
@@ -70,6 +71,11 @@
         copy.start()
         self.open.append(copy)
         return copy
+
+    def both(self, copy):
+        copy.wait_send()
+        self.open = [one for one in self.open if one is not copy]
+        copy.wait_recv()
 
     def close(self):
         assert self.used == len(self.sems), self.used
@@ -445,13 +451,13 @@
     z, x, c, y = at.z, at.x, at.c, at.y
     from_c = wire.send(grad.at[:, :, at.nc], rc, at.to_c)
     yield
-    from_c.wait_recv()
+    wire.both(from_c)
     add_blocks(rc, grad.at[:, :, c], rc, (4, 2))
     from_x = wire.send(rc.at[:, at.nx], rx, at.to_x)
     yield
     from_x.wait_recv()
     add_blocks(rx, rc.at[:, x], rx, (4,))
-    from_z = [wire.send(rx.at[p], rz.at[j], to) for j, (p, to) in enumerate(zip(at.zs, at.to_z))]
+    from_z = [wire.send(rx.at[p], rz.at[at.count[j]], to) for j, (p, to) in enumerate(zip(at.zs, at.to_z))]
     yield
     for k in from_z:
         k.wait_recv()
@@ -464,7 +470,7 @@
     half_a, half_b = pl.ds(0, mid - lo), pl.ds(mid - lo, hi - mid)
     from_c = wire.send(grad.at[:, :, :, at.nc, :, ab], rc, at.to_c)
     yield
-    from_c.wait_recv()
+    wire.both(from_c)
     add_blocks(rc, grad.at[:, :, :, c, :, ab], rc, (2, 4, 2))
     from_y_a = wire.send(rc.at[at.ny, :, :, :, half_a], ya, at.to_y)
     from_x_b = wire.send(rc.at[:, :, at.nx, :, half_b], xb, at.to_x)
@@ -482,8 +488,8 @@
     add_blocks(yb, xb.at[y], yb, (4,))
     from_z = []
     for j, (p, to) in enumerate(zip(at.zs, at.to_z)):
-        from_z.append(wire.send(xa.at[p], rz.at[j, :, half_a], to))
-        from_z.append(wire.send(yb.at[p], rz.at[j, :, half_b], to))
+        from_z.append(wire.send(xa.at[p], rz.at[at.count[j], :, half_a], to))
+        from_z.append(wire.send(yb.at[p], rz.at[at.count[j], :, half_b], to))
     yield
     for k in from_z:
         k.wait_recv()
@@ -513,69 +519,257 @@
     out[...] = ((sums[2] + got[3]) + got[4]) + got[5]
 
 
-ALL_CUTS = (1, 2, 2)
-
-
-def reduce_kernel(v_g, o_g, i_g, d_g, x_part, small, v_out, o_out, i_out, d_out, x_got, s_out, *rest):
+def turn_rows(src, dst):
+    def one(t, _):
+        r = pl.ds(pl.multiple_of(t * 128, 128), 128)
+        dst[r, :] = src[:, r].astype(F32).T.astype(BF16)
+        return 0
+
+    lax.fori_loop(0, src.shape[1] // 128, one, 0)
+
+
+def backward_kernel(
+    ffn_ref, mid_ref, attn_ref, act_ref, pre_ref, mix_ref, qkv_ref, embed_ref, v_ref,
+    far_ref, mine_ref, stats_ref, sr_ref, sc_ref, small_ref,
+    v_out, o_out, i_out, d_out, x_own, x_got, s_out, *rest,
+):
     at = Place()
+    y = at.y
     at.enter(False)
-    rest = list(rest)
-    send_sems, recv_sems = rest[0], rest[1]
-    scratch = iter(rest[2:])
-    wire = Wire(at, send_sems, recv_sems)
-    sums, got = next(scratch), next(scratch)
-    tiny = reduce_small(wire, at, small, sums, got, s_out)
-    from_y = wire.send(x_part.at[at.ny], x_got, at.to_y)
-    streams = []
-    for grad, out, parts in ((d_g, d_out, ALL_CUTS[2]), (i_g, i_out, ALL_CUTS[1]), (o_g, o_out, ALL_CUTS[0])):
-        for cut in parts_of(out.shape[1], parts):
-            bufs = [next(scratch) for _ in range(6)]
-            streams.append(reduce_all(wire, at, grad, *bufs, out, *cut))
-    bufs = [next(scratch) for _ in range(3)]
-    streams.append(reduce_dp(wire, at, v_g, *bufs, v_out))
-    stagger([tiny] + streams)
-    from_y.wait_recv()
+    rest = iter(rest)
+    wire, local = Wire(at, next(rest), next(rest)), Local(next(rest))
+    raw, tr, big, d_heads, d_g, i_g, o_g, v_g, acc_k, acc_v, table, sums, got = (next(rest) for _ in range(13))
+    own_rows, width = raw.shape
+    hidden, cols, length = big.shape[2], d_heads.shape[2], 2 * own_rows
+
+    def stream(grad, out, cut):
+        return reduce_all(wire, at, grad, *(next(rest) for _ in range(6)), out, *cut)
+
+    d_s = [stream(d_g, d_out, cut) for cut in parts_of(hidden, 2)]
+    i_s = [stream(i_g, i_out, cut) for cut in parts_of(hidden, 2)]
+    o_s = stream(o_g, o_out, parts_of(cols, 1)[0])
+    v_s = [reduce_dp(wire, at, v_g.at[k], *(next(rest) for _ in range(3)), v_out.at[k]) for k in range(2)]
+    tiny = reduce_small(wire, at, table, sums, got, s_out)
+
+    def done(one):
+        one.wait()
+        local.open = [other for other in local.open if other is not one]
+
+    from_mix = wire.send(mix_ref.at[at.ny], d_heads.at[y], at.to_y)
+    halves = [pl.ds(lo, hi - lo) for lo, _, hi in parts_of(hidden, 2)]
+    raw_in = local.copy(ffn_ref, raw)
+    big_in = [local.copy(act_ref.at[:, :, cut], big.at[:, :, cut]) for cut in halves]
+    mix_in = local.copy(mix_ref.at[y], d_heads.at[y])
+    table[...] = small_ref[...]
+    done(raw_in)
+    turn_rows(raw, tr.at[0])
+    raw_in = local.copy(mid_ref, raw)
+
+    chunk = 512
+    per = hidden // 2 // chunk
+
+    def products(left, grad, part):
+        def one(t, _):
+            side = t // per
+            n = pl.ds(pl.multiple_of(part * (hidden // 2) + (t % per) * chunk, chunk), chunk)
+            made = dg(left[...], big[side, :, n], 1, 0).astype(BF16)
+            grad[side, :, :, :, :, n] = made.reshape(grad.shape[1:5] + (chunk,))
+            return 0
+
+        lax.fori_loop(0, 2 * per, one, 0)
+
+    for part in range(2):
+        done(big_in[part])
+        products(tr.at[0], d_g, part)
+        next(d_s[part])
+        big_in[part] = local.copy(pre_ref.at[:, :, halves[part]], big.at[:, :, halves[part]])
+    done(raw_in)
+    turn_rows(raw, tr.at[1])
+    raw_in = local.copy(attn_ref, raw)
+    done(big_in[0])
+    products(tr.at[1], i_g, 0)
+    next(i_s[0])
+    next(d_s[0])
+    done(big_in[1])
+    products(tr.at[1], i_g, 1)
+    next(i_s[1])
+    qkv_in = local.copy(qkv_ref, big.at[:, :, 0 : 3 * cols])
+    done(raw_in)
+    turn_rows(raw, tr.at[0])
+    for side, right in ((y, mine_ref.at[y]), (at.ny, far_ref)):
+        made = dg(tr[0], right[...], 1, 0).astype(BF16)
+        o_g[side] = made.reshape(o_g.shape[1:])
+    next(o_s)
+    next(d_s[1])
+
+    embed_in = local.copy(embed_ref, d_g.at[0, :, :, :, :, 0:width])
+    v_in = local.copy(v_ref, d_g.at[1, :, :, :, :, 0 : v_ref.shape[4]])
+    done(embed_in)
+
+    def turn_embed(t, _):
+        n = pl.ds(pl.multiple_of(t * 128, 128), 128)
+        block = d_g[0, :, :, :, :, n].reshape(length, 128)
+        d_g[0, t // 2, t % 2, :, :, width : 2 * width] = (
+            block.astype(F32).T.astype(BF16).reshape(d_g.shape[3:5] + (length,))
+        )
+        return 0
+
+    lax.fori_loop(0, width // 128, turn_embed, 0)
+    done(v_in)
+    done(qkv_in)
+    done(mix_in)
+    from_mix.wait_recv()
+
+    part_cols = cols // 2
+
+    def project_grad(k):
+        def one(j, _):
+            n = pl.ds(pl.multiple_of(j * cols + k * part_cols, part_cols), part_cols)
+            made = dg(
+                d_g[0, :, :, :, :, width : 2 * width].reshape(width, length),
+                big[:, :, n].reshape(length, part_cols), 1, 0,
+            ).astype(BF16)
+            v_g[k, :, :, :, :, pl.ds(pl.multiple_of(j * part_cols, part_cols), part_cols)] = made.reshape(
+                v_g.shape[1:5] + (part_cols,)
+            )
+            return 0
+
+        lax.fori_loop(0, 3, one, 0)
+
+    pair = 2 * HD
+    scale = 1.0 / math.sqrt(HD)
+    ticks = {
+        0: lambda: next(d_s[0]),
+        1: lambda: next(i_s[0]),
+        2: lambda: next(i_s[1]),
+        3: lambda: (project_grad(0), next(v_s[0]), next(d_s[0])),
+        4: lambda: (next(d_s[1]), next(o_s)),
+        5: lambda: next(v_s[0]),
+        6: lambda: next(i_s[0]),
+        7: lambda: (next(d_s[0], None), next(d_s[1])),
+    }
+
+    def attend_step(t, _):
+        p, half = t // 2, t % 2
+        n = pl.multiple_of(p * pair, pair)
+        r = pl.ds(pl.multiple_of(half * own_rows, own_rows), own_rows)
+        cq, ck, cv = pl.ds(n, pair), pl.ds(cols + n, pair), pl.ds(2 * cols + n, pair)
+        same = sc_ref[:, 0:1] == sr_ref[:, r]
+        queries = big[half, :, cq]
+        keys, values = big[:, :, ck].reshape(length, pair), big[:, :, cv].reshape(length, pair)
+        d_rows, o_rows = d_heads[half, :, cq], mine_ref[half, :, cq]
+        here = pl.ds(pl.multiple_of(y * cols + n, pair), pair)
+        d_q, d_k, d_v = [], [], []
+        for h in range(2):
+            k = slice(h * HD, h * HD + HD)
+            delta = jnp.sum((d_rows[:, k].astype(F32) * o_rows[:, k].astype(F32)).T, axis=0, keepdims=True)
+            scores = dg(keys[:, k], queries[:, k], 1, 1) * scale
+            prob = jnp.where(same, jnp.exp(scores - stats_ref[p, h : h + 1, r]), 0.0)
+            d_prob = dg(values[:, k], d_rows[:, k], 1, 1)
+            d_score = (prob * (d_prob - delta) * scale).astype(BF16)
+            d_v.append(dg(prob.astype(BF16), d_rows[:, k], 1, 0))
+            d_k.append(dg(d_score, queries[:, k], 1, 0))
+            d_q.append(dg(d_score, keys[:, k], 0, 0))
+        d_q, d_k, d_v = (jnp.concatenate(a, axis=1) for a in (d_q, d_k, d_v))
+        big[half, :, cq] = d_q.astype(BF16)
+        table[16:17, here] += jnp.sum(d_q, axis=0, keepdims=True)
+        table[17:18, here] += jnp.sum(d_v, axis=0, keepdims=True)
+
+        @pl.when(half == 0)
+        def _():
+            acc_k[...] = d_k
+            acc_v[...] = d_v
+
+        @pl.when(half == 1)
+        def _():
+            big[:, :, ck] = (acc_k[...] + d_k).astype(BF16).reshape(2, own_rows, pair)
+            big[:, :, cv] = (acc_v[...] + d_v).astype(BF16).reshape(2, own_rows, pair)
+
+        for k, tick in ticks.items():
+            pl.when(t == k)(lambda tick=tick: (tick(), None)[1])
+        return 0
+
+    lax.fori_loop(0, 2 * (cols // pair), attend_step, 0)
+    project_grad(1)
+    next(v_s[1])
+
+    step = 256
+    total = table[18:19]
+    for half in (at.ny, y):
+
+        def embed_grad(t, acc, half=half):
+            r = pl.ds(pl.multiple_of(t * step, step), step)
+            made = dg(
+                big[half, r, 0 : 3 * cols],
+                d_g[1, :, :, :, :, 0 : 3 * cols].reshape(width, 3 * cols), 1, 1,
+            )
+            i_g[0, 2 * half + t, :, :, :, 0:width] = made.astype(BF16).reshape(i_g.shape[2:5] + (width,))
+            return acc + jnp.sum(made, axis=0, keepdims=True)
+
+        total = lax.fori_loop(0, own_rows // step, embed_grad, total)
+        if half is y:
+            local.copy(i_g.at[0, pl.ds(2 * half, 2), :, :, :, 0:width], x_own)
+        else:
+            from_x = wire.send(i_g.at[0, pl.ds(2 * half, 2), :, :, :, 0:width], x_got, at.to_y)
+    down = lax.broadcasted_iota(jnp.int32, (16, width), 0)
+    table[0:16] = jnp.where(down == at.i, total, 0.0)
+    left = [tiny, i_s[1], v_s[1], o_s, v_s[0], i_s[0], d_s[1]]
+    for _ in range(7):
+        for one in left:
+            next(one, None)
+    from_x.wait_recv()
+    local.close()
     wire.close()
 
 
-def reduce_grads(v_g, o_g, i_g, d_g, x_part, small):
-    rows = v_g.shape[-2]
-    out = [jax.ShapeDtypeStruct((rows, a.shape[-1]), F32) for a in (v_g, o_g, i_g, d_g)]
-    scratch = [pltpu.VMEM((3,) + small.shape, F32), pltpu.VMEM((6,) + small.shape, F32)]
-    copies = 6 + 1
-    for a, parts in ((d_g, ALL_CUTS[2]), (i_g, ALL_CUTS[1]), (o_g, ALL_CUTS[0])):
-        n = a.shape[-1] // parts
+def backward(d_ffn, mid, d_attn, act, d_pre, d_mix, qkv, embed, v_all, far, mine, stats, seg_row, seg_col, small):
+    own_rows, width = mid.shape
+    hidden, cols, rows = act.shape[2], far.shape[1], v_all.shape[3]
+    dp3 = (4, 2, 2)
+    S = jax.ShapeDtypeStruct
+    x_part = S((2, 2, 2, rows, width), BF16)
+    outs = [
+        S((2, rows, 3 * cols // 2), F32), S((rows, cols), F32), S((rows, hidden), F32), S((rows, hidden), F32),
+        x_part, x_part, S(small.shape, F32),
+    ]
+    wide = S((2,) + dp3 + (rows, hidden), BF16)
+    acc = S((2 * own_rows, 2 * HD), F32)
+    scratch = [
+        S((own_rows, width), BF16), S((2, width, own_rows), BF16), S((2, own_rows, hidden), BF16),
+        S((2, own_rows, cols), BF16), wide, wide, S((2,) + dp3 + (rows, cols), BF16),
+        S((2,) + dp3 + (rows, 3 * cols // 2), BF16), acc, acc,
+        S(small.shape, F32), S((3,) + small.shape, F32), S((6,) + small.shape, F32),
+    ]
+    copies = 1 + 1 + 6
+    for n in [hidden // 2] * 4 + [cols]:
         h = n // 2
-        for _ in range(parts):
-            copies += 11
-            scratch += [
-                pltpu.VMEM(s, BF16)
-                for s in (
-                    (2, 4, 2, rows, n),
-                    (4, 2, rows, h),
-                    (2, 4, rows, h),
-                    (4, rows, h),
-                    (4, rows, h),
-                    (3, rows, n),
-                )
-            ]
-    n = v_g.shape[-1]
-    copies += 5
-    scratch += [pltpu.VMEM(s, BF16) for s in ((4, 2, rows, n), (4, rows, n), (3, rows, n))]
-    vm = pl.BlockSpec(memory_space=pltpu.VMEM)
-    hbm = pl.BlockSpec(memory_space=pl.ANY)
+        copies += 11
+        scratch += [
+            S(s, BF16)
+            for s in ((2, 4, 2, rows, n), (4, 2, rows, h), (2, 4, rows, h), (4, rows, h), (4, rows, h), (3, rows, n))
+        ]
+    for n in [3 * cols // 2] * 2:
+        copies += 5
+        scratch += [S(s, BF16) for s in ((4, 2, rows, n), (4, rows, n), (3, rows, n))]
+    vm, hbm = pl.BlockSpec(memory_space=pltpu.VMEM), pl.BlockSpec(memory_space=pl.ANY)
     return pl.pallas_call(
-        reduce_kernel,
-        name="reduce_grads",
-        out_shape=out
-        + [jax.ShapeDtypeStruct(x_part.shape[1:], x_part.dtype), jax.ShapeDtypeStruct(small.shape, F32)],
-        in_specs=[vm] * 4 + [hbm, vm],
-        out_specs=[vm] * 4 + [hbm, vm],
-        scratch_shapes=[pltpu.SemaphoreType.DMA((copies,)), pltpu.SemaphoreType.DMA((copies,))] + scratch,
+        backward_kernel,
+        name="backward",
+        out_shape=outs,
+        in_specs=[hbm] * 9 + [vm] * 6,
+        out_specs=[vm] * 4 + [hbm] * 2 + [vm],
+        scratch_shapes=[
+            pltpu.SemaphoreType.DMA((copies,)), pltpu.SemaphoreType.DMA((copies,)),
+            pltpu.SemaphoreType.DMA((BACKWARD_LOCAL,)),
+        ]
+        + [pltpu.VMEM(a.shape, a.dtype) for a in scratch],
         compiler_params=pltpu.CompilerParams(
-            collective_id=1, has_side_effects=True, vmem_limit_bytes=VMEM_LIMIT
+            collective_id=1, has_side_effects=True, vmem_limit_bytes=VMEM_ALL
         ),
-    )(v_g, o_g, i_g, d_g, x_part, small)
+    )(d_ffn, mid, d_attn, act, d_pre, d_mix, qkv, embed, v_all, far, mine, stats, seg_row, seg_col, small)
+
+
+BACKWARD_LOCAL = 12
 
 
 def attend_kernel(tile, q_ref, k_ref, v_ref, sr_ref, sc_ref, o_ref, l_ref):
@@ -748,8 +942,6 @@
         )
         few = few.reshape(dp, -1)
         inv_one = inv_one[:, :1]
-        own = jnp.arange(2)[:, None, None] == mp_index
-        mixed = jnp.where(own, mixed_heads, mixed_far[None])
     else:
         v_all = lax.all_gather(v_shard, "dp", axis=0)
         o_all, i_all, d_all = (
@@ -758,7 +950,7 @@
         )
         few = lax.all_gather(few_row, "dp", axis=0, tiled=True)
         time_w = lax.all_gather(time_weight, "dp", axis=0, tiled=True)
-    v_all = v_all.reshape(width, -1)
+    v_raw, v_all = v_all, v_all.reshape(width, -1)
     o_all, i_all, d_all = (a.reshape(mp, width, -1) for a in (o_all, i_all, d_all))
     qkv_w = v_all[:, : 3 * cols]
     column = mp_index * cols
@@ -791,16 +983,6 @@
         below = 0.5 + 0.5 * lax.erf(pre_act * math.sqrt(0.5))
         hidden_act = (pre_act * below).astype(BF16)
         slope = below + pre_act * jnp.exp(-0.5 * pre_act * pre_act) * (1.0 / math.sqrt(2.0 * math.pi))
-    embed_low = embed_low.reshape(length, width)
-    mixed_heads = mixed_heads.reshape(length, cols)
-
-    def rows_to_heads(cut):
-        if mp == 2:
-            far = lax.ppermute(
-                lax.dynamic_index_in_dim(cut, 1 - mp_index, 0, False), "mp", [(0, 1), (1, 0)]
-            )
-            return jnp.where(own, cut, far[None]).reshape(length, cols)
-        return lax.all_to_all(cut, "mp", 0, 0, tiled=True).reshape(length, cols)
 
     ffn_total = ein("yrf,ynf->rn", hidden_act, d_all)
     unit_two, inv_two = normalize(middle + ffn_total + bias_all[5])
@@ -812,62 +994,48 @@
     d_pre_two = norm_back(grad_out, unit_two, inv_two, gain_all[1])
     bias_five_part = jnp.sum(d_pre_two, axis=0)
     d_ffn = d_pre_two.astype(BF16)
-    down_grad = ein("rn,yrf->ynf", d_ffn, hidden_act).astype(BF16)
     d_act = ein("rn,ynf->yrf", d_ffn, d_all)
     d_pre_act = d_act * slope.astype(F32)
     ffn_bias_part = jnp.sum(d_pre_act, axis=1).reshape(-1, width)
     d_pre_low = d_pre_act.astype(BF16)
-    in_grad = ein("rd,yrf->ydf", middle_low, d_pre_low).astype(BF16)
     d_middle = d_pre_two + ein("yrf,ydf->rd", d_pre_low, i_all)
     gain_one_part = jnp.sum(d_middle * unit_one, axis=0)
     shift_one_part = jnp.sum(d_middle, axis=0)
     d_pre_one = norm_back(d_middle, unit_one, inv_one, gain_all[0])
     bias_three_part = jnp.sum(d_pre_one, axis=0)
     d_attn = d_pre_one.astype(BF16)
-    out_grad_t = ein("rn,yrk->ynk", d_attn, mixed).astype(BF16)
-    d_mixed = rows_to_heads(ein("rn,ynk->yrk", d_attn, o_all).astype(BF16))
-    d_q, d_k, d_v = attend_back(qkv, d_mixed, mixed_heads, stats, segments)
-    d_qkv = jnp.concatenate([d_q, d_k, d_v], axis=1).astype(BF16)
-    v_grad = dg(embed_low, d_qkv, 0, 0).astype(BF16)
-    d_embed = dg(d_qkv, qkv_w, 1, 1)
-    time_part = bias_three_part + jnp.sum(d_embed, axis=0)
-    d_embed = d_embed.astype(BF16).reshape(mp, own_rows, width)
-
+    d_mix = ein("rn,ynk->yrk", d_attn, o_all).astype(BF16)
     zero_row = jnp.zeros((width,), F32)
-    seq_rows = jnp.where(jnp.arange(dp)[:, None] == dp_index, time_part[None, :], 0.0)
-    small = jnp.concatenate(
-        [
-            seq_rows,
-            jnp.stack(
-                [
-                    lax.dynamic_update_slice_in_dim(zero_row, jnp.sum(d_q, axis=0), column, 0),
-                    lax.dynamic_update_slice_in_dim(zero_row, jnp.sum(d_v, axis=0), column, 0),
-                    bias_three_part,
-                    shift_one_part,
-                    bias_five_part,
-                    shift_two_part,
-                    gain_one_part,
-                    gain_two_part,
-                ]
-            ),
-            ffn_bias_part,
-        ],
-        axis=0,
-    )
-    small = jnp.pad(small, ((0, -small.shape[0] % 8), (0, 0)))
+    sums = [bias_three_part, shift_one_part, bias_five_part, shift_two_part, gain_one_part, gain_two_part]
+
+    def pad_rows(a):
+        return jnp.pad(a, ((0, -a.shape[0] % 8), (0, 0)))
 
     if fast:
-        shape = (2, 4, 2, 2, rows, -1)
-        v_sum, o_sum, i_sum, d_sum, d_far, small = reduce_grads(
-            v_grad.reshape(shape[1:]),
-            out_grad_t.reshape(shape),
-            in_grad.reshape(shape),
-            down_grad.reshape(shape),
-            d_embed,
-            small,
+        small = jnp.concatenate([jnp.zeros((dp + 2, width), F32), jnp.stack(sums), ffn_bias_part], axis=0)
+        v_sum, o_sum, i_sum, d_sum, d_near, d_far, small = backward(
+            d_ffn, middle_low, d_attn, hidden_act, d_pre_low, d_mix, qkv.reshape(mp, own_rows, -1),
+            embed_low.reshape(v_raw.shape[:4] + (width,)), v_raw, mixed_far, mixed_heads, stats, segments, seg_col,
+            pad_rows(small),
         )
-        d_own = lax.dynamic_index_in_dim(d_embed, mp_index, 0, False).astype(F32) + d_far.astype(F32)
+        d_own = (d_near.astype(F32) + d_far.astype(F32)).reshape(own_rows, width)
+        qkv_grad = v_sum.reshape(2, rows, 3, -1).transpose(2, 1, 0, 3).reshape(3, rows, cols)
     else:
+        embed_low = embed_low.reshape(length, width)
+        mixed_heads = mixed_heads.reshape(length, cols)
+        down_grad = ein("rn,yrf->ynf", d_ffn, hidden_act).astype(BF16)
+        in_grad = ein("rd,yrf->ydf", middle_low, d_pre_low).astype(BF16)
+        out_grad_t = ein("rn,yrk->ynk", d_attn, mixed).astype(BF16)
+        d_mixed = lax.all_to_all(d_mix, "mp", 0, 0, tiled=True).reshape(length, cols)
+        d_q, d_k, d_v = attend_back(qkv, d_mixed, mixed_heads, stats, segments)
+        d_qkv = jnp.concatenate([d_q, d_k, d_v], axis=1).astype(BF16)
+        v_grad = dg(embed_low, d_qkv, 0, 0).astype(BF16)
+        d_embed = dg(d_qkv, qkv_w, 1, 1)
+        time_part = bias_three_part + jnp.sum(d_embed, axis=0)
+        d_embed = d_embed.astype(BF16).reshape(mp, own_rows, width)
+        seq_rows = jnp.where(jnp.arange(dp)[:, None] == dp_index, time_part[None, :], 0.0)
+        spread = [lax.dynamic_update_slice_in_dim(zero_row, jnp.sum(a, axis=0), column, 0) for a in (d_q, d_v)]
+        small = pad_rows(jnp.concatenate([seq_rows, jnp.stack(spread + sums), ffn_bias_part], axis=0))
         v_sum = lax.psum_scatter(v_grad, "dp", scatter_dimension=0, tiled=True).astype(F32)
 
         def both(a):
@@ -877,6 +1045,7 @@
         o_sum, i_sum, d_sum = both(out_grad_t), both(in_grad), both(down_grad)
         d_own = lax.psum_scatter(d_embed, "mp", scatter_dimension=0).astype(F32)
         small = lax.psum(small, ("dp", "mp"))
+        qkv_grad = v_sum.reshape(rows, 3, cols).transpose(1, 0, 2)
 
     input_grad = d_pre_one + d_own
     d_time = small[:dp]
@@ -893,7 +1062,6 @@
     ffn_rows = ffn_bias.shape[0]
     ffn_all = tail[8:].reshape(-1)
     ffn_bias_grad = lax.dynamic_slice_in_dim(ffn_all, dp_index * ffn_rows, ffn_rows)
-    qkv_grad = v_sum.reshape(rows, 3, cols).transpose(1, 0, 2)
     return (
         layer_out,
         input_grad,

time: 455 us -> 379 us (0.83)
  matrix products: 65.6 us -> 29.4 us
  Pallas kernels: 336 us -> 312 us
  local copies, waits for them, and re-layouts: 26.9 us -> 19.3 us
  other arithmetic: 17.2 us -> 11.4 us
    dot_general x7 -> x4, matrix products: 53.5 us -> 27.5 us  [ein(): return jnp.einsum(spec, left, right, preferred_element_type=F32)]
    pallas_call x2 -> x1, Pallas kernels: 180 us -> 155 us  [backward(): pl.pallas_call(backward_kernel, name='backward', out_shape=outs, in_specs...]
    dot_general x2 -> x0, matrix products: 10.2 us -> none  [dg(): lax.dot_general(left, right, (((left_dim,), (right_dim,)), ((), ())), pre...]
    unnamed x45 -> x40, local copies, waits for them, and re-layouts: 9.74 us -> 7.82 us
  transfers between devices with their start and end apart: 1 -> 0, of which waited for: 0 -> 0; matrix products, arithmetic and copies ran while one was open for 6% -> 0% of each run, Pallas kernels for 0% -> 0%
where the time goes in v3:
time: 379 us; the launch traced here: 374 us
  Pallas kernels  312 us (82%)
  matrix products  29.4 us (8%)
  local copies, waits for them, and re-layouts  19.3 us (5%)
  other arithmetic  11.4 us (3%)
    pallas_call x1, Pallas kernels, forward(): pl.pallas_call(forward_kernel, name='forward', out_shape=outs, in_specs=[...  157 us
    pallas_call x1, Pallas kernels, backward(): pl.pallas_call(backward_kernel, name='backward', out_shape=outs, in_specs...  155 us
    dot_general x4, matrix products, ein(): return jnp.einsum(spec, left, right, preferred_element_type=F32)  27.5 us
    unnamed x40, local copies, waits for them, and re-layouts  7.82 us

profile of v3, /device:TPU:20, one launch (start us, length us, event | category | flops | bytes accessed | tf_op | source)
XLA Modules:
  0.0 373.6 jit_solution(5127536741516590295)
XLA Ops:
  1.3 1.2 slice.61.b_ref
  2.5 0.7 broadcast_in_dim.14
  3.8 0.8 copy.32
  4.6 0.8 copy.31
  5.4 0.9 slice_bitcast_fusion
  6.3 0.8 concatenate.29.v_ref
  7.1 1.7 broadcast_in_dim.31.sc_ref
  8.8 156.6 %forward.1 = (bf16[4,2,2,64,1664]{4,3,2,1,0:T(8,128)(2,1)}, bf16[2,4,2,2,64,512]{5,4,3,2,1,0:T(8,128)(2,1)}, bf16[2,4,2,2,64,2048]{5,4,3,2,1,0:T(8,128)(2,1)}, b...) custom-call(bf16[64,1664]{1,0:T(8,128)(2,1)} %concatenate.29.v_ref, ...), custom_call_target="tpu_custom_call" | custom-call | tf_op jit(solution)/shard_map/forward/pallas_call | solution.py:413
  165.3 0.9 fusion.22
  166.3 1.1 slice_reduce_fusion
  167.4 0.9 copy.42
  168.9 9.8 %fusion.23 = (f32[512]{0:T(512)S(1)}, f32[512,1024]{1,0:T(8,128)S(1)}) fusion(f32[1024]{0:T(1024)S(1)} %bitcast.95, bf16[2,512,2048]{2,1,0:T(8,128)(2,1)} %get-tuple-element.35.act_ref, bf16[2,1024,2048]{2,1,0:T(8,128)(2,1)} %bitcast.100, f32[1024]{0:T(1024)S(1)} %bitcast.96, f32[512,1024]{1,0:T(8,128)} %get-tuple-element.33, f32[1024]{0:T(1024)S(1)} %bitcast.87), kind=kOutput, calls=%fused_computation.59 | convolution fusion | flops 4297588224 | bytes 16791552 | tf_op jit(solution)/shard_map/yrf,ynf->rn/dot_general | solution.py:899
  179.1 0.9 copy-done.5
  180.0 1.0 fusion.8
  181.0 1.8 fusion.19
  183.5 9.1 %fusion = (f32[2,2048]{1,0:T(2,128)S(1)}, bf16[2,512,2048]{2,1,0:T(8,128)(2,1)S(1)}) fusion(bf16[2,512,2048]{2,1,0:T(8,128)(2,1)S(1)} %copy-done.12, bf16[2,1024,2048]{2,1,0:T(8,128)(2,1)} %bitcast.101, bf16[512,1024]{1,0:T(8,128)(2,1)S(1)} %convert_element_type.56.ffn_ref), kind=kOutput, calls=%fused_computation.1 | convolution fusion | flops 4303351808 | bytes 17842176 | tf_op jit(solution)/shard_map/rn,ynf->yrf/dot_general | solution.py:899
  192.7 6.3 %multiply_reduce_fusion = (f32[1024]{0:T(1024)S(1)}, f32[512]{0:T(512)S(1)}, f32[512]{0:T(512)S(1)}, f32[1024]{0:T(1024)S(1)}, f32[512,1024]{1,0:T(8,128)}) fusion(f32[512,1024]{1,0:T(8,128)S(1)} %copy-done.6, f32[1024]{0:T(1024)S(1)} %bitcast.88, f32[512,1024]{1,0:T(8,128)S(1)} %get-tuple-element.65, ...), kind=kOutput, calls=%fused_computation.18 | convolution fusion | flops 4299158528 | bytes 18890752 | tf_op jit(solution)/shard_map/yrf,ydf->rd/dot_general | solution.py:899
  199.0 2.7 fusion.21
  201.9 0.7 pad.4.small_ref
  203.3 1.0 copy-done.4
  204.3 2.3 fusion.10.mix_ref
  206.5 155.3 %backward.1 = (f32[2,64,768]{2,1,0:T(8,128)}, f32[64,512]{1,0:T(8,128)}, f32[64,2048]{1,0:T(8,128)}, f32[64,2048]{1,0:T(8,128)}, bf16[2,2,2,64,1024]{4,3,2,1,0:T...) custom-call(bf16[512,1024]{1,0:T(8,128)(2,1)} %copy-done.3, ...), custom_call_target="tpu_custom_call" | custom-call | tf_op jit(solution)/shard_map/backward/pallas_call | solution.py:755
  361.9 2.1 convert_add_fusion
  364.1 1.7 bitcast_add_fusion
  365.9 0.6 constant_dynamic-slice_fusion
  366.5 0.6 dynamic_slice.15
  367.1 0.7 fusion.17
  367.8 1.9 fusion.14
  370.3 1.1 reshape.132
  371.4 0.7 copy.48
  372.0 0.8 copy.49
  372.8 0.8 copy.50
  (56 shorter events, 3.9 us)
Async XLA Ops:
  178.7 1.2 copy-start.5
  181.0 2.6 copy-start.12
  182.8 9.8 %slice-start = ((s8[8388608]{0:T(1024)(128)(4,1)}), s8[4194304]{0:T(1024)(128)(4,1)S(1)}, s32[]{:S(2)}) async-start(s8[8388608]{0:T(1024)(128)(4,1)} %bitcast.97), calls=%async_computation | async-start | bytes 8388608
  183.5 9.1 %copy-start.3 = (bf16[512,1024]{1,0:T(8,128)(2,1)}, bf16[512,1024]{1,0:T(8,128)(2,1)S(1)}, u32[]{:S(2)}) copy-start(bf16[512,1024]{1,0:T(8,128)(2,1)S(1)} %convert_element_type.56.ffn_ref) | copy-start | bytes 3145732
  183.5 9.1 %copy-start.6 = (f32[512,1024]{1,0:T(8,128)S(1)}, f32[512,1024]{1,0:T(8,128)}, u32[]{:S(2)}) copy-start(f32[512,1024]{1,0:T(8,128)} %get-tuple-element.33) | copy-start | bytes 6291460
  183.5 9.1 %slice-start.1 = ((s8[8388608]{0:T(1024)(128)(4,1)}), s8[4194304]{0:T(1024)(128)(4,1)S(1)}, s32[]{:S(2)}) async-start(s8[8388608]{0:T(1024)(128)(4,1)} %bitcast.97), calls=%async_computation.1 | async-start | bytes 8388608
  192.7 6.3 %copy-start.2 = (bf16[2,512,2048]{2,1,0:T(8,128)(2,1)}, bf16[2,512,2048]{2,1,0:T(8,128)(2,1)S(1)}, u32[]{:S(2)}) copy-start(bf16[2,512,2048]{2,1,0:T(8,128)(2,1)S(1)} %get-tuple-element.69.pre_ref) | copy-start | bytes 12582916
  201.8 1.4 copy-start
  201.9 2.4 copy-start.13
  203.3 1.0 copy-start.4
  361.8 2.2 copy-start.1
  364.1 1.7 copy-start.10
  364.1 5.7 %copy-start.9 = (f32[2,64,768]{2,1,0:T(8,128)S(1)}, f32[2,64,768]{2,1,0:T(8,128)}, u32[]{:S(2)}) copy-start(f32[2,64,768]{2,1,0:T(8,128)} %get-tuple-element.52) | copy-start | bytes 1179652
  365.8 5.5 %copy-start.11 = (f32[64,512]{1,0:T(8,128)S(1)}, f32[64,512]{1,0:T(8,128)}, u32[]{:S(2)}) copy-start(f32[64,512]{1,0:T(8,128)} %get-tuple-element.53) | copy-start | bytes 393220
  365.8 6.2 %copy-start.8 = (f32[64,2048]{1,0:T(8,128)S(1)}, f32[64,2048]{1,0:T(8,128)}, u32[]{:S(2)}) copy-start(f32[64,2048]{1,0:T(8,128)} %get-tuple-element.99) | copy-start | bytes 1572868
  367.8 5.0 %copy-start.7 = (f32[64,2048]{1,0:T(8,128)S(1)}, f32[64,2048]{1,0:T(8,128)}, u32[]{:S(2)}) copy-start(f32[64,2048]{1,0:T(8,128)} %get-tuple-element.55) | copy-start | bytes 1572868

commit v4 on v3

--- a/solution.py
+++ b/solution.py
@@ -100,9 +100,9 @@
             one.wait()
 
 
-def parts_of(width, parts):
+def parts_of(width, parts, first=0.5):
     step = width // parts
-    return [(p * step, p * step + step // 2, (p + 1) * step) for p in range(parts)]
+    return [(p * step, p * step + int(step * first), (p + 1) * step) for p in range(parts)]
 
 
 def stagger(streams, ahead=0):
@@ -137,33 +137,40 @@
 def gather_all(wire, at, shard, whole, lo, mid, hi):
     a, b, ab = pl.ds(lo, mid - lo), pl.ds(mid, hi - mid), pl.ds(lo, hi - lo)
     y, z, x, c = at.y, at.z, at.x, at.c
-    own = whole.at[y, z, x, c, :, ab]
-    from_z = [wire.send(shard.at[:, ab], own, to) for to in at.to_z]
-    late = [wire.send(shard.at[:, ab], own, at.to_c)]
-    yield
-    for k in from_z:
+    from_z_a = [wire.send(shard.at[:, a], whole.at[y, z, x, c, :, a], to) for to in at.to_z]
+    from_y_b = wire.send(shard.at[:, b], whole.at[y, z, x, c, :, b], at.to_y)
+    late = [wire.send(shard.at[:, ab], whole.at[y, z, x, c, :, ab], at.to_c)]
+
+    def to_core(*refs):
+        for ref in refs:
+            late.append(wire.send(ref, ref, at.to_c))
+
+    yield
+    from_y_b.wait_recv()
+    ref = whole.at[:, z, x, c, :, b]
+    from_z_b = [wire.send(ref, ref, to) for to in at.to_z]
+    to_core(whole.at[at.ny, z, x, c, :, b])
+    yield
+    for k in from_z_a:
         k.wait_recv()
     ref = whole.at[y, :, x, c, :, a]
     from_x_a = wire.send(ref, ref, at.to_x)
-    ref = whole.at[y, :, x, c, :, b]
-    from_y_b = wire.send(ref, ref, at.to_y)
-    for p in at.zs:
-        ref = whole.at[y, p, x, c, :, ab]
-        late.append(wire.send(ref, ref, at.to_c))
+    to_core(*(whole.at[y, p, x, c, :, a] for p in at.zs))
     yield
     from_x_a.wait_recv()
     ref = whole.at[y, :, :, c, :, a]
     from_y_a = wire.send(ref, ref, at.to_y)
-    from_y_b.wait_recv()
+    to_core(whole.at[y, :, at.nx, c, :, a])
+    yield
+    for k in from_z_b:
+        k.wait_recv()
     ref = whole.at[:, :, x, c, :, b]
     from_x_b = wire.send(ref, ref, at.to_x)
-    for ref in (whole.at[y, :, at.nx, c, :, a], whole.at[at.ny, :, x, c, :, b]):
-        late.append(wire.send(ref, ref, at.to_c))
+    to_core(*(whole.at[:, p, x, c, :, b] for p in at.zs))
     yield
     from_y_a.wait_recv()
     from_x_b.wait_recv()
-    for ref in (whole.at[at.ny, :, :, c, :, a], whole.at[:, :, at.nx, c, :, b]):
-        late.append(wire.send(ref, ref, at.to_c))
+    to_core(whole.at[at.ny, :, :, c, :, a], whole.at[:, :, at.nx, c, :, b])
     yield
     for k in late:
         k.wait_recv()
@@ -199,15 +206,18 @@
     v0 = gather_dp(wire, at, v_ref, v_all, 0, v_mid)
     v1 = gather_dp(wire, at, v_ref, v_all, v_mid, v_ref.shape[1])
     out_w = gather_all(wire, at, o_ref, o_all, *parts_of(cols, 1)[0])
-    in_w = [gather_all(wire, at, i_ref, i_all, *cut) for cut in parts_of(hidden, 2)]
-    down_w = [gather_all(wire, at, d_ref, d_all, *cut) for cut in parts_of(hidden, 2)]
-    next(v0)
+    in_w = [gather_all(wire, at, i_ref, i_all, *cut) for cut in parts_of(hidden, 2, 0.625)]
+    down_w = [gather_all(wire, at, d_ref, d_all, *cut) for cut in parts_of(hidden, 2, 0.625)]
     kept = [
         local.copy(v_ref, v_all.at[z, x, c]),
         local.copy(o_ref, o_all.at[y, z, x, c]),
         local.copy(i_ref, i_all.at[y, z, x, c]),
         local.copy(d_ref, d_all.at[y, z, x, c]),
     ]
+    next(v0)
+    next(v1)
+    next(out_w)
+    next(in_w[0])
     few[at.i] = f_ref[...]
     for k in from_few:
         k.wait_recv()
@@ -221,23 +231,26 @@
     ffn_b[...] = jnp.concatenate([few[s][:, width:] for s in range(seqs)], axis=1)
     local.copy(few, few_out)
     from_part = [wire.send(part.at[p], got.at[j], (p, y)) for j, p in enumerate(at.dp)]
-    next(v1)
-    next(out_w)
-    next(in_w[0])
     for k in kept:
         k.wait()
         local.open.remove(k)
     next(v0)
     next(v1)
+    next(out_w)
     next(in_w[1])
     next(down_w[0])
-    next(down_w[1])
+    next(v0)
+    next(out_w)
     for k in from_part:
         k.wait_recv()
     total = part[at.i]
     for j in range(seqs - 1):
         total = total + got[j]
     time_out[...] = total
+    next(in_w[0])
+    next(v1)
+    next(in_w[0])
+    next(v0, None)
 
     from_h.wait_recv()
     step = 128
@@ -250,12 +263,10 @@
 
     lax.fori_loop(0, own_rows // step, embed_rows, 0)
     local.copy(embed, embed_out)
-    next(v0)
+    next(v1, None)
+    next(in_w[1])
     next(out_w)
-    next(v1)
-    next(in_w[0])
-    next(v0, None)
-    next(v1, None)
+    next(down_w[1])
     local.copy(v_all, v_out)
     par[...] = v_all[:, :, :, :, 3 * cols :].reshape(width, 128).astype(F32).T
     local.copy(par, par_out)
@@ -276,8 +287,8 @@
 
     lax.fori_loop(0, length // step_q, project, 0)
     local.copy(qkv, qkv_out)
+    next(in_w[0])
     next(out_w)
-    next(in_w[1])
 
     pair, tile = 2 * HD, own_rows
     from_far = []
@@ -287,14 +298,11 @@
         from_far.append(wire.send(mine.at[at.ny, :, n], far.at[:, n], at.to_y))
 
     ticks = {
-        0: lambda: next(in_w[0]),
-        1: lambda: (give(0), next(out_w)),
-        2: lambda: next(down_w[0]),
-        3: lambda: (give(1), next(in_w[0])),
-        4: lambda: next(in_w[1]),
-        5: lambda: (give(2), next(down_w[1])),
-        6: lambda: next(down_w[0]),
-        7: lambda: (give(3), next(out_w, None), next(in_w[0], None)),
+        1: lambda: (give(0), next(down_w[0]), next(down_w[1]), next(in_w[1]),),
+        3: lambda: (give(1), next(in_w[1]), next(down_w[0]), next(in_w[0]),),
+        5: lambda: (give(2),),
+        6: lambda: (next(in_w[1]), next(out_w),),
+        7: lambda: (give(3), next(in_w[0]), next(down_w[0]), next(out_w, None), next(in_w[1]), next(down_w[1]), next(in_w[0], None), next(down_w[0]),),
     }
 
     def attend_step(t, _):
@@ -345,14 +353,14 @@
     local.copy(inv, inv_out)
     local.copy(mid, mid_out)
 
+
     chunk = 512
     per = hidden // 2 // chunk
     later = {
-        0: lambda: next(in_w[1]),
-        1: lambda: next(down_w[1]),
-        3: lambda: next(in_w[1], None),
-        4: lambda: next(down_w[0]),
-        6: lambda: next(down_w[1]),
+        0: lambda: (next(down_w[1]),),
+        2: lambda: (next(in_w[1], None), next(down_w[1]),),
+        4: lambda: (next(down_w[0]),),
+        6: lambda: (next(down_w[1]),),
     }
 
     def feed_step(t, _):
@@ -409,7 +417,7 @@
     part, got = S((16, 1, width), F32), S((15, 1, width), F32)
     h_far, ffn_b = S(h.shape, BF16), S((1, 2 * hidden), F32)
     scratch = [v_all, o_all, i_all, few, part, got, h_far, par, ffn_b, embed, qkv, mine, far, stats, unit, inv, mid, act, act]
-    copies = 15 + 15 + 1 + 2 * 9 + 5 * 15 + pairs
+    copies = 15 + 15 + 1 + 2 * 9 + 5 * 21 + pairs
     return pl.pallas_call(
         forward_kernel,
         name="forward",

time: 379 us -> 351 us (0.926); the launches traced: 374 us -> 350 us
  Pallas kernels: 312 us -> 289 us
    pallas_call x1, Pallas kernels: 157 us -> 135 us  [forward(): pl.pallas_call(forward_kernel, name='forward', out_shape=outs, in_specs=[...]
where the time goes in v4:
time: 351 us; the launch traced here: 350 us
  Pallas kernels  289 us (82%)
  matrix products  29.4 us (8%)
  local copies, waits for them, and re-layouts  19.3 us (5%)
  other arithmetic  11.4 us (3%)
    pallas_call x1, Pallas kernels, backward(): pl.pallas_call(backward_kernel, name='backward', out_shape=outs, in_specs...  154 us
    pallas_call x1, Pallas kernels, forward(): pl.pallas_call(forward_kernel, name='forward', out_shape=outs, in_specs=[...  135 us
    dot_general x4, matrix products, ein(): return jnp.einsum(spec, left, right, preferred_element_type=F32)  27.5 us
    unnamed x40, local copies, waits for them, and re-layouts  7.82 us

profile of v4, /device:TPU:20, one launch (start us, length us, event | category | flops | bytes accessed | tf_op | source)
XLA Modules:
  0.0 350.5 jit_solution(9985216455670323796)
XLA Ops:
  1.3 1.2 slice.61.b_ref
  2.5 0.7 broadcast_in_dim.14
  3.8 0.8 copy.32
  4.6 0.8 copy.31
  5.4 0.9 slice_bitcast_fusion
  6.3 0.8 concatenate.29.v_ref
  7.1 1.7 broadcast_in_dim.31.sc_ref
  8.8 134.7 %forward.1 = (bf16[4,2,2,64,1664]{4,3,2,1,0:T(8,128)(2,1)}, bf16[2,4,2,2,64,512]{5,4,3,2,1,0:T(8,128)(2,1)}, bf16[2,4,2,2,64,2048]{5,4,3,2,1,0:T(8,128)(2,1)}, b...) custom-call(bf16[64,1664]{1,0:T(8,128)(2,1)} %concatenate.29.v_ref, ...), custom_call_target="tpu_custom_call" | custom-call | tf_op jit(solution)/shard_map/forward/pallas_call | solution.py:421
  143.5 0.9 fusion.22
  144.4 1.1 slice_reduce_fusion
  145.5 0.9 copy.42
  147.1 9.8 %fusion.23 = (f32[512]{0:T(512)S(1)}, f32[512,1024]{1,0:T(8,128)S(1)}) fusion(f32[1024]{0:T(1024)S(1)} %bitcast.95, bf16[2,512,2048]{2,1,0:T(8,128)(2,1)} %get-tuple-element.35.act_ref, bf16[2,1024,2048]{2,1,0:T(8,128)(2,1)} %bitcast.100, f32[1024]{0:T(1024)S(1)} %bitcast.96, f32[512,1024]{1,0:T(8,128)} %get-tuple-element.33, f32[1024]{0:T(1024)S(1)} %bitcast.87), kind=kOutput, calls=%fused_computation.59 | convolution fusion | flops 4297588224 | bytes 16791552 | tf_op jit(solution)/shard_map/yrf,ynf->rn/dot_general | solution.py:907
  157.3 0.9 copy-done.5
  158.1 1.0 fusion.8
  159.1 1.8 fusion.19
  161.7 9.1 %fusion = (f32[2,2048]{1,0:T(2,128)S(1)}, bf16[2,512,2048]{2,1,0:T(8,128)(2,1)S(1)}) fusion(bf16[2,512,2048]{2,1,0:T(8,128)(2,1)S(1)} %copy-done.12, bf16[2,1024,2048]{2,1,0:T(8,128)(2,1)} %bitcast.101, bf16[512,1024]{1,0:T(8,128)(2,1)S(1)} %convert_element_type.56.ffn_ref), kind=kOutput, calls=%fused_computation.1 | convolution fusion | flops 4303351808 | bytes 17842176 | tf_op jit(solution)/shard_map/rn,ynf->yrf/dot_general | solution.py:907
  170.9 6.3 %multiply_reduce_fusion = (f32[1024]{0:T(1024)S(1)}, f32[512]{0:T(512)S(1)}, f32[512]{0:T(512)S(1)}, f32[1024]{0:T(1024)S(1)}, f32[512,1024]{1,0:T(8,128)}) fusion(f32[512,1024]{1,0:T(8,128)S(1)} %copy-done.6, f32[1024]{0:T(1024)S(1)} %bitcast.88, f32[512,1024]{1,0:T(8,128)S(1)} %get-tuple-element.65, ...), kind=kOutput, calls=%fused_computation.18 | convolution fusion | flops 4299158528 | bytes 18890752 | tf_op jit(solution)/shard_map/yrf,ydf->rd/dot_general | solution.py:907
  177.2 2.7 fusion.21
  180.1 0.7 pad.4.small_ref
  181.5 1.0 copy-done.4
  182.4 2.3 fusion.10.mix_ref
  184.7 154.0 %backward.1 = (f32[2,64,768]{2,1,0:T(8,128)}, f32[64,512]{1,0:T(8,128)}, f32[64,2048]{1,0:T(8,128)}, f32[64,2048]{1,0:T(8,128)}, bf16[2,2,2,64,1024]{4,3,2,1,0:T...) custom-call(bf16[512,1024]{1,0:T(8,128)(2,1)} %copy-done.3, ...), custom_call_target="tpu_custom_call" | custom-call | tf_op jit(solution)/shard_map/backward/pallas_call | solution.py:763
  338.7 2.1 convert_add_fusion
  340.9 1.7 bitcast_add_fusion
  342.7 0.6 constant_dynamic-slice_fusion
  343.4 0.6 dynamic_slice.15
  344.0 0.7 fusion.17
  344.7 1.9 fusion.14
  347.2 1.1 reshape.132
  348.2 0.7 copy.48
  348.9 0.8 copy.49
  349.7 0.8 copy.50
  (56 shorter events, 3.9 us)
Async XLA Ops:
  156.9 1.2 copy-start.5
  159.1 2.6 copy-start.12
  161.0 9.8 %slice-start = ((s8[8388608]{0:T(1024)(128)(4,1)}), s8[4194304]{0:T(1024)(128)(4,1)S(1)}, s32[]{:S(2)}) async-start(s8[8388608]{0:T(1024)(128)(4,1)} %bitcast.97), calls=%async_computation | async-start | bytes 8388608
  161.7 9.1 %copy-start.3 = (bf16[512,1024]{1,0:T(8,128)(2,1)}, bf16[512,1024]{1,0:T(8,128)(2,1)S(1)}, u32[]{:S(2)}) copy-start(bf16[512,1024]{1,0:T(8,128)(2,1)S(1)} %convert_element_type.56.ffn_ref) | copy-start | bytes 3145732
  161.7 9.1 %copy-start.6 = (f32[512,1024]{1,0:T(8,128)S(1)}, f32[512,1024]{1,0:T(8,128)}, u32[]{:S(2)}) copy-start(f32[512,1024]{1,0:T(8,128)} %get-tuple-element.33) | copy-start | bytes 6291460
  161.7 9.1 %slice-start.1 = ((s8[8388608]{0:T(1024)(128)(4,1)}), s8[4194304]{0:T(1024)(128)(4,1)S(1)}, s32[]{:S(2)}) async-start(s8[8388608]{0:T(1024)(128)(4,1)} %bitcast.97), calls=%async_computation.1 | async-start | bytes 8388608
  170.8 6.3 %copy-start.2 = (bf16[2,512,2048]{2,1,0:T(8,128)(2,1)}, bf16[2,512,2048]{2,1,0:T(8,128)(2,1)S(1)}, u32[]{:S(2)}) copy-start(bf16[2,512,2048]{2,1,0:T(8,128)(2,1)S(1)} %get-tuple-element.69.pre_ref) | copy-start | bytes 12582916
  179.9 1.4 copy-start
  180.0 2.4 copy-start.13
  181.5 1.0 copy-start.4
  338.7 2.2 copy-start.1
  340.9 1.7 copy-start.10
  340.9 5.7 %copy-start.9 = (f32[2,64,768]{2,1,0:T(8,128)S(1)}, f32[2,64,768]{2,1,0:T(8,128)}, u32[]{:S(2)}) copy-start(f32[2,64,768]{2,1,0:T(8,128)} %get-tuple-element.52) | copy-start | bytes 1179652
  342.7 5.5 %copy-start.11 = (f32[64,512]{1,0:T(8,128)S(1)}, f32[64,512]{1,0:T(8,128)}, u32[]{:S(2)}) copy-start(f32[64,512]{1,0:T(8,128)} %get-tuple-element.53) | copy-start | bytes 393220
  342.7 6.2 %copy-start.8 = (f32[64,2048]{1,0:T(8,128)S(1)}, f32[64,2048]{1,0:T(8,128)}, u32[]{:S(2)}) copy-start(f32[64,2048]{1,0:T(8,128)} %get-tuple-element.99) | copy-start | bytes 1572868
  344.7 5.0 %copy-start.7 = (f32[64,2048]{1,0:T(8,128)S(1)}, f32[64,2048]{1,0:T(8,128)}, u32[]{:S(2)}) copy-start(f32[64,2048]{1,0:T(8,128)} %get-tuple-element.55) | copy-start | bytes 1572868

commit v5 on v4

--- a/solution.py
+++ b/solution.py
@@ -472,10 +472,18 @@
     out[...] = ((rx[z].astype(F32) + rz[0].astype(F32)) + rz[1].astype(F32)) + rz[2].astype(F32)
 
 
-def reduce_all(wire, at, grad, rc, ya, xb, xa, yb, rz, out, lo, mid, hi):
+def reduce_all(wire, at, grad, bufs, out, lo, mid, hi, early):
+    rc, ya, xb, xa, za, zb, yb, zs = bufs
     z, x, c, y = at.z, at.x, at.c, at.y
     a, b, ab = pl.ds(lo, mid - lo), pl.ds(mid, hi - mid), pl.ds(lo, hi - lo)
     half_a, half_b = pl.ds(0, mid - lo), pl.ds(mid - lo, hi - mid)
+
+    def over_z(pick, got):
+        return [wire.send(pick(p), got.at[at.count[j]], to) for j, (p, to) in enumerate(zip(at.zs, at.to_z))]
+
+    def add_z(own, got):
+        return ((own.astype(F32) + got[0].astype(F32)) + got[1].astype(F32)) + got[2].astype(F32)
+
     from_c = wire.send(grad.at[:, :, :, at.nc, :, ab], rc, at.to_c)
     yield
     wire.both(from_c)
@@ -486,25 +494,44 @@
     from_y_a.wait_recv()
     add_blocks(ya, rc.at[y, :, :, :, half_a], ya, (4, 2))
     from_x_a = wire.send(ya.at[:, at.nx], xa, at.to_x)
+    yield
     from_x_b.wait_recv()
     add_blocks(xb, rc.at[:, :, x, :, half_b], xb, (2, 4))
-    from_y_b = wire.send(xb.at[at.ny], yb, at.to_y)
+    if early:
+        from_z_b = over_z(lambda p: xb.at[:, p], zb)
+    else:
+        from_y_b = wire.send(xb.at[at.ny], yb, at.to_y)
     yield
     from_x_a.wait_recv()
     add_blocks(xa, ya.at[:, x], xa, (4,))
-    from_y_b.wait_recv()
-    add_blocks(yb, xb.at[y], yb, (4,))
-    from_z = []
-    for j, (p, to) in enumerate(zip(at.zs, at.to_z)):
-        from_z.append(wire.send(xa.at[p], rz.at[at.count[j], :, half_a], to))
-        from_z.append(wire.send(yb.at[p], rz.at[at.count[j], :, half_b], to))
-    yield
-    for k in from_z:
+    from_z_a = over_z(lambda p: xa.at[p], za)
+    yield
+    if early:
+        for k in from_z_b:
+            k.wait_recv()
+        zs[...] = add_z(xb[:, z], zb).astype(BF16)
+        from_y_b = wire.send(zs.at[at.ny], yb, at.to_y)
+    else:
+        from_y_b.wait_recv()
+        add_blocks(yb, xb.at[y], yb, (4,))
+        from_z_b = over_z(lambda p: yb.at[p], zb)
+    yield
+    for k in from_z_a:
         k.wait_recv()
-    for acc, half, cols in ((xa, half_a, a), (yb, half_b, b)):
-        out[:, cols] = (
-            (acc[z].astype(F32) + rz[0, :, half].astype(F32)) + rz[1, :, half].astype(F32)
-        ) + rz[2, :, half].astype(F32)
+    out[:, a] = add_z(xa[z], za)
+    if early:
+        from_y_b.wait_recv()
+        out[:, b] = zs[y].astype(F32) + yb[...].astype(F32)
+    else:
+        for k in from_z_b:
+            k.wait_recv()
+        out[:, b] = add_z(yb[z], zb)
+
+
+def reduce_bufs(rows, lo, mid, hi, early):
+    ha, hb = mid - lo, hi - mid
+    last = [(3, 2, rows, hb), (rows, hb), (2, rows, hb)] if early else [(3, rows, hb), (4, rows, hb), (8, 128)]
+    return [(2, 4, 2, rows, hi - lo), (4, 2, rows, ha), (2, 4, rows, hb), (4, rows, ha), (3, rows, ha)] + last
 
 
 def reduce_small(wire, at, mine, sums, got, out):
@@ -525,6 +552,40 @@
     for k in last:
         k.wait_recv()
     out[...] = ((sums[2] + got[3]) + got[4]) + got[5]
+
+
+D_PARTS = ((0.75, True), (0.5, True), (0.75, True), (0.5, True))
+I_PARTS = ((0.75, True), (0.5, True), (0.5, False), (0.75, False))
+O_PARTS = ((0.5, False),)
+
+AFTER = {
+    "pd0": ("d0",),
+    "pd2": ("d1",),
+    "pd3": ("d3", "d0",),
+    "pi0": ("d1",),
+    "pi1": ("i0",),
+    "pi2": ("d2", "d3", "i1",),
+    "pi3": ("d0",),
+    "po": ("d1", "d2", "d1", "i3",),
+    "emb": ("d0", "i2", "d0", "i1",),
+    "a0": ("d3", "i0", "d3",),
+    "a1": ("d2", "d1", "i2", "o", "d2",),
+    "a2": ("i1",),
+    "a3": ("d3", "i1",),
+    "vp0": ("i0", "i0", "o", "d2",),
+    "a4": ("i2", "i1", "i3",),
+    "a5": ("o", "i2",),
+    "a6": ("i0",),
+    "a7": ("i2",),
+    "vp1": ("v0", "v1", "i3", "o", "i3", "i2",),
+    "e0": ("o", "v0", "o", "i3",),
+    "e1": ("t", "i0", "v1", "i3", "v0", "t", "v1", "i3", "t", "i2", "t", "v1", "i1", "o", "d3", "d1", "d2", "d2", "d1", "d3", "v0", "i1", "d0", "d0", "i0", "t",),
+}
+
+
+def cuts_of(width, parts):
+    step = width // len(parts)
+    return [(k * step, k * step + int(step * first), (k + 1) * step, early) for k, (first, early) in enumerate(parts)]
 
 
 def turn_rows(src, dst):
@@ -550,65 +611,71 @@
     own_rows, width = raw.shape
     hidden, cols, length = big.shape[2], d_heads.shape[2], 2 * own_rows
 
-    def stream(grad, out, cut):
-        return reduce_all(wire, at, grad, *(next(rest) for _ in range(6)), out, *cut)
-
-    d_s = [stream(d_g, d_out, cut) for cut in parts_of(hidden, 2)]
-    i_s = [stream(i_g, i_out, cut) for cut in parts_of(hidden, 2)]
-    o_s = stream(o_g, o_out, parts_of(cols, 1)[0])
-    v_s = [reduce_dp(wire, at, v_g.at[k], *(next(rest) for _ in range(3)), v_out.at[k]) for k in range(2)]
-    tiny = reduce_small(wire, at, table, sums, got, s_out)
+    streams = {}
+    for name, grad, out, parts in (("d", d_g, d_out, D_PARTS), ("i", i_g, i_out, I_PARTS), ("o", o_g, o_out, O_PARTS)):
+        for k, cut in enumerate(cuts_of(out.shape[1], parts)):
+            bufs = [next(rest) for _ in range(8)]
+            streams[name + str(k)] = reduce_all(wire, at, grad, bufs, out, *cut)
+    streams["o"] = streams["o0"]
+    for k in range(2):
+        bufs = [next(rest) for _ in range(3)]
+        streams["v" + str(k)] = reduce_dp(wire, at, v_g.at[k], *bufs, v_out.at[k])
+    streams["t"] = reduce_small(wire, at, table, sums, got, s_out)
+
+    def run(step):
+        for name in AFTER.get(step, ()):
+            next(streams[name], None)
 
     def done(one):
         one.wait()
         local.open = [other for other in local.open if other is not one]
 
     from_mix = wire.send(mix_ref.at[at.ny], d_heads.at[y], at.to_y)
-    halves = [pl.ds(lo, hi - lo) for lo, _, hi in parts_of(hidden, 2)]
+    chunk = 512
+    pieces = [pl.ds(lo, chunk) for lo in range(0, hidden, chunk)]
     raw_in = local.copy(ffn_ref, raw)
-    big_in = [local.copy(act_ref.at[:, :, cut], big.at[:, :, cut]) for cut in halves]
+    act_in = [local.copy(act_ref.at[:, :, n], big.at[:, :, n]) for n in pieces]
+    pre_in = []
     mix_in = local.copy(mix_ref.at[y], d_heads.at[y])
     table[...] = small_ref[...]
     done(raw_in)
     turn_rows(raw, tr.at[0])
     raw_in = local.copy(mid_ref, raw)
 
-    chunk = 512
-    per = hidden // 2 // chunk
-
-    def products(left, grad, part):
+    def products(left, grad, lo, hi):
+        per = (hi - lo) // chunk
+
         def one(t, _):
             side = t // per
-            n = pl.ds(pl.multiple_of(part * (hidden // 2) + (t % per) * chunk, chunk), chunk)
+            n = pl.ds(pl.multiple_of(lo + (t % per) * chunk, chunk), chunk)
             made = dg(left[...], big[side, :, n], 1, 0).astype(BF16)
             grad[side, :, :, :, :, n] = made.reshape(grad.shape[1:5] + (chunk,))
             return 0
 
         lax.fori_loop(0, 2 * per, one, 0)
 
-    for part in range(2):
-        done(big_in[part])
-        products(tr.at[0], d_g, part)
-        next(d_s[part])
-        big_in[part] = local.copy(pre_ref.at[:, :, halves[part]], big.at[:, :, halves[part]])
+    for k, (lo, _, hi, _) in enumerate(cuts_of(hidden, D_PARTS)):
+        mine = range(lo // chunk, hi // chunk)
+        for n in mine:
+            done(act_in[n])
+        products(tr.at[0], d_g, lo, hi)
+        pre_in += [local.copy(pre_ref.at[:, :, pieces[n]], big.at[:, :, pieces[n]]) for n in mine]
+        run("pd" + str(k))
     done(raw_in)
     turn_rows(raw, tr.at[1])
     raw_in = local.copy(attn_ref, raw)
-    done(big_in[0])
-    products(tr.at[1], i_g, 0)
-    next(i_s[0])
-    next(d_s[0])
-    done(big_in[1])
-    products(tr.at[1], i_g, 1)
-    next(i_s[1])
+    for k, (lo, _, hi, _) in enumerate(cuts_of(hidden, I_PARTS)):
+        for n in range(lo // chunk, hi // chunk):
+            done(pre_in[n])
+        products(tr.at[1], i_g, lo, hi)
+        run("pi" + str(k))
     qkv_in = local.copy(qkv_ref, big.at[:, :, 0 : 3 * cols])
     done(raw_in)
     turn_rows(raw, tr.at[0])
     for side, right in ((y, mine_ref.at[y]), (at.ny, far_ref)):
         made = dg(tr[0], right[...], 1, 0).astype(BF16)
         o_g[side] = made.reshape(o_g.shape[1:])
-    next(o_s)
-    next(d_s[1])
+    run("po")
 
     embed_in = local.copy(embed_ref, d_g.at[0, :, :, :, :, 0:width])
     v_in = local.copy(v_ref, d_g.at[1, :, :, :, :, 0 : v_ref.shape[4]])
@@ -627,6 +694,7 @@
     done(qkv_in)
     done(mix_in)
     from_mix.wait_recv()
+    run("emb")
 
     part_cols = cols // 2
 
@@ -646,16 +714,8 @@
 
     pair = 2 * HD
     scale = 1.0 / math.sqrt(HD)
-    ticks = {
-        0: lambda: next(d_s[0]),
-        1: lambda: next(i_s[0]),
-        2: lambda: next(i_s[1]),
-        3: lambda: (project_grad(0), next(v_s[0]), next(d_s[0])),
-        4: lambda: (next(d_s[1]), next(o_s)),
-        5: lambda: next(v_s[0]),
-        6: lambda: next(i_s[0]),
-        7: lambda: (next(d_s[0], None), next(d_s[1])),
-    }
+    ticks = {t: lambda t=t: run("a" + str(t)) for t in range(8) if "a" + str(t) in AFTER}
+    ticks[3] = lambda: (run("a3"), project_grad(0), run("vp0"))
 
     def attend_step(t, _):
         p, half = t // 2, t % 2
@@ -699,7 +759,7 @@
 
     lax.fori_loop(0, 2 * (cols // pair), attend_step, 0)
     project_grad(1)
-    next(v_s[1])
+    run("vp1")
 
     step = 256
     total = table[18:19]
@@ -719,12 +779,10 @@
             local.copy(i_g.at[0, pl.ds(2 * half, 2), :, :, :, 0:width], x_own)
         else:
             from_x = wire.send(i_g.at[0, pl.ds(2 * half, 2), :, :, :, 0:width], x_got, at.to_y)
+            run("e0")
     down = lax.broadcasted_iota(jnp.int32, (16, width), 0)
     table[0:16] = jnp.where(down == at.i, total, 0.0)
-    left = [tiny, i_s[1], v_s[1], o_s, v_s[0], i_s[0], d_s[1]]
-    for _ in range(7):
-        for one in left:
-            next(one, None)
+    run("e1")
     from_x.wait_recv()
     local.close()
     wire.close()
@@ -749,13 +807,10 @@
         S(small.shape, F32), S((3,) + small.shape, F32), S((6,) + small.shape, F32),
     ]
     copies = 1 + 1 + 6
-    for n in [hidden // 2] * 4 + [cols]:
-        h = n // 2
-        copies += 11
-        scratch += [
-            S(s, BF16)
-            for s in ((2, 4, 2, rows, n), (4, 2, rows, h), (2, 4, rows, h), (4, rows, h), (4, rows, h), (3, rows, n))
-        ]
+    for n, parts in ((hidden, D_PARTS), (hidden, I_PARTS), (cols, O_PARTS)):
+        for cut in cuts_of(n, parts):
+            copies += 11
+            scratch += [S(a, BF16) for a in reduce_bufs(rows, *cut)]
     for n in [3 * cols // 2] * 2:
         copies += 5
         scratch += [S(s, BF16) for s in ((4, 2, rows, n), (4, rows, n), (3, rows, n))]
@@ -777,7 +832,7 @@
     )(d_ffn, mid, d_attn, act, d_pre, d_mix, qkv, embed, v_all, far, mine, stats, seg_row, seg_col, small)
 
 
-BACKWARD_LOCAL = 12
+BACKWARD_LOCAL = 16
 
 
 def attend_kernel(tile, q_ref, k_ref, v_ref, sr_ref, sc_ref, o_ref, l_ref):

time: 351 us -> 334 us (0.952); the launches traced: 350 us -> 327 us
  Pallas kernels: 289 us -> 265 us
    pallas_call x1, Pallas kernels: 154 us -> 130 us  [backward(): pl.pallas_call(backward_kernel, name='backward', out_shape=outs, in_specs...]
where the time goes in v5:
time: 334 us; the launch traced here: 327 us
  Pallas kernels  265 us (79%)
  matrix products  29.4 us (9%)
  local copies, waits for them, and re-layouts  19.3 us (6%)
  other arithmetic  11.4 us (3%)
    pallas_call x1, Pallas kernels, forward(): pl.pallas_call(forward_kernel, name='forward', out_shape=outs, in_specs=[...  135 us
    pallas_call x1, Pallas kernels, backward(): pl.pallas_call(backward_kernel, name='backward', out_shape=outs, in_specs...  130 us
    dot_general x4, matrix products, ein(): return jnp.einsum(spec, left, right, preferred_element_type=F32)  27.4 us
    unnamed x40, local copies, waits for them, and re-layouts  7.82 us

profile of v5, /device:TPU:20, one launch (start us, length us, event | category | flops | bytes accessed | tf_op | source)
XLA Modules:
  0.0 327.4 jit_solution(11172055510369814772)
XLA Ops:
  1.3 1.2 slice.61.b_ref
  2.5 0.7 broadcast_in_dim.14
  3.8 0.8 copy.32
  4.6 0.8 copy.31
  5.4 0.9 slice_bitcast_fusion
  6.3 0.8 concatenate.29.v_ref
  7.1 1.7 broadcast_in_dim.31.sc_ref
  8.8 135.0 %forward.1 = (bf16[4,2,2,64,1664]{4,3,2,1,0:T(8,128)(2,1)}, bf16[2,4,2,2,64,512]{5,4,3,2,1,0:T(8,128)(2,1)}, bf16[2,4,2,2,64,2048]{5,4,3,2,1,0:T(8,128)(2,1)}, b...) custom-call(bf16[64,1664]{1,0:T(8,128)(2,1)} %concatenate.29.v_ref, ...), custom_call_target="tpu_custom_call" | custom-call | tf_op jit(solution)/shard_map/forward/pallas_call | solution.py:421
  143.8 0.9 fusion.22
  144.7 1.1 slice_reduce_fusion
  145.8 0.9 copy.42
  147.3 9.8 %fusion.23 = (f32[512]{0:T(512)S(1)}, f32[512,1024]{1,0:T(8,128)S(1)}) fusion(f32[1024]{0:T(1024)S(1)} %bitcast.95, bf16[2,512,2048]{2,1,0:T(8,128)(2,1)} %get-tuple-element.35.act_ref, bf16[2,1024,2048]{2,1,0:T(8,128)(2,1)} %bitcast.100, f32[1024]{0:T(1024)S(1)} %bitcast.96, f32[512,1024]{1,0:T(8,128)} %get-tuple-element.33, f32[1024]{0:T(1024)S(1)} %bitcast.87), kind=kOutput, calls=%fused_computation.59 | convolution fusion | flops 4297588224 | bytes 16791552 | tf_op jit(solution)/shard_map/yrf,ynf->rn/dot_general | solution.py:962
  157.5 0.9 copy-done.5
  158.4 1.0 fusion.8
  159.4 1.8 fusion.19
  162.0 9.0 %fusion = (f32[2,2048]{1,0:T(2,128)S(1)}, bf16[2,512,2048]{2,1,0:T(8,128)(2,1)S(1)}) fusion(bf16[2,512,2048]{2,1,0:T(8,128)(2,1)S(1)} %copy-done.12, bf16[2,1024,2048]{2,1,0:T(8,128)(2,1)} %bitcast.101, bf16[512,1024]{1,0:T(8,128)(2,1)S(1)} %convert_element_type.56.ffn_ref), kind=kOutput, calls=%fused_computation.1 | convolution fusion | flops 4303351808 | bytes 17842176 | tf_op jit(solution)/shard_map/rn,ynf->yrf/dot_general | solution.py:962
  171.1 6.3 %multiply_reduce_fusion = (f32[1024]{0:T(1024)S(1)}, f32[512]{0:T(512)S(1)}, f32[512]{0:T(512)S(1)}, f32[1024]{0:T(1024)S(1)}, f32[512,1024]{1,0:T(8,128)}) fusion(f32[512,1024]{1,0:T(8,128)S(1)} %copy-done.6, f32[1024]{0:T(1024)S(1)} %bitcast.88, f32[512,1024]{1,0:T(8,128)S(1)} %get-tuple-element.65, ...), kind=kOutput, calls=%fused_computation.18 | convolution fusion | flops 4299158528 | bytes 18890752 | tf_op jit(solution)/shard_map/yrf,ydf->rd/dot_general | solution.py:962
  177.4 2.7 fusion.21
  180.3 0.7 pad.4.small_ref
  181.7 1.0 copy-done.4
  182.7 2.3 fusion.10.mix_ref
  184.9 130.4 %backward.1 = (f32[2,64,768]{2,1,0:T(8,128)}, f32[64,512]{1,0:T(8,128)}, f32[64,2048]{1,0:T(8,128)}, f32[64,2048]{1,0:T(8,128)}, bf16[2,2,2,64,1024]{4,3,2,1,0:T...) custom-call(bf16[512,1024]{1,0:T(8,128)(2,1)} %copy-done.3, ...), custom_call_target="tpu_custom_call" | custom-call | tf_op jit(solution)/shard_map/backward/pallas_call | solution.py:818
  315.4 2.1 convert_add_fusion
  317.6 1.7 bitcast_add_fusion
  319.4 0.6 constant_dynamic-slice_fusion
  320.1 0.6 dynamic_slice.15
  320.7 0.7 fusion.17
  321.4 1.9 fusion.14
  323.8 1.1 reshape.132
  324.9 0.7 copy.48
  325.6 0.8 copy.49
  326.3 0.8 copy.50
  (56 shorter events, 3.9 us)
Async XLA Ops:
  157.2 1.2 copy-start.5
  159.4 2.6 copy-start.12
  161.3 9.8 %slice-start = ((s8[8388608]{0:T(1024)(128)(4,1)}), s8[4194304]{0:T(1024)(128)(4,1)S(1)}, s32[]{:S(2)}) async-start(s8[8388608]{0:T(1024)(128)(4,1)} %bitcast.97), calls=%async_computation | async-start | bytes 8388608
  162.0 9.1 %copy-start.3 = (bf16[512,1024]{1,0:T(8,128)(2,1)}, bf16[512,1024]{1,0:T(8,128)(2,1)S(1)}, u32[]{:S(2)}) copy-start(bf16[512,1024]{1,0:T(8,128)(2,1)S(1)} %convert_element_type.56.ffn_ref) | copy-start | bytes 3145732
  162.0 9.1 %copy-start.6 = (f32[512,1024]{1,0:T(8,128)S(1)}, f32[512,1024]{1,0:T(8,128)}, u32[]{:S(2)}) copy-start(f32[512,1024]{1,0:T(8,128)} %get-tuple-element.33) | copy-start | bytes 6291460
  162.0 9.1 %slice-start.1 = ((s8[8388608]{0:T(1024)(128)(4,1)}), s8[4194304]{0:T(1024)(128)(4,1)S(1)}, s32[]{:S(2)}) async-start(s8[8388608]{0:T(1024)(128)(4,1)} %bitcast.97), calls=%async_computation.1 | async-start | bytes 8388608
  171.1 6.3 %copy-start.2 = (bf16[2,512,2048]{2,1,0:T(8,128)(2,1)}, bf16[2,512,2048]{2,1,0:T(8,128)(2,1)S(1)}, u32[]{:S(2)}) copy-start(bf16[2,512,2048]{2,1,0:T(8,128)(2,1)S(1)} %get-tuple-element.69.pre_ref) | copy-start | bytes 12582916
  180.2 1.4 copy-start
  180.3 2.4 copy-start.13
  181.7 1.0 copy-start.4
  315.4 2.2 copy-start.1
  317.6 1.7 copy-start.10
  317.6 5.7 %copy-start.9 = (f32[2,64,768]{2,1,0:T(8,128)S(1)}, f32[2,64,768]{2,1,0:T(8,128)}, u32[]{:S(2)}) copy-start(f32[2,64,768]{2,1,0:T(8,128)} %get-tuple-element.52) | copy-start | bytes 1179652
  319.4 5.5 %copy-start.11 = (f32[64,512]{1,0:T(8,128)S(1)}, f32[64,512]{1,0:T(8,128)}, u32[]{:S(2)}) copy-start(f32[64,512]{1,0:T(8,128)} %get-tuple-element.53) | copy-start | bytes 393220
  319.4 6.2 %copy-start.8 = (f32[64,2048]{1,0:T(8,128)S(1)}, f32[64,2048]{1,0:T(8,128)}, u32[]{:S(2)}) copy-start(f32[64,2048]{1,0:T(8,128)} %get-tuple-element.99) | copy-start | bytes 1572868
  321.4 5.0 %copy-start.7 = (f32[64,2048]{1,0:T(8,128)S(1)}, f32[64,2048]{1,0:T(8,128)}, u32[]{:S(2)}) copy-start(f32[64,2048]{1,0:T(8,128)} %get-tuple-element.55) | copy-start | bytes 1572868

commit v6 on v5

--- a/solution.py
+++ b/solution.py
@@ -84,32 +84,51 @@
 
 
 class Local:
-    def __init__(self, sems):
-        self.sems, self.used, self.open = sems, 0, []
+    def __init__(self, at, sems):
+        self.sems, self.used, self.open = [sems.at[at.zero + k] for k in range(sems.shape[0])], 0, []
 
     def copy(self, src, dst):
-        one = pltpu.make_async_copy(src, dst, self.sems.at[self.used])
+        one = pltpu.make_async_copy(src, dst, self.sems[self.used])
         self.used += 1
         one.start()
         self.open.append(one)
         return one
 
+    def wait(self, one):
+        one.wait()
+        self.open = [other for other in self.open if other is not one]
+
     def close(self):
-        assert self.used == self.sems.shape[0], self.used
+        assert self.used == len(self.sems), self.used
         for one in self.open:
             one.wait()
 
 
-def parts_of(width, parts, first=0.5):
-    step = width // parts
-    return [(p * step, p * step + int(step * first), (p + 1) * step) for p in range(parts)]
-
-
-def stagger(streams, ahead=0):
-    for depth in range(ahead, len(streams) + 6):
-        for k, s in enumerate(streams):
-            if k <= depth:
-                next(s, None)
+D_CUTS = ((0.625, True), (0.625, True))
+I_CUTS = ((0.625, True), (0.625, True))
+O_CUTS = ((0.5, True),)
+
+FORWARD_AFTER = {
+    "start": ("v0", "v1", "o", "i0",),
+    "few": ("v0", "v1", "o", "i1", "d0", "v0", "o",),
+    "part": ("i0", "v1", "i0", "v0",),
+    "emb": ("v1", "i1", "o", "d1",),
+    "proj": ("i0", "o",),
+    "a1": ("d0", "d1", "i1",),
+    "a3": ("i1", "d0", "i0",),
+    "a6": ("i1", "o",),
+    "a7": ("i0", "d0", "o", "i1", "d1", "i0", "d0",),
+    "f0": ("d1",),
+    "f2": ("i1", "d1",),
+    "f4": ("d0",),
+    "f6": ("d1",),
+    "end": ("d0", "d1",),
+}
+
+
+def cuts_of(width, parts):
+    step = width // len(parts)
+    return [(k * step, k * step + int(step * first), (k + 1) * step, early) for k, (first, early) in enumerate(parts)]
 
 
 def gather_dp(wire, at, shard, whole, lo, hi):
@@ -134,11 +153,13 @@
         k.wait_recv()
 
 
-def gather_all(wire, at, shard, whole, lo, mid, hi):
+def gather_all(wire, at, shard, whole, lo, mid, hi, early):
     a, b, ab = pl.ds(lo, mid - lo), pl.ds(mid, hi - mid), pl.ds(lo, hi - lo)
     y, z, x, c = at.y, at.z, at.x, at.c
-    from_z_a = [wire.send(shard.at[:, a], whole.at[y, z, x, c, :, a], to) for to in at.to_z]
-    from_y_b = wire.send(shard.at[:, b], whole.at[y, z, x, c, :, b], at.to_y)
+    first = a if early else ab
+    from_z_a = [wire.send(shard.at[:, first], whole.at[y, z, x, c, :, first], to) for to in at.to_z]
+    if early:
+        from_y_b = wire.send(shard.at[:, b], whole.at[y, z, x, c, :, b], at.to_y)
     late = [wire.send(shard.at[:, ab], whole.at[y, z, x, c, :, ab], at.to_c)]
 
     def to_core(*refs):
@@ -146,13 +167,21 @@
             late.append(wire.send(ref, ref, at.to_c))
 
     yield
-    from_y_b.wait_recv()
-    ref = whole.at[:, z, x, c, :, b]
-    from_z_b = [wire.send(ref, ref, to) for to in at.to_z]
-    to_core(whole.at[at.ny, z, x, c, :, b])
-    yield
-    for k in from_z_a:
-        k.wait_recv()
+    if early:
+        from_y_b.wait_recv()
+        ref = whole.at[:, z, x, c, :, b]
+        from_z_b = [wire.send(ref, ref, to) for to in at.to_z]
+        to_core(whole.at[at.ny, z, x, c, :, b])
+    else:
+        for k in from_z_a:
+            k.wait_recv()
+        ref = whole.at[y, :, x, c, :, b]
+        from_y_b = wire.send(ref, ref, at.to_y)
+        to_core(*(whole.at[y, p, x, c, :, b] for p in at.zs))
+    yield
+    if early:
+        for k in from_z_a:
+            k.wait_recv()
     ref = whole.at[y, :, x, c, :, a]
     from_x_a = wire.send(ref, ref, at.to_x)
     to_core(*(whole.at[y, p, x, c, :, a] for p in at.zs))
@@ -162,11 +191,15 @@
     from_y_a = wire.send(ref, ref, at.to_y)
     to_core(whole.at[y, :, at.nx, c, :, a])
     yield
-    for k in from_z_b:
-        k.wait_recv()
+    if early:
+        for k in from_z_b:
+            k.wait_recv()
+        to_core(*(whole.at[:, p, x, c, :, b] for p in at.zs))
+    else:
+        from_y_b.wait_recv()
+        to_core(whole.at[at.ny, :, x, c, :, b])
     ref = whole.at[:, :, x, c, :, b]
     from_x_b = wire.send(ref, ref, at.to_x)
-    to_core(*(whole.at[:, p, x, c, :, b] for p in at.zs))
     yield
     from_y_a.wait_recv()
     from_x_b.wait_recv()
@@ -192,7 +225,7 @@
     at = Place()
     y, z, x, c = at.y, at.z, at.x, at.c
     at.enter(True)
-    wire, local = Wire(at, send_sems, recv_sems), Local(local_sems)
+    wire, local = Wire(at, send_sems, recv_sems), Local(at, local_sems)
     width = h_ref.shape[1]
     own_rows = h_ref.shape[0]
     rows = v_ref.shape[0]
@@ -203,21 +236,32 @@
     from_few = [wire.send(f_ref, few.at[at.i], (p, y)) for p in at.dp]
     from_h = wire.send(h_ref, h_far, at.to_y)
     v_mid = 7 * 128
-    v0 = gather_dp(wire, at, v_ref, v_all, 0, v_mid)
-    v1 = gather_dp(wire, at, v_ref, v_all, v_mid, v_ref.shape[1])
-    out_w = gather_all(wire, at, o_ref, o_all, *parts_of(cols, 1)[0])
-    in_w = [gather_all(wire, at, i_ref, i_all, *cut) for cut in parts_of(hidden, 2, 0.625)]
-    down_w = [gather_all(wire, at, d_ref, d_all, *cut) for cut in parts_of(hidden, 2, 0.625)]
+    streams = {
+        "v0": gather_dp(wire, at, v_ref, v_all, 0, v_mid),
+        "v1": gather_dp(wire, at, v_ref, v_all, v_mid, v_ref.shape[1]),
+    }
+    for name, shard, whole, parts in (("d", d_ref, d_all, D_CUTS), ("i", i_ref, i_all, I_CUTS), ("o", o_ref, o_all, O_CUTS)):
+        for k, cut in enumerate(cuts_of(shard.shape[1], parts)):
+            streams[name + str(k)] = gather_all(wire, at, shard, whole, *cut)
+    streams["o"] = streams["o0"]
+    begun = set()
+
     kept = [
         local.copy(v_ref, v_all.at[z, x, c]),
         local.copy(o_ref, o_all.at[y, z, x, c]),
         local.copy(i_ref, i_all.at[y, z, x, c]),
         local.copy(d_ref, d_all.at[y, z, x, c]),
     ]
-    next(v0)
-    next(v1)
-    next(out_w)
-    next(in_w[0])
+
+    def run(step):
+        for name in FORWARD_AFTER.get(step, ()):
+            if name in begun:
+                while kept:
+                    local.wait(kept.pop())
+            begun.add(name)
+            next(streams[name], None)
+
+    run("start")
     few[at.i] = f_ref[...]
     for k in from_few:
         k.wait_recv()
@@ -231,26 +275,14 @@
     ffn_b[...] = jnp.concatenate([few[s][:, width:] for s in range(seqs)], axis=1)
     local.copy(few, few_out)
     from_part = [wire.send(part.at[p], got.at[j], (p, y)) for j, p in enumerate(at.dp)]
-    for k in kept:
-        k.wait()
-        local.open.remove(k)
-    next(v0)
-    next(v1)
-    next(out_w)
-    next(in_w[1])
-    next(down_w[0])
-    next(v0)
-    next(out_w)
+    run("few")
     for k in from_part:
         k.wait_recv()
     total = part[at.i]
     for j in range(seqs - 1):
         total = total + got[j]
     time_out[...] = total
-    next(in_w[0])
-    next(v1)
-    next(in_w[0])
-    next(v0, None)
+    run("part")
 
     from_h.wait_recv()
     step = 128
@@ -263,11 +295,9 @@
 
     lax.fori_loop(0, own_rows // step, embed_rows, 0)
     local.copy(embed, embed_out)
-    next(v1, None)
-    next(in_w[1])
-    next(out_w)
-    next(down_w[1])
+    run("emb")
     local.copy(v_all, v_out)
+    run("vdone")
     par[...] = v_all[:, :, :, :, 3 * cols :].reshape(width, 128).astype(F32).T
     local.copy(par, par_out)
     heads = pl.ds(pl.multiple_of(y * cols, cols), cols)
@@ -287,8 +317,7 @@
 
     lax.fori_loop(0, length // step_q, project, 0)
     local.copy(qkv, qkv_out)
-    next(in_w[0])
-    next(out_w)
+    run("proj")
 
     pair, tile = 2 * HD, own_rows
     from_far = []
@@ -297,13 +326,12 @@
         n = pl.ds(p * pair, pair)
         from_far.append(wire.send(mine.at[at.ny, :, n], far.at[:, n], at.to_y))
 
-    ticks = {
-        1: lambda: (give(0), next(down_w[0]), next(down_w[1]), next(in_w[1]),),
-        3: lambda: (give(1), next(in_w[1]), next(down_w[0]), next(in_w[0]),),
-        5: lambda: (give(2),),
-        6: lambda: (next(in_w[1]), next(out_w),),
-        7: lambda: (give(3), next(in_w[0]), next(down_w[0]), next(out_w, None), next(in_w[1]), next(down_w[1]), next(in_w[0], None), next(down_w[0]),),
-    }
+    def tick_of(t):
+        if t % 2:
+            give(t // 2)
+        run("a" + str(t))
+
+    ticks = {t: lambda t=t: tick_of(t) for t in range(8) if t % 2 or "a" + str(t) in FORWARD_AFTER}
 
     def attend_step(t, _):
         p, half = t // 2, t % 2
@@ -352,20 +380,14 @@
     local.copy(unit, unit_out)
     local.copy(inv, inv_out)
     local.copy(mid, mid_out)
-
+    run("out")
 
     chunk = 512
-    per = hidden // 2 // chunk
-    later = {
-        0: lambda: (next(down_w[1]),),
-        2: lambda: (next(in_w[1], None), next(down_w[1]),),
-        4: lambda: (next(down_w[0]),),
-        6: lambda: (next(down_w[1]),),
-    }
+    later = {t: lambda t=t: run("f" + str(t)) for t in range(8) if "f" + str(t) in FORWARD_AFTER}
 
     def feed_step(t, _):
-        side = (t // per) % 2
-        n = pl.multiple_of((t // (2 * per)) * (hidden // 2) + (t % per) * chunk, chunk)
+        side = t % 2
+        n = pl.multiple_of((t // 2) * chunk, chunk)
         made = dg(mid[...], i_all[side, :, :, :, :, pl.ds(n, chunk)].reshape(width, chunk), 1, 0)
         made = made + ffn_b[:, pl.ds(pl.multiple_of(side * hidden, hidden) + n, chunk)]
         below = 0.5 + 0.5 * lax.erf(made * math.sqrt(0.5))
@@ -382,11 +404,10 @@
             pl.when(t == k)(lambda tick=tick: (tick(), None)[1])
         return 0
 
-    tiles = 4 * per
+    tiles = 2 * hidden // chunk
     lax.fori_loop(0, tiles, feed_step, 0)
     local.copy(i_all, i_out)
-    next(down_w[0], None)
-    next(down_w[1], None)
+    run("end")
     for t in range(tiles):
         n = pl.ds(0, chunk)
         pltpu.make_async_copy(act.at[0, :, n], act_out.at[0, :, n], tile_sems.at[0, t]).wait()
@@ -417,7 +438,7 @@
     part, got = S((16, 1, width), F32), S((15, 1, width), F32)
     h_far, ffn_b = S(h.shape, BF16), S((1, 2 * hidden), F32)
     scratch = [v_all, o_all, i_all, few, part, got, h_far, par, ffn_b, embed, qkv, mine, far, stats, unit, inv, mid, act, act]
-    copies = 15 + 15 + 1 + 2 * 9 + 5 * 21 + pairs
+    copies = 15 + 15 + 1 + 2 * 9 + sum(21 if early else 18 for _, early in D_CUTS + I_CUTS + O_CUTS) + pairs
     return pl.pallas_call(
         forward_kernel,
         name="forward",
@@ -583,11 +604,6 @@
 }
 
 
-def cuts_of(width, parts):
-    step = width // len(parts)
-    return [(k * step, k * step + int(step * first), (k + 1) * step, early) for k, (first, early) in enumerate(parts)]
-
-
 def turn_rows(src, dst):
     def one(t, _):
         r = pl.ds(pl.multiple_of(t * 128, 128), 128)
@@ -606,7 +622,7 @@
     y = at.y
     at.enter(False)
     rest = iter(rest)
-    wire, local = Wire(at, next(rest), next(rest)), Local(next(rest))
+    wire, local = Wire(at, next(rest), next(rest)), Local(at, next(rest))
     raw, tr, big, d_heads, d_g, i_g, o_g, v_g, acc_k, acc_v, table, sums, got = (next(rest) for _ in range(13))
     own_rows, width = raw.shape
     hidden, cols, length = big.shape[2], d_heads.shape[2], 2 * own_rows
@@ -619,16 +635,14 @@
     streams["o"] = streams["o0"]
     for k in range(2):
         bufs = [next(rest) for _ in range(3)]
-        streams["v" + str(k)] = reduce_dp(wire, at, v_g.at[k], *bufs, v_out.at[k])
+        streams["v" + str(k)] = reduce_dp(wire, at, v_g.at[at.count[k]], *bufs, v_out.at[at.count[k]])
     streams["t"] = reduce_small(wire, at, table, sums, got, s_out)
 
     def run(step):
         for name in AFTER.get(step, ()):
             next(streams[name], None)
 
-    def done(one):
-        one.wait()
-        local.open = [other for other in local.open if other is not one]
+    done = local.wait
 
     from_mix = wire.send(mix_ref.at[at.ny], d_heads.at[y], at.to_y)
     chunk = 512
@@ -642,33 +656,36 @@
     turn_rows(raw, tr.at[0])
     raw_in = local.copy(mid_ref, raw)
 
-    def products(left, grad, lo, hi):
-        per = (hi - lo) // chunk
+    def products(left, grad, arrived, after):
+        steps = {2 * k + 1: (lambda k=k: after(k)) for k in range(len(pieces))}
 
         def one(t, _):
-            side = t // per
-            n = pl.ds(pl.multiple_of(lo + (t % per) * chunk, chunk), chunk)
-            made = dg(left[...], big[side, :, n], 1, 0).astype(BF16)
-            grad[side, :, :, :, :, n] = made.reshape(grad.shape[1:5] + (chunk,))
+            n = pl.ds(pl.multiple_of((t // 2) * chunk, chunk), chunk)
+            made = dg(left[...], big[t % 2, :, n], 1, 0).astype(BF16)
+            grad[t % 2, :, :, :, :, n] = made.reshape(grad.shape[1:5] + (chunk,))
+            for k, step in steps.items():
+                pl.when(t == k)(lambda step=step: (step(), None)[1])
             return 0
 
-        lax.fori_loop(0, 2 * per, one, 0)
-
-    for k, (lo, _, hi, _) in enumerate(cuts_of(hidden, D_PARTS)):
-        mine = range(lo // chunk, hi // chunk)
-        for n in mine:
-            done(act_in[n])
-        products(tr.at[0], d_g, lo, hi)
-        pre_in += [local.copy(pre_ref.at[:, :, pieces[n]], big.at[:, :, pieces[n]]) for n in mine]
+        done(arrived[0])
+        lax.fori_loop(0, 2 * len(pieces), one, 0)
+
+    def after_down(k):
+        pre_in.append(local.copy(pre_ref.at[:, :, pieces[k]], big.at[:, :, pieces[k]]))
         run("pd" + str(k))
+        if k + 1 < len(pieces):
+            done(act_in[k + 1])
+
+    def after_in(k):
+        run("pi" + str(k))
+        if k + 1 < len(pieces):
+            done(pre_in[k + 1])
+
+    products(tr.at[0], d_g, act_in, after_down)
     done(raw_in)
     turn_rows(raw, tr.at[1])
     raw_in = local.copy(attn_ref, raw)
-    for k, (lo, _, hi, _) in enumerate(cuts_of(hidden, I_PARTS)):
-        for n in range(lo // chunk, hi // chunk):
-            done(pre_in[n])
-        products(tr.at[1], i_g, lo, hi)
-        run("pi" + str(k))
+    products(tr.at[1], i_g, pre_in, after_in)
     qkv_in = local.copy(qkv_ref, big.at[:, :, 0 : 3 * cols])
     done(raw_in)
     turn_rows(raw, tr.at[0])
@@ -714,8 +731,12 @@
 
     pair = 2 * HD
     scale = 1.0 / math.sqrt(HD)
-    ticks = {t: lambda t=t: run("a" + str(t)) for t in range(8) if "a" + str(t) in AFTER}
-    ticks[3] = lambda: (run("a3"), project_grad(0), run("vp0"))
+    def tick_of(t):
+        run("a" + str(t))
+        if t % 4 == 3:
+            run("vp" + str(t // 4))
+
+    ticks = {t: lambda t=t: tick_of(t) for t in range(8)}
 
     def attend_step(t, _):
         p, half = t // 2, t % 2
@@ -753,37 +774,42 @@
             big[:, :, ck] = (acc_k[...] + d_k).astype(BF16).reshape(2, own_rows, pair)
             big[:, :, cv] = (acc_v[...] + d_v).astype(BF16).reshape(2, own_rows, pair)
 
+        pl.when(t % 4 == 3)(lambda: project_grad(t // 4))
         for k, tick in ticks.items():
             pl.when(t == k)(lambda tick=tick: (tick(), None)[1])
         return 0
 
     lax.fori_loop(0, 2 * (cols // pair), attend_step, 0)
-    project_grad(1)
-    run("vp1")
 
     step = 256
-    total = table[18:19]
-    for half in (at.ny, y):
-
-        def embed_grad(t, acc, half=half):
-            r = pl.ds(pl.multiple_of(t * step, step), step)
-            made = dg(
-                big[half, r, 0 : 3 * cols],
-                d_g[1, :, :, :, :, 0 : 3 * cols].reshape(width, 3 * cols), 1, 1,
-            )
-            i_g[0, 2 * half + t, :, :, :, 0:width] = made.astype(BF16).reshape(i_g.shape[2:5] + (width,))
-            return acc + jnp.sum(made, axis=0, keepdims=True)
-
-        total = lax.fori_loop(0, own_rows // step, embed_grad, total)
-        if half is y:
-            local.copy(i_g.at[0, pl.ds(2 * half, 2), :, :, :, 0:width], x_own)
-        else:
-            from_x = wire.send(i_g.at[0, pl.ds(2 * half, 2), :, :, :, 0:width], x_got, at.to_y)
+    per_half = own_rows // step
+
+    def rows_of(half):
+        return i_g.at[at.zero, pl.ds(2 * half, 2), :, :, :, 0:width]
+
+    def embed_grad(t, acc):
+        half = (at.ny + t // per_half) % 2
+        r = pl.ds(pl.multiple_of((t % per_half) * step, step), step)
+        made = dg(
+            big[half, r, 0 : 3 * cols],
+            d_g[1, :, :, :, :, 0 : 3 * cols].reshape(width, 3 * cols), 1, 1,
+        )
+        i_g[0, 2 * half + t % per_half, :, :, :, 0:width] = made.astype(BF16).reshape(i_g.shape[2:5] + (width,))
+
+        @pl.when(t == per_half - 1)
+        def _():
+            from_x.append(wire.send(far_rows, x_got, at.to_y))
             run("e0")
+
+        return acc + jnp.sum(made, axis=0, keepdims=True)
+
+    from_x, far_rows = [], rows_of(at.ny)
+    total = lax.fori_loop(0, 2 * per_half, embed_grad, table[18:19])
+    local.copy(rows_of(y), x_own)
     down = lax.broadcasted_iota(jnp.int32, (16, width), 0)
     table[0:16] = jnp.where(down == at.i, total, 0.0)
     run("e1")
-    from_x.wait_recv()
+    from_x[0].wait_recv()
     local.close()
     wire.close()
 

time: 334 us -> 329 us (0.985); the launches traced: 327 us -> 327 us
  no operation moved by 1% of the time
where the time goes in v6:
time: 329 us; the launch traced here: 327 us
  Pallas kernels  266 us (81%)
  matrix products  29.4 us (9%)
  local copies, waits for them, and re-layouts  19.3 us (6%)
  other arithmetic  11.4 us (3%)
    pallas_call x1, Pallas kernels, forward(): pl.pallas_call(forward_kernel, name='forward', out_shape=outs, in_specs=[...  135 us
    pallas_call x1, Pallas kernels, backward(): pl.pallas_call(backward_kernel, name='backward', out_shape=outs, in_specs...  131 us
    dot_general x4, matrix products, ein(): return jnp.einsum(spec, left, right, preferred_element_type=F32)  27.5 us
    unnamed x40, local copies, waits for them, and re-layouts  7.82 us

profile of v6, /device:TPU:20, one launch (start us, length us, event | category | flops | bytes accessed | tf_op | source)
XLA Modules:
  0.0 327.5 jit_solution(10995622771826201002)
XLA Ops:
  1.3 1.2 slice.61.b_ref
  2.5 0.7 broadcast_in_dim.14
  3.8 0.8 copy.32
  4.6 0.8 copy.31
  5.4 0.9 slice_bitcast_fusion
  6.3 0.8 concatenate.29.v_ref
  7.1 1.7 broadcast_in_dim.31.sc_ref
  8.8 134.7 %forward.1 = (bf16[4,2,2,64,1664]{4,3,2,1,0:T(8,128)(2,1)}, bf16[2,4,2,2,64,512]{5,4,3,2,1,0:T(8,128)(2,1)}, bf16[2,4,2,2,64,2048]{5,4,3,2,1,0:T(8,128)(2,1)}, b...) custom-call(bf16[64,1664]{1,0:T(8,128)(2,1)} %concatenate.29.v_ref, ...), custom_call_target="tpu_custom_call" | custom-call | tf_op jit(solution)/shard_map/forward/pallas_call | solution.py:442
  143.5 0.9 fusion.22
  144.4 1.1 slice_reduce_fusion
  145.5 0.9 copy.42
  147.1 9.8 %fusion.23 = (f32[512]{0:T(512)S(1)}, f32[512,1024]{1,0:T(8,128)S(1)}) fusion(f32[1024]{0:T(1024)S(1)} %bitcast.95, bf16[2,512,2048]{2,1,0:T(8,128)(2,1)} %get-tuple-element.35.act_ref, bf16[2,1024,2048]{2,1,0:T(8,128)(2,1)} %bitcast.100, f32[1024]{0:T(1024)S(1)} %bitcast.96, f32[512,1024]{1,0:T(8,128)} %get-tuple-element.33, f32[1024]{0:T(1024)S(1)} %bitcast.87), kind=kOutput, calls=%fused_computation.59 | convolution fusion | flops 4297588224 | bytes 16791552 | tf_op jit(solution)/shard_map/yrf,ynf->rn/dot_general | solution.py:988
  157.3 0.9 copy-done.5
  158.1 1.0 fusion.8
  159.1 1.8 fusion.19
  161.7 9.1 %fusion = (f32[2,2048]{1,0:T(2,128)S(1)}, bf16[2,512,2048]{2,1,0:T(8,128)(2,1)S(1)}) fusion(bf16[2,512,2048]{2,1,0:T(8,128)(2,1)S(1)} %copy-done.12, bf16[2,1024,2048]{2,1,0:T(8,128)(2,1)} %bitcast.101, bf16[512,1024]{1,0:T(8,128)(2,1)S(1)} %convert_element_type.56.ffn_ref), kind=kOutput, calls=%fused_computation.1 | convolution fusion | flops 4303351808 | bytes 17842176 | tf_op jit(solution)/shard_map/rn,ynf->yrf/dot_general | solution.py:988
  170.9 6.3 %multiply_reduce_fusion = (f32[1024]{0:T(1024)S(1)}, f32[512]{0:T(512)S(1)}, f32[512]{0:T(512)S(1)}, f32[1024]{0:T(1024)S(1)}, f32[512,1024]{1,0:T(8,128)}) fusion(f32[512,1024]{1,0:T(8,128)S(1)} %copy-done.6, f32[1024]{0:T(1024)S(1)} %bitcast.88, f32[512,1024]{1,0:T(8,128)S(1)} %get-tuple-element.65, ...), kind=kOutput, calls=%fused_computation.18 | convolution fusion | flops 4299158528 | bytes 18890752 | tf_op jit(solution)/shard_map/yrf,ydf->rd/dot_general | solution.py:988
  177.2 2.7 fusion.21
  180.1 0.7 pad.4.small_ref
  181.5 1.0 copy-done.4
  182.4 2.3 fusion.10.mix_ref
  184.7 131.0 %backward.1 = (f32[2,64,768]{2,1,0:T(8,128)}, f32[64,512]{1,0:T(8,128)}, f32[64,2048]{1,0:T(8,128)}, f32[64,2048]{1,0:T(8,128)}, bf16[2,2,2,64,1024]{4,3,2,1,0:T...) custom-call(bf16[512,1024]{1,0:T(8,128)(2,1)} %copy-done.3, ...), custom_call_target="tpu_custom_call" | custom-call | tf_op jit(solution)/shard_map/backward/pallas_call | solution.py:844
  315.7 2.1 convert_add_fusion
  318.0 1.7 bitcast_add_fusion
  319.7 0.6 constant_dynamic-slice_fusion
  320.4 0.6 dynamic_slice.15
  321.0 0.7 fusion.17
  321.7 1.9 fusion.14
  324.2 1.1 reshape.132
  325.2 0.7 copy.48
  325.9 0.8 copy.49
  326.7 0.8 copy.50
  (56 shorter events, 3.9 us)
Async XLA Ops:
  156.9 1.2 copy-start.5
  159.1 2.6 copy-start.12
  161.0 9.8 %slice-start = ((s8[8388608]{0:T(1024)(128)(4,1)}), s8[4194304]{0:T(1024)(128)(4,1)S(1)}, s32[]{:S(2)}) async-start(s8[8388608]{0:T(1024)(128)(4,1)} %bitcast.97), calls=%async_computation | async-start | bytes 8388608
  161.7 9.1 %copy-start.3 = (bf16[512,1024]{1,0:T(8,128)(2,1)}, bf16[512,1024]{1,0:T(8,128)(2,1)S(1)}, u32[]{:S(2)}) copy-start(bf16[512,1024]{1,0:T(8,128)(2,1)S(1)} %convert_element_type.56.ffn_ref) | copy-start | bytes 3145732
  161.7 9.1 %copy-start.6 = (f32[512,1024]{1,0:T(8,128)S(1)}, f32[512,1024]{1,0:T(8,128)}, u32[]{:S(2)}) copy-start(f32[512,1024]{1,0:T(8,128)} %get-tuple-element.33) | copy-start | bytes 6291460
  161.7 9.1 %slice-start.1 = ((s8[8388608]{0:T(1024)(128)(4,1)}), s8[4194304]{0:T(1024)(128)(4,1)S(1)}, s32[]{:S(2)}) async-start(s8[8388608]{0:T(1024)(128)(4,1)} %bitcast.97), calls=%async_computation.1 | async-start | bytes 8388608
  170.8 6.3 %copy-start.2 = (bf16[2,512,2048]{2,1,0:T(8,128)(2,1)}, bf16[2,512,2048]{2,1,0:T(8,128)(2,1)S(1)}, u32[]{:S(2)}) copy-start(bf16[2,512,2048]{2,1,0:T(8,128)(2,1)S(1)} %get-tuple-element.69.pre_ref) | copy-start | bytes 12582916
  179.9 1.4 copy-start
  180.0 2.4 copy-start.13
  181.5 1.0 copy-start.4
  315.7 2.2 copy-start.1
  318.0 1.7 copy-start.10
  318.0 5.7 %copy-start.9 = (f32[2,64,768]{2,1,0:T(8,128)S(1)}, f32[2,64,768]{2,1,0:T(8,128)}, u32[]{:S(2)}) copy-start(f32[2,64,768]{2,1,0:T(8,128)} %get-tuple-element.52) | copy-start | bytes 1179652
  319.7 5.5 %copy-start.11 = (f32[64,512]{1,0:T(8,128)S(1)}, f32[64,512]{1,0:T(8,128)}, u32[]{:S(2)}) copy-start(f32[64,512]{1,0:T(8,128)} %get-tuple-element.53) | copy-start | bytes 393220
  319.7 6.2 %copy-start.8 = (f32[64,2048]{1,0:T(8,128)S(1)}, f32[64,2048]{1,0:T(8,128)}, u32[]{:S(2)}) copy-start(f32[64,2048]{1,0:T(8,128)} %get-tuple-element.99) | copy-start | bytes 1572868
  321.7 5.0 %copy-start.7 = (f32[64,2048]{1,0:T(8,128)S(1)}, f32[64,2048]{1,0:T(8,128)}, u32[]{:S(2)}) copy-start(f32[64,2048]{1,0:T(8,128)} %get-tuple-element.55) | copy-start | bytes 1572868

commit v7 on v6

--- a/solution.py
+++ b/solution.py
@@ -1107,7 +1107,7 @@
             embed_low.reshape(v_raw.shape[:4] + (width,)), v_raw, mixed_far, mixed_heads, stats, segments, seg_col,
             pad_rows(small),
         )
-        d_own = (d_near.astype(F32) + d_far.astype(F32)).reshape(own_rows, width)
+        d_own = d_near.astype(F32) + d_far.astype(F32)
         qkv_grad = v_sum.reshape(2, rows, 3, -1).transpose(2, 1, 0, 3).reshape(3, rows, cols)
     else:
         embed_low = embed_low.reshape(length, width)
@@ -1132,11 +1132,11 @@
             return lax.psum_scatter(a, "dp", scatter_dimension=0, tiled=True).astype(F32)
 
         o_sum, i_sum, d_sum = both(out_grad_t), both(in_grad), both(down_grad)
-        d_own = lax.psum_scatter(d_embed, "mp", scatter_dimension=0).astype(F32)
+        d_own = lax.psum_scatter(d_embed, "mp", scatter_dimension=0).astype(F32).reshape(own_rows, width)
         small = lax.psum(small, ("dp", "mp"))
         qkv_grad = v_sum.reshape(rows, 3, cols).transpose(1, 0, 2)
 
-    input_grad = d_pre_one + d_own
+    input_grad = (d_pre_one.reshape(d_own.shape) + d_own).reshape(own_rows, width)
     d_time = small[:dp]
     start = dp_index * rows
     features = few[:, :width]

time: 329 us -> 329 us (level)
    unnamed x40 -> x38, local copies, waits for them, and re-layouts: 7.82 us -> 7.7 us
where the time goes in v7:
time: 329 us; the launch traced here: 328 us
  Pallas kernels  266 us (81%)
  matrix products  29.4 us (9%)
  local copies, waits for them, and re-layouts  19.2 us (6%)
  other arithmetic  11.7 us (4%)
    pallas_call x1, Pallas kernels, forward(): pl.pallas_call(forward_kernel, name='forward', out_shape=outs, in_specs=[...  135 us
    pallas_call x1, Pallas kernels, backward(): pl.pallas_call(backward_kernel, name='backward', out_shape=outs, in_specs...  131 us
    dot_general x4, matrix products, ein(): return jnp.einsum(spec, left, right, preferred_element_type=F32)  27.5 us
    unnamed x38, local copies, waits for them, and re-layouts  7.7 us

profile of v7, /device:TPU:20, one launch (start us, length us, event | category | flops | bytes accessed | tf_op | source)
XLA Modules:
  0.0 327.7 jit_solution(1699528073847313545)
XLA Ops:
  1.3 1.2 slice.61.b_ref
  2.5 0.7 broadcast_in_dim.14
  3.8 0.8 copy.32
  4.6 0.8 copy.31
  5.4 0.9 slice_bitcast_fusion
  6.3 0.8 concatenate.29.v_ref
  7.1 1.7 broadcast_in_dim.31.sc_ref
  8.8 134.7 %forward.1 = (bf16[4,2,2,64,1664]{4,3,2,1,0:T(8,128)(2,1)}, bf16[2,4,2,2,64,512]{5,4,3,2,1,0:T(8,128)(2,1)}, bf16[2,4,2,2,64,2048]{5,4,3,2,1,0:T(8,128)(2,1)}, b...) custom-call(bf16[64,1664]{1,0:T(8,128)(2,1)} %concatenate.29.v_ref, ...), custom_call_target="tpu_custom_call" | custom-call | tf_op jit(solution)/shard_map/forward/pallas_call | solution.py:442
  143.5 0.9 fusion.22
  144.4 1.1 slice_reduce_fusion
  145.5 0.9 copy.42
  146.4 0.6 slice.73
  147.1 9.8 %fusion.23 = (f32[512]{0:T(512)S(1)}, f32[512,1024]{1,0:T(8,128)S(1)}) fusion(f32[1024]{0:T(1024)S(1)} %bitcast.97, bf16[2,512,2048]{2,1,0:T(8,128)(2,1)} %get-tuple-element.35.act_ref, bf16[2,1024,2048]{2,1,0:T(8,128)(2,1)} %bitcast.102, f32[1024]{0:T(1024)S(1)} %bitcast.98, f32[512,1024]{1,0:T(8,128)} %get-tuple-element.33, f32[1024]{0:T(1024)S(1)} %bitcast.89), kind=kOutput, calls=%fused_computation.58 | convolution fusion | flops 4297588224 | bytes 16791552 | tf_op jit(solution)/shard_map/yrf,ynf->rn/dot_general | solution.py:988
  157.3 0.9 copy-done.4
  158.1 1.0 fusion.8
  159.1 1.8 fusion.19
  161.7 9.1 %fusion = (f32[2,2048]{1,0:T(2,128)S(1)}, bf16[2,512,2048]{2,1,0:T(8,128)(2,1)S(1)}) fusion(bf16[2,512,2048]{2,1,0:T(8,128)(2,1)S(1)} %copy-done.11, bf16[2,1024,2048]{2,1,0:T(8,128)(2,1)} %bitcast.103, bf16[512,1024]{1,0:T(8,128)(2,1)S(1)} %convert_element_type.56.ffn_ref), kind=kOutput, calls=%fused_computation.1 | convolution fusion | flops 4303351808 | bytes 17842176 | tf_op jit(solution)/shard_map/rn,ynf->yrf/dot_general | solution.py:988
  170.9 6.3 %multiply_reduce_fusion = (f32[1024]{0:T(1024)S(1)}, f32[512]{0:T(512)S(1)}, f32[512]{0:T(512)S(1)}, f32[1024]{0:T(1024)S(1)}, f32[512,1024]{1,0:T(8,128)}) fusion(f32[512,1024]{1,0:T(8,128)S(1)} %copy-done.5, f32[1024]{0:T(1024)S(1)} %bitcast.90, f32[512,1024]{1,0:T(8,128)S(1)} %get-tuple-element.65, ...), kind=kOutput, calls=%fused_computation.17 | convolution fusion | flops 4299158528 | bytes 18890752 | tf_op jit(solution)/shard_map/yrf,ydf->rd/dot_general | solution.py:988
  177.2 2.7 fusion.21
  180.1 0.7 pad.4.small_ref
  181.5 1.0 copy-done.3
  182.4 2.3 fusion.10.mix_ref
  184.7 131.0 %backward.1 = (f32[2,64,768]{2,1,0:T(8,128)}, f32[64,512]{1,0:T(8,128)}, f32[64,2048]{1,0:T(8,128)}, f32[64,2048]{1,0:T(8,128)}, bf16[2,2,2,64,1024]{4,3,2,1,0:T...) custom-call(bf16[512,1024]{1,0:T(8,128)(2,1)} %copy-done.2, ...), custom_call_target="tpu_custom_call" | custom-call | tf_op jit(solution)/shard_map/backward/pallas_call | solution.py:844
  315.8 4.1 %add_add_fusion = f32[2,2,2,64,1024]{4,3,2,1,0:T(8,128)} fusion(f32[2,2,2,64,1024]{4,3,2,1,0:T(8,128)} %bitcast.70, bf16[2,2,2,64,1024]{4,3,2,1,0:T(8,128)(2,1)} %get-tuple-element.49, bf16[2,2,2,64,1024]{4,3,2,1,0:T(8,128)(2,1)} %get-tuple-element.48), kind=kLoop, calls=%fused_computation.16 | loop fusion | flops 2097152 | bytes 6291456 | tf_op jit(solution)/shard_map/add | solution.py:1139
  319.9 0.6 constant_dynamic-slice_fusion
  320.6 0.6 dynamic_slice.15
  321.2 0.7 fusion.17
  321.9 1.9 fusion.14
  324.4 1.1 reshape.136
  325.4 0.7 copy.48
  326.1 0.8 copy.49
  326.9 0.8 copy.50
  (53 shorter events, 3.2 us)
Async XLA Ops:
  156.9 1.2 copy-start.4
  159.1 2.6 copy-start.11
  161.0 9.8 %slice-start = ((s8[8388608]{0:T(1024)(128)(4,1)}), s8[4194304]{0:T(1024)(128)(4,1)S(1)}, s32[]{:S(2)}) async-start(s8[8388608]{0:T(1024)(128)(4,1)} %bitcast.99), calls=%async_computation | async-start | bytes 8388608
  161.7 9.1 %copy-start.2 = (bf16[512,1024]{1,0:T(8,128)(2,1)}, bf16[512,1024]{1,0:T(8,128)(2,1)S(1)}, u32[]{:S(2)}) copy-start(bf16[512,1024]{1,0:T(8,128)(2,1)S(1)} %convert_element_type.56.ffn_ref) | copy-start | bytes 3145732
  161.7 9.1 %copy-start.5 = (f32[512,1024]{1,0:T(8,128)S(1)}, f32[512,1024]{1,0:T(8,128)}, u32[]{:S(2)}) copy-start(f32[512,1024]{1,0:T(8,128)} %get-tuple-element.33) | copy-start | bytes 6291460
  161.7 9.1 %slice-start.1 = ((s8[8388608]{0:T(1024)(128)(4,1)}), s8[4194304]{0:T(1024)(128)(4,1)S(1)}, s32[]{:S(2)}) async-start(s8[8388608]{0:T(1024)(128)(4,1)} %bitcast.99), calls=%async_computation.1 | async-start | bytes 8388608
  170.8 6.3 %copy-start.1 = (bf16[2,512,2048]{2,1,0:T(8,128)(2,1)}, bf16[2,512,2048]{2,1,0:T(8,128)(2,1)S(1)}, u32[]{:S(2)}) copy-start(bf16[2,512,2048]{2,1,0:T(8,128)(2,1)S(1)} %get-tuple-element.69.pre_ref) | copy-start | bytes 12582916
  179.9 1.4 copy-start
  180.0 2.4 copy-start.12
  181.5 1.0 copy-start.3
  315.7 4.2 %copy-start.9 = (f32[32,1024]{1,0:T(8,128)S(1)}, f32[32,1024]{1,0:T(8,128)}, u32[]{:S(2)}) copy-start(f32[32,1024]{1,0:T(8,128)} %get-tuple-element.51) | copy-start | bytes 393220
  315.7 8.1 %copy-start.8 = (f32[2,64,768]{2,1,0:T(8,128)S(1)}, f32[2,64,768]{2,1,0:T(8,128)}, u32[]{:S(2)}) copy-start(f32[2,64,768]{2,1,0:T(8,128)} %get-tuple-element.52) | copy-start | bytes 1179652
  319.9 5.5 %copy-start.10 = (f32[64,512]{1,0:T(8,128)S(1)}, f32[64,512]{1,0:T(8,128)}, u32[]{:S(2)}) copy-start(f32[64,512]{1,0:T(8,128)} %get-tuple-element.53) | copy-start | bytes 393220
  319.9 6.2 %copy-start.7 = (f32[64,2048]{1,0:T(8,128)S(1)}, f32[64,2048]{1,0:T(8,128)}, u32[]{:S(2)}) copy-start(f32[64,2048]{1,0:T(8,128)} %get-tuple-element.99) | copy-start | bytes 1572868
  321.9 5.0 %copy-start.6 = (f32[64,2048]{1,0:T(8,128)S(1)}, f32[64,2048]{1,0:T(8,128)}, u32[]{:S(2)}) copy-start(f32[64,2048]{1,0:T(8,128)} %get-tuple-element.55) | copy-start | bytes 1572868
